TPU v7x, 32 devices: a whole 2x2x4 slice. The times are simulated.
32 devices in a mesh: groups: 2 (over x), sect: 2 (over core), tile: 8 (over z, y).
Axes of the slice: x: 2, y: 2, z: 4, core: 2. Of those that a mesh axis runs over, the one named last changes fastest.
Arguments:
- features: bfloat16 [4, 16, 64, 512], P(('groups', 'sect'), 'tile'), parts along dimension 0, may hold values from -6 to 6
- conv_first: bfloat16 [3, 3, 3, 512, 512], replicated, may hold values from -0.0546875 to 0.0546875
- bias_first: bfloat16 [512], replicated, may hold values from -3 to 3
- conv_second: bfloat16 [3, 3, 3, 512, 256], replicated, may hold values from -0.0546875 to 0.0546875
- bias_second: bfloat16 [256], replicated, may hold values from -3 to 3
- conv_third: bfloat16 [3, 3, 3, 256, 128], replicated, may hold values from -0.078125 to 0.078125
- bias_third: bfloat16 [128], replicated, may hold values from -3 to 3
Outputs:
- decoded: bfloat16 [4, 64, 256, 128], P(('groups', 'sect'), 'tile'), parts along dimension 0
There are 2 independent parts, one for each index of `groups`. A program takes and returns all parts, laid end to end along the dimension named above; an argument that names none is the same for every part. Nothing has to cross between parts.
All inputs are finite; a program needn't handle non-finite values.
Results may differ from a plain program's by a relative error of at most 0.014.
Values may be sent and summed in bfloat16 or wider, within the bound.
No kernel may reach another device: no remote copies, remote signals or barrier semaphores. Data moves between devices by JAX's collectives and lax.ppermute only.
A program may use at most 128 MiB of HBM per device.

v0:
```python
import jax
import jax.numpy as jnp
from jax import lax
from jax.sharding import PartitionSpec as P


def with_halo(block, sides, width):
    for axis, dim in sides:
        count = lax.axis_size(axis)
        forward = [(i, i + 1) for i in range(count - 1)]
        backward = [(target, source) for source, target in forward]
        low = lax.ppermute(
            lax.slice_in_dim(block, block.shape[dim] - width, None, axis=dim), axis, forward
        )
        high = lax.ppermute(lax.slice_in_dim(block, 0, width, axis=dim), axis, backward)
        block = jnp.concatenate([low, block, high], axis=dim)
    return block


def enlarge(padded, upsample):
    if upsample:
        padded = jnp.repeat(jnp.repeat(padded, 2, axis=0), 2, axis=1)[1:-1, 1:-1]
    return padded


def window(padded, row_tap, col_tap, row_count, col_count):
    return padded[row_tap : row_tap + row_count, col_tap : col_tap + col_count].reshape(
        row_count * col_count, padded.shape[2]
    )


def single_taps(padded, weight_all, offset):
    row_count = padded.shape[0] - 2
    col_count = padded.shape[1] - 2
    summed = jnp.zeros((row_count * col_count, weight_all.shape[3]), jnp.float32)
    for row_tap in range(3):
        for col_tap in range(3):
            summed = summed + jnp.dot(
                window(padded, row_tap, col_tap, row_count, col_count),
                weight_all[row_tap, col_tap],
                preferred_element_type=jnp.float32,
            )
    return summed.reshape(row_count, col_count, -1) + offset.astype(jnp.float32)


def paired_taps(cur_pad, prev_pad, weight_early, weight_now, offset):
    row_count = cur_pad.shape[0] - 2
    col_count = cur_pad.shape[1] - 2
    summed = jnp.zeros((row_count * col_count, weight_now.shape[3]), jnp.float32)
    for row_tap in range(3):
        for col_tap in range(3):
            summed = summed + (
                jnp.dot(
                    window(prev_pad, row_tap, col_tap, row_count, col_count),
                    weight_early[row_tap, col_tap],
                    preferred_element_type=jnp.float32,
                )
                + jnp.dot(
                    window(cur_pad, row_tap, col_tap, row_count, col_count),
                    weight_now[row_tap, col_tap],
                    preferred_element_type=jnp.float32,
                )
            )
    return summed.reshape(row_count, col_count, -1) + offset.astype(jnp.float32)


def merge_weights(weight):
    weight_early = weight[0].astype(jnp.float32) + weight[1].astype(jnp.float32)
    return (weight_early + weight[2].astype(jnp.float32), weight_early)


def per_device(features, conv_first, bias_first, conv_second, bias_second, conv_third, bias_third):
    kernels = [merge_weights(conv_first), merge_weights(conv_second), merge_weights(conv_third)]
    both = lax.all_to_all(features, "sect", split_axis=2, concat_axis=0, tiled=True)

    def convolve_both(active, layer, weight, offset, upsample):
        padded = with_halo(active, (("sect", 2), ("tile", 1)), 1)
        earlier = enlarge(padded[0], upsample)
        later = enlarge(padded[1], upsample)
        weight_all, weight_early = kernels[layer]
        return jnp.stack(
            [
                single_taps(earlier, weight_all, offset),
                paired_taps(later, earlier, weight_early, weight[2], offset),
            ]
        )

    silu_in = jax.nn.silu(both.astype(jnp.float32)).astype(jnp.bfloat16)
    hidden = (
        both.astype(jnp.float32) + convolve_both(silu_in, 0, conv_first, bias_first, False)
    ).astype(jnp.bfloat16)
    silu_mid = jax.nn.silu(hidden.astype(jnp.float32)).astype(jnp.bfloat16)
    silu_low = jax.nn.silu(convolve_both(silu_mid, 1, conv_second, bias_second, True)).astype(
        jnp.bfloat16
    )
    decoded = convolve_both(silu_low, 2, conv_third, bias_third, True).astype(jnp.bfloat16)
    return lax.all_to_all(decoded, "sect", split_axis=0, concat_axis=2, tiled=True)


def solution(mesh):
    return jax.shard_map(
        per_device,
        mesh=mesh,
        in_specs=(P(("groups", "sect"), "tile", None, None), P(), P(), P(), P(), P(), P()),
        out_specs=P(("groups", "sect"), "tile", None, None),
        check_vma=False,
    )
```

profile of v0, /device:TPU:0, one launch (start us, length us, event | category | flops | bytes accessed | tf_op | source)
XLA Modules:
  0.0 107.1 jit_solution(17171230268341012411)
XLA Ops:
  0.0 1.0 copy.36
  1.0 3.8 %all_to_all.27 = bf16[1,2,64,512]{3,1,0,2:T(2,128)(2,1)S(1)} all-to-all(bf16[1,2,64,512]{3,1,0,2:T(2,128)(2,1)S(1)} %copy.36), channel_id=1, replica_groups=mesh['groups'=2,'sect'=2,'tile'=8] {'sect'}, dimensions={2} | all-to-all | bytes 262144 | tf_op jit(solution)/shard_map/all_to_all | solution.py:74
  5.1 2.1 %collective-permute-start = (bf16[2,2,1,512]{3,2,1,0:T(2,128)(2,1)S(1)}, bf16[2,2,1,512]{3,2,1,0:T(2,128)(2,1)S(1)}, u32[]{:S(2)}, u32[]{:S(2)}) collective-permute-start(bf16[2,2,1,512]{3,2,1,0:T(2,128)(2,1)S(1)} %get-tuple-element.81), channel_id=1, source_target_pairs={{0,8},{1,9},{2,10},{3,11},{4,12},{5,13},{6,14},{7,15},{16,24},{17,... | collective-permute-start | bytes 12296 | tf_op jit(solution)/shard_map/ppermute | solution.py:12
  7.2 1.3 %collective-permute-start.1 = (bf16[2,2,1,512]{3,2,1,0:T(2,128)(2,1)S(1)}, bf16[2,2,1,512]{3,2,1,0:T(2,128)(2,1)S(1)}, u32[]{:S(2)}, u32[]{:S(2)}) collective-permute-start(bf16[2,2,1,512]{3,2,1,0:T(2,128)(2,1)S(1)} %get-tuple-element.82), channel_id=1, source_target_pairs={{8,0},{9,1},{10,2},{11,3},{12,4},{13,5},{14,6},{15,7},{24,16},{25,... | collective-permute-start | bytes 12296 | tf_op jit(solution)/shard_map/ppermute | solution.py:15
  8.5 6.3 %convert_add_fusion = bf16[3,3,512,512]{3,2,1,0:T(8,128)(2,1)S(1)} fusion(bf16[3,3,3,512,512]{4,3,2,1,0:T(8,128)(2,1)} %param.8), kind=kLoop, calls=%fused_computation | loop fusion | flops 14155776 | bytes 18874368 | tf_op jit(solution)/shard_map/add | solution.py:69
  14.9 5.2 %collective-permute-start.2 = (bf16[2,1,34,512]{3,2,1,0:T(8,128)(2,1)S(1)}, bf16[2,1,34,512]{3,2,1,0:T(8,128)(2,1)S(1)}, u32[]{:S(2)}, u32[]{:S(2)}) collective-permute-start(bf16[2,1,34,512]{3,2,1,0:T(8,128)(2,1)S(1)} %get-tuple-element.77), channel_id=1, source_target_pairs={{0,1},{1,2},{2,3},{3,4},{4,5},{5,6},{6,7},{8,9},{9,10},{10,11},{11... | collective-permute-start | bytes 208904 | tf_op jit(solution)/shard_map/ppermute | solution.py:12
  20.1 1.3 %collective-permute-start.3 = (bf16[2,1,34,512]{3,2,1,0:T(8,128)(2,1)S(1)}, bf16[2,1,34,512]{3,2,1,0:T(8,128)(2,1)S(1)}, u32[]{:S(2)}, u32[]{:S(2)}) collective-permute-start(bf16[2,1,34,512]{3,2,1,0:T(8,128)(2,1)S(1)} %get-tuple-element.78), channel_id=1, source_target_pairs={{1,0},{2,1},{3,2},{4,3},{5,4},{6,5},{7,6},{9,8},{10,9},{11,10},{12... | collective-permute-start | bytes 208904 | tf_op jit(solution)/shard_map/ppermute | solution.py:15
  21.4 1.7 %slice_bitcast_fusion = (bf16[3,3,512,512]{3,2,1,0:T(8,128)(2,1)S(1)}, bf16[3,3,512,512]{3,2,1,0:T(8,128)(2,1)S(1)}) fusion(bf16[3,3,3,512,512]{4,3,2,1,0:T(8,128)(2,1)S(1)} %copy-done), kind=kLoop, calls=%fused_computation.4 | loop fusion | flops 9437184 | bytes 23592960 | tf_op jit(solution)/shard_map/squeeze | solution.py:69
  23.2 4.1 %collective-permute-done.3 = bf16[2,1,34,512]{3,2,1,0:T(8,128)(2,1)S(1)} collective-permute-done((bf16[2,1,34,512]{3,2,1,0:T(8,128)(2,1)S(1)}, bf16[2,1,34,512]{3,2,1,0:T(8,128)(2,1)S(1)}, u32[]{:S(2)}, u32[]{:S(2)}) %collective-permute-start.3) | collective-permute-done | bytes 69664 | tf_op jit(solution)/shard_map/ppermute | solution.py:15
  33.4 1.9 %collective-permute-start.4 = (bf16[2,2,1,512]{3,2,1,0:T(2,128)(2,1)S(1)}, bf16[2,2,1,512]{3,2,1,0:T(2,128)(2,1)S(1)}, u32[]{:S(2)}, u32[]{:S(2)}) collective-permute-start(bf16[2,2,1,512]{3,2,1,0:T(2,128)(2,1)S(1)} %get-tuple-element.79), channel_id=1, source_target_pairs={{0,8},{1,9},{2,10},{3,11},{4,12},{5,13},{6,14},{7,15},{16,24},{17,... | collective-permute-start | bytes 12296 | tf_op jit(solution)/shard_map/ppermute | solution.py:12
  35.3 1.3 %collective-permute-start.5 = (bf16[2,2,1,512]{3,2,1,0:T(2,128)(2,1)S(1)}, bf16[2,2,1,512]{3,2,1,0:T(2,128)(2,1)S(1)}, u32[]{:S(2)}, u32[]{:S(2)}) collective-permute-start(bf16[2,2,1,512]{3,2,1,0:T(2,128)(2,1)S(1)} %get-tuple-element.80), channel_id=1, source_target_pairs={{8,0},{9,1},{10,2},{11,3},{12,4},{13,5},{14,6},{15,7},{24,16},{25,... | collective-permute-start | bytes 12296 | tf_op jit(solution)/shard_map/ppermute | solution.py:15
  36.6 2.3 %slice_bitcast_fusion.1 = (bf16[3,3,512,256]{3,2,1,0:T(8,128)(2,1)S(1)}, bf16[3,3,512,256]{3,2,1,0:T(8,128)(2,1)}) fusion(bf16[3,3,3,512,256]{4,3,2,1,0:T(8,128)(2,1)S(1)} %bitcast.453), kind=kLoop, calls=%fused_computation.5 | loop fusion | flops 4718592 | bytes 11796480 | tf_op jit(solution)/shard_map/squeeze | solution.py:69
  38.9 4.3 %collective-permute-start.6 = (bf16[2,1,34,512]{3,2,1,0:T(8,128)(2,1)S(1)}, bf16[2,1,34,512]{3,2,1,0:T(8,128)(2,1)S(1)}, u32[]{:S(2)}, u32[]{:S(2)}) collective-permute-start(bf16[2,1,34,512]{3,2,1,0:T(8,128)(2,1)S(1)} %get-tuple-element.57), channel_id=1, source_target_pairs={{0,1},{1,2},{2,3},{3,4},{4,5},{5,6},{6,7},{8,9},{9,10},{10,11},{11... | collective-permute-start | bytes 208904 | tf_op jit(solution)/shard_map/ppermute | solution.py:12
  43.3 1.5 %collective-permute-start.7 = (bf16[2,1,34,512]{3,2,1,0:T(8,128)(2,1)S(1)}, bf16[2,1,34,512]{3,2,1,0:T(8,128)(2,1)S(1)}, u32[]{:S(2)}, u32[]{:S(2)}) collective-permute-start(bf16[2,1,34,512]{3,2,1,0:T(8,128)(2,1)S(1)} %get-tuple-element.58), channel_id=1, source_target_pairs={{1,0},{2,1},{3,2},{4,3},{5,4},{6,5},{7,6},{9,8},{10,9},{11,10},{12... | collective-permute-start | bytes 208904 | tf_op jit(solution)/shard_map/ppermute | solution.py:15
  44.8 2.4 %convert_add_fusion.1 = bf16[3,3,512,256]{3,2,1,0:T(8,128)(2,1)} fusion(bf16[3,3,3,512,256]{4,3,2,1,0:T(8,128)(2,1)S(1)} %bitcast.453), kind=kLoop, calls=%fused_computation.2 | loop fusion | flops 7077888 | bytes 9437184 | tf_op jit(solution)/shard_map/add | solution.py:69
  47.1 3.2 %collective-permute-done.7 = bf16[2,1,34,512]{3,2,1,0:T(8,128)(2,1)S(1)} collective-permute-done((bf16[2,1,34,512]{3,2,1,0:T(8,128)(2,1)S(1)}, bf16[2,1,34,512]{3,2,1,0:T(8,128)(2,1)S(1)}, u32[]{:S(2)}, u32[]{:S(2)}) %collective-permute-start.7) | collective-permute-done | bytes 69664 | tf_op jit(solution)/shard_map/ppermute | solution.py:15
  50.9 1.8 %fusion.66 = (bf16[4,64,512]{2,0,1:T(4,128)(2,1)S(1)}, bf16[4,64,512]{2,0,1:T(4,128)(2,1)}, bf16[4,64,512]{2,0,1:T(4,128)(2,1)}, bf16[4,64,512]{2,0,1:T(4,128)(2...) fusion(bf16[8,68,512]{2,0,1:T(8,128)(2,1)S(1)} %bitcast.454), kind=kLoop, calls=%fused_computation.235 | loop fusion | bytes 4718592 | tf_op jit(solution)/shard_map/slice | solution.py:27
  53.2 0.6 fusion.65
  54.1 1.2 %fusion.42 = f32[256,256]{1,0:T(8,128)S(1)} fusion(bf16[256,512]{1,0:T(8,128)(2,1)S(1)} %bitcast.474, bf16[3,3,512,256]{3,2,1,0:T(8,128)(2,1)} %get-tuple-element.8), kind=kOutput, calls=%fused_computation.129 | convolution fusion | flops 67108864 | bytes 786432 | tf_op jit(solution)/shard_map/dot_general | solution.py:53
  55.3 1.2 %fusion.41 = f32[256,256]{1,0:T(8,128)S(1)} fusion(bf16[256,512]{1,0:T(8,128)(2,1)S(1)} %bitcast.476, bf16[3,3,512,256]{3,2,1,0:T(8,128)(2,1)} %get-tuple-element.8), kind=kOutput, calls=%fused_computation.127 | convolution fusion | flops 67108864 | bytes 786432 | tf_op jit(solution)/shard_map/dot_general | solution.py:53
  56.6 1.2 %fusion.40 = f32[256,256]{1,0:T(8,128)S(1)} fusion(bf16[256,512]{1,0:T(8,128)(2,1)S(1)} %bitcast.478, bf16[3,3,512,256]{3,2,1,0:T(8,128)(2,1)} %get-tuple-element.8), kind=kOutput, calls=%fused_computation.125 | convolution fusion | flops 67108864 | bytes 786432 | tf_op jit(solution)/shard_map/dot_general | solution.py:53
  58.0 1.2 %fusion.39 = f32[256,256]{1,0:T(8,128)S(1)} fusion(bf16[256,512]{1,0:T(8,128)(2,1)S(1)} %bitcast.480, bf16[3,3,512,256]{3,2,1,0:T(8,128)(2,1)} %get-tuple-element.8), kind=kOutput, calls=%fused_computation.123 | convolution fusion | flops 67108864 | bytes 786432 | tf_op jit(solution)/shard_map/dot_general | solution.py:53
  59.3 1.3 %fusion.38 = f32[256,256]{1,0:T(8,128)S(1)} fusion(bf16[256,512]{1,0:T(8,128)(2,1)S(1)} %bitcast.482, bf16[3,3,512,256]{3,2,1,0:T(8,128)(2,1)} %get-tuple-element.8), kind=kOutput, calls=%fused_computation.121 | convolution fusion | flops 67108864 | bytes 786432 | tf_op jit(solution)/shard_map/dot_general | solution.py:53
  60.7 1.2 %fusion.37 = f32[256,256]{1,0:T(8,128)S(1)} fusion(bf16[256,512]{1,0:T(8,128)(2,1)S(1)} %bitcast.484, bf16[3,3,512,256]{3,2,1,0:T(8,128)(2,1)} %get-tuple-element.8), kind=kOutput, calls=%fused_computation.119 | convolution fusion | flops 67108864 | bytes 786432 | tf_op jit(solution)/shard_map/dot_general | solution.py:53
  62.0 1.2 %fusion.36 = f32[256,256]{1,0:T(8,128)S(1)} fusion(bf16[256,512]{1,0:T(8,128)(2,1)S(1)} %bitcast.486, bf16[3,3,512,256]{3,2,1,0:T(8,128)(2,1)} %get-tuple-element.8), kind=kOutput, calls=%fused_computation.117 | convolution fusion | flops 67108864 | bytes 786432 | tf_op jit(solution)/shard_map/dot_general | solution.py:53
  63.4 1.2 %fusion.35 = f32[256,256]{1,0:T(8,128)S(1)} fusion(bf16[256,512]{1,0:T(8,128)(2,1)S(1)} %bitcast.488, bf16[3,3,512,256]{3,2,1,0:T(8,128)(2,1)} %get-tuple-element.8), kind=kOutput, calls=%fused_computation.115 | convolution fusion | flops 67108864 | bytes 786432 | tf_op jit(solution)/shard_map/dot_general | solution.py:53
  64.7 1.2 %fusion.34 = f32[256,256]{1,0:T(8,128)S(1)} fusion(bf16[256,512]{1,0:T(8,128)(2,1)S(1)} %bitcast.490, bf16[3,3,512,256]{3,2,1,0:T(8,128)(2,1)} %get-tuple-element.8), kind=kOutput, calls=%fused_computation.113 | convolution fusion | flops 67108864 | bytes 786432 | tf_op jit(solution)/shard_map/dot_general | solution.py:53
  70.4 1.9 %collective-permute-start.8 = (bf16[2,4,1,256]{3,2,1,0:T(2,128)(2,1)S(1)}, bf16[2,4,1,256]{3,2,1,0:T(2,128)(2,1)S(1)}, u32[]{:S(2)}, u32[]{:S(2)}) collective-permute-start(bf16[2,4,1,256]{3,2,1,0:T(2,128)(2,1)S(1)} %get-tuple-element.55), channel_id=1, source_target_pairs={{0,8},{1,9},{2,10},{3,11},{4,12},{5,13},{6,14},{7,15},{16,24},{17,... | collective-permute-start | bytes 12296 | tf_op jit(solution)/shard_map/ppermute | solution.py:12
  72.3 1.3 %collective-permute-start.9 = (bf16[2,4,1,256]{3,2,1,0:T(2,128)(2,1)S(1)}, bf16[2,4,1,256]{3,2,1,0:T(2,128)(2,1)S(1)}, u32[]{:S(2)}, u32[]{:S(2)}) collective-permute-start(bf16[2,4,1,256]{3,2,1,0:T(2,128)(2,1)S(1)} %get-tuple-element.56), channel_id=1, source_target_pairs={{8,0},{9,1},{10,2},{11,3},{12,4},{13,5},{14,6},{15,7},{24,16},{25,... | collective-permute-start | bytes 12296 | tf_op jit(solution)/shard_map/ppermute | solution.py:15
  73.6 1.2 %slice_bitcast_fusion.38 = (bf16[3,3,256,128]{3,2,1,0:T(8,128)(2,1)}, bf16[3,3,256,128]{3,2,1,0:T(8,128)(2,1)}) fusion(bf16[3,3,3,256,128]{4,3,2,1,0:T(8,128)(2,1)S(1)} %copy-done.2), kind=kLoop, calls=%fused_computation.111 | loop fusion | flops 1179648 | bytes 2949120 | tf_op jit(solution)/shard_map/squeeze | solution.py:69
  74.8 0.6 collective-permute-done.9
  75.4 3.4 %collective-permute-start.10 = (bf16[2,1,66,256]{3,2,1,0:T(8,128)(2,1)S(1)}, bf16[2,1,66,256]{3,2,1,0:T(8,128)(2,1)S(1)}, u32[]{:S(2)}, u32[]{:S(2)}) collective-permute-start(bf16[2,1,66,256]{3,2,1,0:T(8,128)(2,1)S(1)} %get-tuple-element.53), channel_id=1, source_target_pairs={{0,1},{1,2},{2,3},{3,4},{4,5},{5,6},{6,7},{8,9},{9,10},{10,11},{11... | collective-permute-start | bytes 202760 | tf_op jit(solution)/shard_map/ppermute | solution.py:12
  78.9 1.5 %collective-permute-start.11 = (bf16[2,1,66,256]{3,2,1,0:T(8,128)(2,1)S(1)}, bf16[2,1,66,256]{3,2,1,0:T(8,128)(2,1)S(1)}, u32[]{:S(2)}, u32[]{:S(2)}) collective-permute-start(bf16[2,1,66,256]{3,2,1,0:T(8,128)(2,1)S(1)} %get-tuple-element.54), channel_id=1, source_target_pairs={{1,0},{2,1},{3,2},{4,3},{5,4},{6,5},{7,6},{9,8},{10,9},{11,10},{12... | collective-permute-start | bytes 202760 | tf_op jit(solution)/shard_map/ppermute | solution.py:15
  80.4 1.1 %convert_add_fusion.2 = bf16[3,3,256,128]{3,2,1,0:T(8,128)(2,1)} fusion(bf16[3,3,3,256,128]{4,3,2,1,0:T(8,128)(2,1)S(1)} %copy-done.2), kind=kLoop, calls=%fused_computation.31 | loop fusion | flops 1769472 | bytes 2359296 | tf_op jit(solution)/shard_map/add | solution.py:69
  81.5 3.7 %collective-permute-done.11 = bf16[2,1,66,256]{3,2,1,0:T(8,128)(2,1)S(1)} collective-permute-done((bf16[2,1,66,256]{3,2,1,0:T(8,128)(2,1)S(1)}, bf16[2,1,66,256]{3,2,1,0:T(8,128)(2,1)S(1)}, u32[]{:S(2)}, u32[]{:S(2)}) %collective-permute-start.11) | collective-permute-done | bytes 67616 | tf_op jit(solution)/shard_map/ppermute | solution.py:15
  85.3 0.7 slice_bitcast_fusion.111
  86.1 0.4 broadcast_in_dim.35
  86.5 0.3 reshape.352
  86.8 2.0 %fusion.64 = (bf16[8,128,256]{2,1,0:T(8,128)(2,1)S(1)}, bf16[8,128,256]{2,1,0:T(8,128)(2,1)S(1)}, bf16[8,128,256]{2,1,0:T(8,128)(2,1)S(1)}, bf16[8,128,256]{2,1,...) fusion(bf16[12,132,256]{2,1,0:T(8,128)(2,1)S(1)} %reshape.352), kind=kLoop, calls=%fused_computation.233 | loop fusion | bytes 9437184 | tf_op jit(solution)/shard_map/slice | solution.py:27
  88.8 1.3 %broadcast_in_dim.37 = bf16[12,66,2,256]{3,2,1,0:T(2,128)(2,1)} broadcast(bf16[12,66,256]{2,1,0:T(8,128)(2,1)S(1)} %bitcast.505), dimensions={0,1,3} | broadcast | bytes 1216512 | tf_op jit(solution)/shard_map/broadcast_in_dim | solution.py:22
  90.2 2.3 %reshape.364 = bf16[12,132,256]{2,1,0:T(8,128)(2,1)S(1)} reshape(bf16[12,66,2,256]{3,2,1,0:T(2,128)(2,1)} %broadcast_in_dim.37) | data formatting | bytes 1622016 | tf_op jit(solution)/shard_map/reshape | solution.py:22
  92.5 0.8 fusion.63
  95.2 0.3 fusion.56
  95.5 0.3 fusion.55
  95.8 0.3 fusion.54
  96.1 0.3 fusion.53
  96.7 0.3 convolution_add_fusion.16
  97.0 0.3 convolution_add_fusion.15
  97.3 0.3 convolution_add_fusion.14
  97.6 0.3 convolution_add_fusion.13
  97.9 0.3 convolution_add_fusion.12
  98.2 0.3 convolution_add_fusion.11
  98.5 0.3 convolution_add_fusion.10
  98.8 0.3 convolution_add_fusion.9
  99.2 0.3 convolution_add_fusion.8
  99.5 0.3 fusion.7
  99.8 0.3 fusion.6
  100.1 0.3 fusion.5
  100.4 0.3 fusion.4
  100.7 0.3 fusion.3
  101.3 0.3 fusion.1
  101.6 0.3 fusion
  102.1 4.2 %all_to_all.28 = bf16[2,8,128,128]{3,2,1,0:T(8,128)(2,1)S(1)} all-to-all(bf16[2,8,128,128]{3,2,1,0:T(8,128)(2,1)S(1)} %pad_maximum_fusion.1), channel_id=1, replica_groups=mesh['groups'=2,'sect'=2,'tile'=8] {'sect'}, dimensions={0} | all-to-all | bytes 1048576 | tf_op jit(solution)/shard_map/all_to_all | solution.py:97
  106.2 0.8 copy.58
  (160 shorter events, 15.3 us)
Async XLA Ops:
  5.1 9.7 %collective-permute-start = (bf16[2,2,1,512]{3,2,1,0:T(2,128)(2,1)S(1)}, bf16[2,2,1,512]{3,2,1,0:T(2,128)(2,1)S(1)}, u32[]{:S(2)}, u32[]{:S(2)}) collective-permute-start(bf16[2,2,1,512]{3,2,1,0:T(2,128)(2,1)S(1)} %get-tuple-element.81), channel_id=1, source_target_pairs={{0,8},{1,9},{2,10},{3,11},{4,12},{5,13},{6,14},{7,15},{16,24},{17,... | collective-permute-start | bytes 12296 | tf_op jit(solution)/shard_map/ppermute | solution.py:12
  7.2 7.7 %collective-permute-start.1 = (bf16[2,2,1,512]{3,2,1,0:T(2,128)(2,1)S(1)}, bf16[2,2,1,512]{3,2,1,0:T(2,128)(2,1)S(1)}, u32[]{:S(2)}, u32[]{:S(2)}) collective-permute-start(bf16[2,2,1,512]{3,2,1,0:T(2,128)(2,1)S(1)} %get-tuple-element.82), channel_id=1, source_target_pairs={{8,0},{9,1},{10,2},{11,3},{12,4},{13,5},{14,6},{15,7},{24,16},{25,... | collective-permute-start | bytes 12296 | tf_op jit(solution)/shard_map/ppermute | solution.py:15
  8.5 13.0 %copy-start = (bf16[3,3,3,512,512]{4,3,2,1,0:T(8,128)(2,1)S(1)}, bf16[3,3,3,512,512]{4,3,2,1,0:T(8,128)(2,1)}, u32[]{:S(2)}) copy-start(bf16[3,3,3,512,512]{4,3,2,1,0:T(8,128)(2,1)} %param.8) | copy-start | bytes 42467332
  14.9 8.2 %collective-permute-start.2 = (bf16[2,1,34,512]{3,2,1,0:T(8,128)(2,1)S(1)}, bf16[2,1,34,512]{3,2,1,0:T(8,128)(2,1)S(1)}, u32[]{:S(2)}, u32[]{:S(2)}) collective-permute-start(bf16[2,1,34,512]{3,2,1,0:T(8,128)(2,1)S(1)} %get-tuple-element.77), channel_id=1, source_target_pairs={{0,1},{1,2},{2,3},{3,4},{4,5},{5,6},{6,7},{8,9},{9,10},{10,11},{11... | collective-permute-start | bytes 208904 | tf_op jit(solution)/shard_map/ppermute | solution.py:12
  20.1 3.0 %copy-start.18 = (bf16[512]{0:T(512)(128)(2,1)S(1)}, bf16[512]{0:T(512)(128)(2,1)}, u32[]{:S(2)}) copy-start(bf16[512]{0:T(512)(128)(2,1)} %param.9) | copy-start | bytes 3076
  20.1 7.1 %collective-permute-start.3 = (bf16[2,1,34,512]{3,2,1,0:T(8,128)(2,1)S(1)}, bf16[2,1,34,512]{3,2,1,0:T(8,128)(2,1)S(1)}, u32[]{:S(2)}, u32[]{:S(2)}) collective-permute-start(bf16[2,1,34,512]{3,2,1,0:T(8,128)(2,1)S(1)} %get-tuple-element.78), channel_id=1, source_target_pairs={{1,0},{2,1},{3,2},{4,3},{5,4},{6,5},{7,6},{9,8},{10,9},{11,10},{12... | collective-permute-start | bytes 208904 | tf_op jit(solution)/shard_map/ppermute | solution.py:15
  30.0 6.6 %slice-start = ((s8[7077888]{0:T(1024)(128)(4,1)}), s8[4194304]{0:T(1024)(128)(4,1)S(1)}, s32[]{:S(2)}) async-start(s8[7077888]{0:T(1024)(128)(4,1)} %bitcast.452), calls=%async_computation.2 | async-start | bytes 8388608
  31.7 4.9 %slice-start.1 = ((s8[7077888]{0:T(1024)(128)(4,1)}), s8[2883584]{0:T(1024)(128)(4,1)S(1)}, s32[]{:S(2)}) async-start(s8[7077888]{0:T(1024)(128)(4,1)} %bitcast.452), calls=%async_computation.3 | async-start | bytes 5767168
  33.4 5.5 %collective-permute-start.4 = (bf16[2,2,1,512]{3,2,1,0:T(2,128)(2,1)S(1)}, bf16[2,2,1,512]{3,2,1,0:T(2,128)(2,1)S(1)}, u32[]{:S(2)}, u32[]{:S(2)}) collective-permute-start(bf16[2,2,1,512]{3,2,1,0:T(2,128)(2,1)S(1)} %get-tuple-element.79), channel_id=1, source_target_pairs={{0,8},{1,9},{2,10},{3,11},{4,12},{5,13},{6,14},{7,15},{16,24},{17,... | collective-permute-start | bytes 12296 | tf_op jit(solution)/shard_map/ppermute | solution.py:12
  35.3 3.6 %collective-permute-start.5 = (bf16[2,2,1,512]{3,2,1,0:T(2,128)(2,1)S(1)}, bf16[2,2,1,512]{3,2,1,0:T(2,128)(2,1)S(1)}, u32[]{:S(2)}, u32[]{:S(2)}) collective-permute-start(bf16[2,2,1,512]{3,2,1,0:T(2,128)(2,1)S(1)} %get-tuple-element.80), channel_id=1, source_target_pairs={{8,0},{9,1},{10,2},{11,3},{12,4},{13,5},{14,6},{15,7},{24,16},{25,... | collective-permute-start | bytes 12296 | tf_op jit(solution)/shard_map/ppermute | solution.py:15
  38.9 8.2 %collective-permute-start.6 = (bf16[2,1,34,512]{3,2,1,0:T(8,128)(2,1)S(1)}, bf16[2,1,34,512]{3,2,1,0:T(8,128)(2,1)S(1)}, u32[]{:S(2)}, u32[]{:S(2)}) collective-permute-start(bf16[2,1,34,512]{3,2,1,0:T(8,128)(2,1)S(1)} %get-tuple-element.57), channel_id=1, source_target_pairs={{0,1},{1,2},{2,3},{3,4},{4,5},{5,6},{6,7},{8,9},{9,10},{10,11},{11... | collective-permute-start | bytes 208904 | tf_op jit(solution)/shard_map/ppermute | solution.py:12
  43.3 3.9 %copy-start.19 = (bf16[256]{0:T(256)(128)(2,1)S(1)}, bf16[256]{0:T(256)(128)(2,1)}, u32[]{:S(2)}) copy-start(bf16[256]{0:T(256)(128)(2,1)} %param.11) | copy-start | bytes 1540
  43.3 7.1 %collective-permute-start.7 = (bf16[2,1,34,512]{3,2,1,0:T(8,128)(2,1)S(1)}, bf16[2,1,34,512]{3,2,1,0:T(8,128)(2,1)S(1)}, u32[]{:S(2)}, u32[]{:S(2)}) collective-permute-start(bf16[2,1,34,512]{3,2,1,0:T(8,128)(2,1)S(1)} %get-tuple-element.58), channel_id=1, source_target_pairs={{1,0},{2,1},{3,2},{4,3},{5,4},{6,5},{7,6},{9,8},{10,9},{11,10},{12... | collective-permute-start | bytes 208904 | tf_op jit(solution)/shard_map/ppermute | solution.py:15
  53.1 1.0 copy-start.16
  53.1 3.5 %copy-start.15 = (bf16[4,64,512]{2,0,1:T(4,128)(2,1)S(1)}, bf16[4,64,512]{2,0,1:T(4,128)(2,1)}, u32[]{:S(2)}) copy-start(bf16[4,64,512]{2,0,1:T(4,128)(2,1)} %get-tuple-element.44) | copy-start | bytes 786436
  53.2 4.8 %copy-start.14 = (bf16[4,64,512]{2,0,1:T(4,128)(2,1)S(1)}, bf16[4,64,512]{2,0,1:T(4,128)(2,1)}, u32[]{:S(2)}) copy-start(bf16[4,64,512]{2,0,1:T(4,128)(2,1)} %get-tuple-element.43) | copy-start | bytes 786436
  53.2 6.1 %copy-start.13 = (bf16[4,64,512]{2,0,1:T(4,128)(2,1)S(1)}, bf16[4,64,512]{2,0,1:T(4,128)(2,1)}, u32[]{:S(2)}) copy-start(bf16[4,64,512]{2,0,1:T(4,128)(2,1)} %get-tuple-element.42) | copy-start | bytes 786436
  53.8 6.9 %copy-start.12 = (bf16[4,64,512]{2,0,1:T(4,128)(2,1)S(1)}, bf16[4,64,512]{2,0,1:T(4,128)(2,1)}, u32[]{:S(2)}) copy-start(bf16[4,64,512]{2,0,1:T(4,128)(2,1)} %get-tuple-element.41) | copy-start | bytes 786436
  54.1 7.9 %copy-start.11 = (bf16[4,64,512]{2,0,1:T(4,128)(2,1)S(1)}, bf16[4,64,512]{2,0,1:T(4,128)(2,1)}, u32[]{:S(2)}) copy-start(bf16[4,64,512]{2,0,1:T(4,128)(2,1)} %get-tuple-element.40) | copy-start | bytes 786436
  56.6 6.7 %copy-start.10 = (bf16[4,64,512]{2,0,1:T(4,128)(2,1)S(1)}, bf16[4,64,512]{2,0,1:T(4,128)(2,1)}, u32[]{:S(2)}) copy-start(bf16[4,64,512]{2,0,1:T(4,128)(2,1)} %get-tuple-element.39) | copy-start | bytes 786436
  59.2 6.7 %copy-start.1 = (bf16[3,3,512,256]{3,2,1,0:T(8,128)(2,1)S(1)}, bf16[3,3,512,256]{3,2,1,0:T(8,128)(2,1)}, u32[]{:S(2)}) copy-start(bf16[3,3,512,256]{3,2,1,0:T(8,128)(2,1)} %convert_add_fusion.1) | copy-start | bytes 7077892
  68.7 4.9 %copy-start.2 = (bf16[3,3,3,256,128]{4,3,2,1,0:T(8,128)(2,1)S(1)}, bf16[3,3,3,256,128]{4,3,2,1,0:T(8,128)(2,1)}, u32[]{:S(2)}) copy-start(bf16[3,3,3,256,128]{4,3,2,1,0:T(8,128)(2,1)} %param.12) | copy-start | bytes 5308420
  69.9 11.5 %copy-start.20 = (bf16[128]{0:T(256)(128)(2,1)S(1)}, bf16[128]{0:T(256)(128)(2,1)}, u32[]{:S(2)}) copy-start(bf16[128]{0:T(256)(128)(2,1)} %param.13) | copy-start | bytes 772
  70.4 4.4 %collective-permute-start.8 = (bf16[2,4,1,256]{3,2,1,0:T(2,128)(2,1)S(1)}, bf16[2,4,1,256]{3,2,1,0:T(2,128)(2,1)S(1)}, u32[]{:S(2)}, u32[]{:S(2)}) collective-permute-start(bf16[2,4,1,256]{3,2,1,0:T(2,128)(2,1)S(1)} %get-tuple-element.55), channel_id=1, source_target_pairs={{0,8},{1,9},{2,10},{3,11},{4,12},{5,13},{6,14},{7,15},{16,24},{17,... | collective-permute-start | bytes 12296 | tf_op jit(solution)/shard_map/ppermute | solution.py:12
  72.3 3.1 %collective-permute-start.9 = (bf16[2,4,1,256]{3,2,1,0:T(2,128)(2,1)S(1)}, bf16[2,4,1,256]{3,2,1,0:T(2,128)(2,1)S(1)}, u32[]{:S(2)}, u32[]{:S(2)}) collective-permute-start(bf16[2,4,1,256]{3,2,1,0:T(2,128)(2,1)S(1)} %get-tuple-element.56), channel_id=1, source_target_pairs={{8,0},{9,1},{10,2},{11,3},{12,4},{13,5},{14,6},{15,7},{24,16},{25,... | collective-permute-start | bytes 12296 | tf_op jit(solution)/shard_map/ppermute | solution.py:15
  75.4 6.1 %collective-permute-start.10 = (bf16[2,1,66,256]{3,2,1,0:T(8,128)(2,1)S(1)}, bf16[2,1,66,256]{3,2,1,0:T(8,128)(2,1)S(1)}, u32[]{:S(2)}, u32[]{:S(2)}) collective-permute-start(bf16[2,1,66,256]{3,2,1,0:T(8,128)(2,1)S(1)} %get-tuple-element.53), channel_id=1, source_target_pairs={{0,1},{1,2},{2,3},{3,4},{4,5},{5,6},{6,7},{8,9},{9,10},{10,11},{11... | collective-permute-start | bytes 202760 | tf_op jit(solution)/shard_map/ppermute | solution.py:12
  78.9 6.3 %collective-permute-start.11 = (bf16[2,1,66,256]{3,2,1,0:T(8,128)(2,1)S(1)}, bf16[2,1,66,256]{3,2,1,0:T(8,128)(2,1)S(1)}, u32[]{:S(2)}, u32[]{:S(2)}) collective-permute-start(bf16[2,1,66,256]{3,2,1,0:T(8,128)(2,1)S(1)} %get-tuple-element.54), channel_id=1, source_target_pairs={{1,0},{2,1},{3,2},{4,3},{5,4},{6,5},{7,6},{9,8},{10,9},{11,10},{12... | collective-permute-start | bytes 202760 | tf_op jit(solution)/shard_map/ppermute | solution.py:15
  86.8 2.0 %copy-start.17 = (bf16[6,66,256]{2,1,0:T(8,128)(2,1)S(1)}, bf16[6,66,256]{2,1,0:T(8,128)(2,1)}, u32[]{:S(2)}) copy-start(bf16[6,66,256]{2,1,0:T(8,128)(2,1)} %get-tuple-element.47) | copy-start | bytes 608260
  92.5 1.0 copy-start.6
  92.5 1.2 %copy-start.9 = (bf16[3,3,256,128]{3,2,1,0:T(8,128)(2,1)S(1)}, bf16[3,3,256,128]{3,2,1,0:T(8,128)(2,1)}, u32[]{:S(2)}) copy-start(bf16[3,3,256,128]{3,2,1,0:T(8,128)(2,1)} %get-tuple-element.10) | copy-start | bytes 1769476
  92.5 1.5 %copy-start.5 = (bf16[8,128,256]{2,1,0:T(8,128)(2,1)S(1)}, bf16[8,128,256]{2,1,0:T(8,128)(2,1)}, u32[]{:S(2)}) copy-start(bf16[8,128,256]{2,1,0:T(8,128)(2,1)} %get-tuple-element.27) | copy-start | bytes 1572868
  92.5 1.8 %copy-start.4 = (bf16[8,128,256]{2,1,0:T(8,128)(2,1)S(1)}, bf16[8,128,256]{2,1,0:T(8,128)(2,1)}, u32[]{:S(2)}) copy-start(bf16[8,128,256]{2,1,0:T(8,128)(2,1)} %get-tuple-element.26) | copy-start | bytes 1572868
  92.5 2.1 %copy-start.3 = (bf16[8,128,256]{2,1,0:T(8,128)(2,1)S(1)}, bf16[8,128,256]{2,1,0:T(8,128)(2,1)}, u32[]{:S(2)}) copy-start(bf16[8,128,256]{2,1,0:T(8,128)(2,1)} %get-tuple-element.25) | copy-start | bytes 1572868
  94.0 2.4 %copy-start.8 = (bf16[3,3,256,128]{3,2,1,0:T(8,128)(2,1)S(1)}, bf16[3,3,256,128]{3,2,1,0:T(8,128)(2,1)}, u32[]{:S(2)}) copy-start(bf16[3,3,256,128]{3,2,1,0:T(8,128)(2,1)} %convert_add_fusion.2) | copy-start | bytes 1769476
  97.3 1.8 %copy-start.7 = (bf16[3,3,256,128]{3,2,1,0:T(8,128)(2,1)S(1)}, bf16[3,3,256,128]{3,2,1,0:T(8,128)(2,1)}, u32[]{:S(2)}) copy-start(bf16[3,3,256,128]{3,2,1,0:T(8,128)(2,1)} %get-tuple-element.9) | copy-start | bytes 1769476
where the time goes:
time: 108 us; the launch traced here: 107 us
  matrix products  28.4 us (26%)
  starting transfers between devices  26.9 us (25%)
  other arithmetic  16 us (15%)
  local copies, waits for them, and re-layouts  14.7 us (14%)
  waiting for transfers between devices  11.6 us (11%)
  blocking collectives  7.99 us (7%)
  between operations  1.41 us (1%)
    ppermute x6, starting transfers between devices, with_halo(): lax.ppermute(lax.slice_in_dim(block, block.shape[dim] - width, None, axis...  18.8 us
    dot_general x27, matrix products, paired_taps(): jnp.dot(window(prev_pad, row_tap, col_tap, row_count, col_count), weight_...  15.2 us
    ppermute x6, waiting for transfers between devices, with_halo(): lax.ppermute(lax.slice_in_dim(block, 0, width, axis=dim), axis, backward)  11.6 us
    add x3, other arithmetic, merge_weights(): return (weight_early + weight[2].astype(jnp.float32), weight_early)  9.81 us
    ppermute x6, starting transfers between devices, with_halo(): lax.ppermute(lax.slice_in_dim(block, 0, width, axis=dim), axis, backward)  8.15 us
    dot_general x27, matrix products, paired_taps(): jnp.dot(window(cur_pad, row_tap, col_tap, row_count, col_count), weight_n...  6.63 us
    dot_general x27, matrix products, single_taps(): jnp.dot(window(padded, row_tap, col_tap, row_count, col_count), weight_al...  6.58 us
    slice x23, local copies, waits for them, and re-layouts, window(): padded[row_tap:row_tap + row_count, col_tap:col_tap + col_count]  6.17 us
  transfers between devices with their start and end apart: 12, of which 4 were waited for; matrix products, arithmetic and copies ran while one was open for 14% of the time, Pallas kernels for 0%

commit v1 on v0

v1 whole, which is shorter than its diff:
```python
import functools

import jax
import jax.numpy as jnp
from jax import lax
from jax.experimental import pallas as pl
from jax.experimental.pallas import tpu as pltpu
from jax.sharding import PartitionSpec as P

F32 = jnp.float32
BF16 = jnp.bfloat16


def silu(v):
    return v / (1.0 + jnp.exp(-v))


def shifted(v):
    count = v.shape[0]
    column = lax.broadcasted_iota(jnp.int32, v.shape, 0)
    before = jnp.where(column == 0, 0.0, pltpu.roll(v, 1, 0))
    after = jnp.where(column == count - 1, 0.0, pltpu.roll(v, count - 1, 0))
    return before, after


def dot(a, b):
    return jnp.dot(a, b, preferred_element_type=F32)


def merge_time(source, target):
    cin = source.shape[3]
    step = 32

    def body(n, _):
        at = pl.multiple_of(n * step, step)
        for i in range(3):
            for j in range(3):
                total = source[0, i, j, pl.ds(at, step), :] + source[1, i, j, pl.ds(at, step), :]
                target[i, pl.ds(j * cin + at, step), :] = total
        return 0

    lax.fori_loop(0, cin // step, body, 0)


def merge_space(source, target, step):
    cin, cout = source.shape[3], source.shape[4]

    def body(n, _):
        at = pl.multiple_of(n * step, step)
        for t in range(2):
            tap = {}
            for i in range(3):
                for j in range(3):
                    if t == 0:
                        tap[i, j] = source[0, i, j, pl.ds(at, step), :].astype(F32) + source[
                            1, i, j, pl.ds(at, step), :
                        ].astype(F32)
                    else:
                        tap[i, j] = source[2, i, j, pl.ds(at, step), :].astype(F32)
            for a in range(2):
                for i in range(2):
                    if a == i:
                        lo = i
                        row = [tap[lo, j] + tap[lo + 1, j] for j in range(3)]
                    else:
                        row = [tap[2 * i, j] for j in range(3)]
                    for b in range(2):
                        if b == 0:
                            columns = (row[0] + row[1], row[2])
                        else:
                            columns = (row[0], row[1] + row[2])
                        for j in range(2):
                            target[t, b, i, pl.ds(j * cin + at, step), pl.ds(a * cout, cout)] = columns[
                                j
                            ].astype(BF16)
        return 0

    lax.fori_loop(0, cin // step, body, 0)


def kernel(
    flags, own, halo, own0, halo0, w1, b1, w2, b2, w3, b3, out, v1, v2, v3, xcat, mcat, lcat, wide
):
    rows, cols, c1 = own.shape
    c2 = b2.shape[1]
    c3 = b3.shape[1]
    second = flags[0] > 0
    first_tile = flags[1] > 0
    last_tile = flags[2] > 0
    merge_time(w1, v1)
    merge_space(w2, v2, 16)
    merge_space(w3, v3, 16)

    def feature(f, r):
        if r < 2:
            mine, other = halo[r], halo0[r]
        elif r < rows + 2:
            mine, other = own[r - 2], own0[r - 2]
        else:
            mine, other = halo[r - rows], halo0[r - rows]
        mine = mine.astype(F32)
        if f == 1:
            return mine
        return jnp.where(second, other.astype(F32), mine)

    for f in range(2):
        for r in range(rows + 4):
            v = silu(feature(f, r))
            before, after = shifted(v)
            xcat[f, r, :, 0:c1] = before.astype(BF16)
            xcat[f, r, :, c1 : 2 * c1] = v.astype(BF16)
            xcat[f, r, :, 2 * c1 : 3 * c1] = after.astype(BF16)

    mrows = rows + 2
    early = jnp.zeros((mrows * cols, c1), F32)
    now = [early, early]
    for i in range(3):
        lhs = [xcat[f, i : i + mrows].reshape(mrows * cols, 3 * c1) for f in range(2)]
        early = early + dot(lhs[0], v1[i])
        for f in range(2):
            now[f] = now[f] + dot(lhs[f], w1[2, i].reshape(3 * c1, c1))
    bias = b1[...].astype(F32)
    for f in range(2):
        total = early + now[f] + bias
        for m in range(mrows):
            v = total[m * cols : (m + 1) * cols] + feature(f, m + 1)
            v = silu(v.astype(BF16).astype(F32))
            if m == 0:
                v = jnp.where(first_tile, 0.0, v)
            if m == mrows - 1:
                v = jnp.where(last_tile, 0.0, v)
            before, after = shifted(v)
            mcat[f, m, :, 0:c1] = before.astype(BF16)
            mcat[f, m, :, c1 : 2 * c1] = v.astype(BF16)
            mcat[f, m, :, 2 * c1 : 3 * c1] = after.astype(BF16)

    wins = mrows - 1
    bias = b2[...].astype(F32)
    for b in range(2):
        lanes = slice(c1, 3 * c1) if b == 0 else slice(0, 2 * c1)
        early = jnp.zeros((wins * cols, 2 * c2), F32)
        now = [early, early]
        for i in range(2):
            lhs = [mcat[f, i : i + wins, :, lanes].reshape(wins * cols, 2 * c1) for f in range(2)]
            early = early + dot(lhs[0], v2[0, b, i])
            for f in range(2):
                now[f] = now[f] + dot(lhs[f], v2[1, b, i])
        for f in range(2):
            total = early + now[f]
            for w in range(wins):
                for a in range(2):
                    v = total[w * cols : (w + 1) * cols, a * c2 : (a + 1) * c2] + bias
                    v = silu(v)
                    if w == 0 and a == 0:
                        v = jnp.where(first_tile, 0.0, v)
                    if w == wins - 1 and a == 1:
                        v = jnp.where(last_tile, 0.0, v)
                    before, after = shifted(v)
                    r = 2 * w + a
                    if b == 0:
                        lcat[f, r, :, 0:c2] = before.astype(BF16)
                        lcat[f, r, :, 2 * c2 : 3 * c2] = v.astype(BF16)
                    else:
                        lcat[f, r, :, c2 : 2 * c2] = v.astype(BF16)
                        lcat[f, r, :, 3 * c2 : 4 * c2] = after.astype(BF16)

    lrows = 2 * wins
    wins = lrows - 1
    bias = b3[...].astype(F32)
    for q in range(4):
        b = 1 if q % 2 == 0 else 0
        at = (0, c2, c2, 2 * c2)[q]
        total = jnp.zeros((wins * cols, 2 * c3), F32)
        for i in range(2):
            for f in range(2):
                lhs = lcat[f, i : i + wins, :, at : at + 2 * c2].reshape(wins * cols, 2 * c2)
                total = total + dot(lhs, v3[f, b, i])
        for o in range(4 * rows):
            a = 1 - o % 2
            w = (o + 1) // 2
            v = total[w * cols : (w + 1) * cols, a * c3 : (a + 1) * c3] + bias
            wide[o, pl.ds(q, cols, stride=4), :] = v
    for o in range(4 * rows):
        out[o] = wide[o].astype(BF16)


def in_vmem(x):
    return pltpu.with_memory_space_constraint(x, pltpu.VMEM)


def per_device(features, conv_first, bias_first, conv_second, bias_second, conv_third, bias_third):
    own = features[0]
    rows, cols, c1 = own.shape
    c2 = conv_second.shape[4]
    c3 = conv_third.shape[4]
    tiles = lax.axis_size("tile")
    forward = [(i, i + 1) for i in range(tiles - 1)]
    backward = [(i + 1, i) for i in range(tiles - 1)]
    across = [(0, 1)]
    own0 = lax.ppermute(own, "sect", across)
    top = lax.ppermute(own[rows - 2 :], "tile", forward)
    bottom = lax.ppermute(own[:2], "tile", backward)
    halo = jnp.concatenate([top, bottom], axis=0)
    halo0 = lax.ppermute(halo, "sect", across)
    tile = lax.axis_index("tile")
    flags = jnp.stack([lax.axis_index("sect"), (tile == 0).astype(jnp.int32), (tile == tiles - 1).astype(jnp.int32)])
    vmem = pl.BlockSpec(memory_space=pltpu.VMEM)
    out = pl.pallas_call(
        kernel,
        out_shape=jax.ShapeDtypeStruct((4 * rows, 4 * cols, c3), BF16),
        in_specs=[pl.BlockSpec(memory_space=pltpu.SMEM)] + [vmem] * 10,
        out_specs=vmem,
        scratch_shapes=[
            pltpu.VMEM((3, 3 * c1, c1), BF16),
            pltpu.VMEM((2, 2, 2, 2 * c1, 2 * c2), BF16),
            pltpu.VMEM((2, 2, 2, 2 * c2, 2 * c3), BF16),
            pltpu.VMEM((2, rows + 4, cols, 3 * c1), BF16),
            pltpu.VMEM((2, rows + 2, cols, 3 * c1), BF16),
            pltpu.VMEM((2, 2 * rows + 2, cols, 4 * c2), BF16),
            pltpu.VMEM((4 * rows, 4 * cols, c3), F32),
        ],
        compiler_params=pltpu.CompilerParams(vmem_limit_bytes=36 << 20),
    )(
        flags,
        own,
        halo,
        own0,
        halo0,
        in_vmem(conv_first),
        bias_first.reshape(1, c1),
        in_vmem(conv_second),
        bias_second.reshape(1, c2),
        in_vmem(conv_third),
        bias_third.reshape(1, c3),
    )
    return out[None]


def solution(mesh):
    return jax.shard_map(
        per_device,
        mesh=mesh,
        in_specs=(P(("groups", "sect"), "tile", None, None), P(), P(), P(), P(), P(), P()),
        out_specs=P(("groups", "sect"), "tile", None, None),
        check_vma=False,
    )
```

time: 108 us -> 40.9 us (0.38)
  matrix products: 28.4 us -> 0 us
  starting transfers between devices: 26.9 us -> 8.79 us
  other arithmetic: 16 us -> 0.61 us
  Pallas kernels: 0 us -> 12.6 us
  blocking collectives: 7.99 us -> 0 us
  waiting for transfers between devices: 11.6 us -> 5.77 us
  local copies, waits for them, and re-layouts: 14.7 us -> 12.7 us
  between operations: 1.41 us -> 0.08 us
    dot_general x81 -> x0, matrix products: 28.4 us -> none  [the longest x27 15.2 us: paired_taps(): jnp.dot(window(prev_pad, row_tap, col_tap, row_count, col_count), weight_...]
    ppermute x12 -> x4, starting transfers between devices: 26.9 us -> 8.79 us  [the longest x1 4.9 us: per_device(): top = lax.ppermute(own[rows - 2:], 'tile', forward)]
    pallas_call x0 -> x1, Pallas kernels: none -> 12.6 us  [per_device(): pl.pallas_call(kernel, out_shape=jax.ShapeDtypeStruct((4 * rows, 4 * cols...]
    add x5 -> x0, other arithmetic: 9.87 us -> none  [the longest x3 9.81 us: merge_weights(): return (weight_early + weight[2].astype(jnp.float32), weight_early)]
    unnamed x47 -> x13, local copies, waits for them, and re-layouts: 1.73 us -> 10.2 us
    all_to_all x2 -> x0, blocking collectives: 7.99 us -> none  [the longest x1 4.15 us: per_device(): lax.all_to_all(decoded, 'sect', split_axis=0, concat_axis=2, tiled=True)]
    slice x28 -> x0, local copies, waits for them, and re-layouts: 6.25 us -> none  [the longest x23 6.17 us: window(): padded[row_tap:row_tap + row_count, col_tap:col_tap + col_count]]
    ppermute x12 -> x4, waiting for transfers between devices: 11.6 us -> 5.77 us  [the longest x1 4.02 us: per_device(): bottom = lax.ppermute(own[:2], 'tile', backward)]
  transfers between devices with their start and end apart: 12 -> 4, of which waited for: 4 -> 2; matrix products, arithmetic and copies ran while one was open for 14% -> 8% of each run, Pallas kernels for 0% -> 0%
where the time goes in v1:
time: 40.9 us; the launch traced here: 40.6 us
  local copies, waits for them, and re-layouts  12.7 us (31%)
  Pallas kernels  12.6 us (31%)
  starting transfers between devices  8.79 us (21%)
  waiting for transfers between devices  5.77 us (14%)
  other arithmetic  0.61 us (1%)
    pallas_call x1, Pallas kernels, per_device(): pl.pallas_call(kernel, out_shape=jax.ShapeDtypeStruct((4 * rows, 4 * cols...  12.6 us
    unnamed x13, local copies, waits for them, and re-layouts  10.2 us
    ppermute x1, starting transfers between devices, per_device(): top = lax.ppermute(own[rows - 2:], 'tile', forward)  4.9 us
    ppermute x1, waiting for transfers between devices, per_device(): bottom = lax.ppermute(own[:2], 'tile', backward)  4.02 us
    ppermute x1, waiting for transfers between devices, per_device(): top = lax.ppermute(own[rows - 2:], 'tile', forward)  1.75 us
    ppermute x1, starting transfers between devices, per_device(): halo0 = lax.ppermute(halo, 'sect', across)  1.31 us
    ppermute x1, starting transfers between devices, per_device(): own0 = lax.ppermute(own, 'sect', across)  1.3 us
    ppermute x1, starting transfers between devices, per_device(): bottom = lax.ppermute(own[:2], 'tile', backward)  1.29 us
  transfers between devices with their start and end apart: 4, of which 2 were waited for; matrix products, arithmetic and copies ran while one was open for 8% of the time, Pallas kernels for 0%

profile of v1, /device:TPU:0, one launch (start us, length us, event | category | flops | bytes accessed | tf_op | source)
XLA Modules:
  0.0 40.6 jit_solution(11290040574378333668)
XLA Ops:
  0.0 4.9 %collective-permute-start = (bf16[2,64,512]{2,1,0:T(8,128)(2,1)}, bf16[2,64,512]{2,1,0:T(8,128)(2,1)S(1)}, u32[]{:S(2)}, u32[]{:S(2)}) collective-permute-start(bf16[2,64,512]{2,1,0:T(8,128)(2,1)} %bitcast.6), channel_id=1, source_target_pairs={{0,1},{1,2},{2,3},{3,4},{4,5},{5,6},{6,7},{8,9},{9,10},{10,11},{11... | collective-permute-start | bytes 393224 | tf_op jit(solution)/shard_map/ppermute | solution.py:201
  4.9 1.3 %collective-permute-start.1 = (bf16[2,64,512]{2,1,0:T(8,128)(2,1)}, bf16[2,64,512]{2,1,0:T(8,128)(2,1)S(1)}, u32[]{:S(2)}, u32[]{:S(2)}) collective-permute-start(bf16[2,64,512]{2,1,0:T(8,128)(2,1)} %bitcast.7), channel_id=1, source_target_pairs={{1,0},{2,1},{3,2},{4,3},{5,4},{6,5},{7,6},{9,8},{10,9},{11,10},{12... | collective-permute-start | bytes 393224 | tf_op jit(solution)/shard_map/ppermute | solution.py:202
  6.2 1.7 %collective-permute-done = bf16[2,64,512]{2,1,0:T(8,128)(2,1)S(1)} collective-permute-done((bf16[2,64,512]{2,1,0:T(8,128)(2,1)}, bf16[2,64,512]{2,1,0:T(8,128)(2,1)S(1)}, u32[]{:S(2)}, u32[]{:S(2)}) %collective-permute-start) | collective-permute-done | bytes 131104 | tf_op jit(solution)/shard_map/ppermute | solution.py:201
  8.0 4.0 %collective-permute-done.1 = bf16[2,64,512]{2,1,0:T(8,128)(2,1)S(1)} collective-permute-done((bf16[2,64,512]{2,1,0:T(8,128)(2,1)}, bf16[2,64,512]{2,1,0:T(8,128)(2,1)S(1)}, u32[]{:S(2)}, u32[]{:S(2)}) %collective-permute-start.1) | collective-permute-done | bytes 131104 | tf_op jit(solution)/shard_map/ppermute | solution.py:202
  12.0 0.0 copy-start.3
  12.0 1.3 %collective-permute-start.3 = (bf16[4,64,512]{2,1,0:T(8,128)(2,1)S(1)}, bf16[4,64,512]{2,1,0:T(8,128)(2,1)S(1)}, u32[]{:S(2)}, u32[]{:S(2)}) collective-permute-start(bf16[4,64,512]{2,1,0:T(8,128)(2,1)S(1)} %constant_dynamic-update-slice_fusion.halo), channel_id=1, source_target_pairs={{0,8},{1,9},{2,10},{3,11},{4,12},{5,13},{6,14},{7,15},{16,24},{17,... | collective-permute-start | bytes 786440 | tf_op jit(solution)/shard_map/ppermute | solution.py:204
  13.3 1.3 %collective-permute-start.2 = (bf16[2,64,512]{2,1,0:T(8,128)(2,1)}, bf16[2,64,512]{2,1,0:T(8,128)(2,1)S(1)}, u32[]{:S(2)}, u32[]{:S(2)}) collective-permute-start(bf16[2,64,512]{2,1,0:T(8,128)(2,1)} %bitcast.8), channel_id=1, source_target_pairs={{0,8},{1,9},{2,10},{3,11},{4,12},{5,13},{6,14},{7,15},{16,24},{17,... | collective-permute-start | bytes 393224 | tf_op jit(solution)/shard_map/ppermute | solution.py:200
  14.6 1.2 %reshape.10.b2 = bf16[1,256]{1,0:T(2,128)(2,1)} reshape(bf16[256]{0:T(256)(128)(2,1)} %param.11) | data formatting | bytes 1024 | tf_op jit(solution)/shard_map/reshape | solution.py:232
  15.9 1.2 %reshape.9.b1 = bf16[1,512]{1,0:T(2,128)(2,1)} reshape(bf16[512]{0:T(512)(128)(2,1)} %param.9) | data formatting | bytes 2048 | tf_op jit(solution)/shard_map/reshape | solution.py:230
  17.1 0.6 %pad_add_fusion.flags = s32[3]{0:T(128)} fusion(s32[1]{0:T(128)} %bitcast.2, s32[1]{0:T(128)} %bitcast.1, s32[1]{0:T(128)} %bitcast), kind=kLoop, calls=%fused_computation.2 | loop fusion | flops 6 | bytes 24 | tf_op jit(solution)/shard_map/stack | solution.py:206
  17.7 0.0 collective-permute-done.2.own0
  17.7 0.0 copy-start.5
  17.7 0.0 collective-permute-done.3.halo0
  17.7 0.0 copy-start.4
  17.7 0.0 copy-done.3
  17.8 0.6 %copy-done.5 = bf16[2,64,512]{2,1,0:T(8,128)(2,1)} copy-done((bf16[2,64,512]{2,1,0:T(8,128)(2,1)}, bf16[2,64,512]{2,1,0:T(8,128)(2,1)S(1)}, u32[]{:S(2)}) %copy-start.5) | copy-done | bytes 131096
  18.4 0.1 copy-done.4
  18.5 0.0 copy-start
  18.5 5.0 %copy-done = bf16[3,3,3,512,512]{4,3,2,1,0:T(8,128)(2,1)S(1)} copy-done((bf16[3,3,3,512,512]{4,3,2,1,0:T(8,128)(2,1)S(1)}, bf16[3,3,3,512,512]{4,3,2,1,0:T(8,128)(2,1)}, u32[]{:S(2)}) %copy-start) | copy-done | bytes 14155800
  23.5 0.0 copy-start.1
  23.5 3.0 %copy-done.1 = bf16[3,3,3,512,256]{4,3,2,1,0:T(8,128)(2,1)S(1)} copy-done((bf16[3,3,3,512,256]{4,3,2,1,0:T(8,128)(2,1)S(1)}, bf16[3,3,3,512,256]{4,3,2,1,0:T(8,128)(2,1)}, u32[]{:S(2)}) %copy-start.1) | copy-done | bytes 7077912
  26.5 0.0 copy-start.2
  26.5 1.5 %copy-done.2 = bf16[3,3,3,256,128]{4,3,2,1,0:T(8,128)(2,1)S(1)} copy-done((bf16[3,3,3,256,128]{4,3,2,1,0:T(8,128)(2,1)S(1)}, bf16[3,3,3,256,128]{4,3,2,1,0:T(8,128)(2,1)}, u32[]{:S(2)}) %copy-start.2) | copy-done | bytes 1769496
  28.0 12.6 %shard_map.73 = bf16[8,256,128]{2,1,0:T(8,128)(2,1)} custom-call(s32[3]{0:T(128)} %pad_add_fusion.flags, bf16[2,64,512]{2,1,0:T(8,128)(2,1)} %bitcast.9, bf16[4,64,512]{2,1,0:T(8,128)(2,1)} %copy-done.3, bf16[2,64,512]{2,1,0:T(8,128)(2,1)} %copy-done.5, bf16[4,64,512]{2,1,0:T(8,128)(2,1)} %copy-done.4, bf16[3,3,3,512,512]{4,3,2,1,0:T(8,128)(2,1)S(1)} %copy-done, ...), custom_call_target="tpu_custom_call" | custom-call | tf_op jit(solution)/shard_map/pallas_call | solution.py:208
  (2 shorter events, 0.0 us)
Async XLA Ops:
  0.0 8.0 %collective-permute-start = (bf16[2,64,512]{2,1,0:T(8,128)(2,1)}, bf16[2,64,512]{2,1,0:T(8,128)(2,1)S(1)}, u32[]{:S(2)}, u32[]{:S(2)}) collective-permute-start(bf16[2,64,512]{2,1,0:T(8,128)(2,1)} %bitcast.6), channel_id=1, source_target_pairs={{0,1},{1,2},{2,3},{3,4},{4,5},{5,6},{6,7},{8,9},{9,10},{10,11},{11... | collective-permute-start | bytes 393224 | tf_op jit(solution)/shard_map/ppermute | solution.py:201
  4.9 7.1 %collective-permute-start.1 = (bf16[2,64,512]{2,1,0:T(8,128)(2,1)}, bf16[2,64,512]{2,1,0:T(8,128)(2,1)S(1)}, u32[]{:S(2)}, u32[]{:S(2)}) collective-permute-start(bf16[2,64,512]{2,1,0:T(8,128)(2,1)} %bitcast.7), channel_id=1, source_target_pairs={{1,0},{2,1},{3,2},{4,3},{5,4},{6,5},{7,6},{9,8},{10,9},{11,10},{12... | collective-permute-start | bytes 393224 | tf_op jit(solution)/shard_map/ppermute | solution.py:202
  12.0 5.8 %copy-start.3 = (bf16[4,64,512]{2,1,0:T(8,128)(2,1)}, bf16[4,64,512]{2,1,0:T(8,128)(2,1)S(1)}, u32[]{:S(2)}) copy-start(bf16[4,64,512]{2,1,0:T(8,128)(2,1)S(1)} %constant_dynamic-update-slice_fusion.halo) | copy-start | bytes 786436
  12.0 5.7 %collective-permute-start.3 = (bf16[4,64,512]{2,1,0:T(8,128)(2,1)S(1)}, bf16[4,64,512]{2,1,0:T(8,128)(2,1)S(1)}, u32[]{:S(2)}, u32[]{:S(2)}) collective-permute-start(bf16[4,64,512]{2,1,0:T(8,128)(2,1)S(1)} %constant_dynamic-update-slice_fusion.halo), channel_id=1, source_target_pairs={{0,8},{1,9},{2,10},{3,11},{4,12},{5,13},{6,14},{7,15},{16,24},{17,... | collective-permute-start | bytes 786440 | tf_op jit(solution)/shard_map/ppermute | solution.py:204
  13.3 4.4 %collective-permute-start.2 = (bf16[2,64,512]{2,1,0:T(8,128)(2,1)}, bf16[2,64,512]{2,1,0:T(8,128)(2,1)S(1)}, u32[]{:S(2)}, u32[]{:S(2)}) collective-permute-start(bf16[2,64,512]{2,1,0:T(8,128)(2,1)} %bitcast.8), channel_id=1, source_target_pairs={{0,8},{1,9},{2,10},{3,11},{4,12},{5,13},{6,14},{7,15},{16,24},{17,... | collective-permute-start | bytes 393224 | tf_op jit(solution)/shard_map/ppermute | solution.py:200
  17.7 0.6 %copy-start.5 = (bf16[2,64,512]{2,1,0:T(8,128)(2,1)}, bf16[2,64,512]{2,1,0:T(8,128)(2,1)S(1)}, u32[]{:S(2)}) copy-start(bf16[2,64,512]{2,1,0:T(8,128)(2,1)S(1)} %collective-permute-done.2.own0) | copy-start | bytes 393220
  17.7 0.7 %copy-start.4 = (bf16[4,64,512]{2,1,0:T(8,128)(2,1)}, bf16[4,64,512]{2,1,0:T(8,128)(2,1)S(1)}, u32[]{:S(2)}) copy-start(bf16[4,64,512]{2,1,0:T(8,128)(2,1)S(1)} %collective-permute-done.3.halo0) | copy-start | bytes 786436
  18.5 5.0 %copy-start = (bf16[3,3,3,512,512]{4,3,2,1,0:T(8,128)(2,1)S(1)}, bf16[3,3,3,512,512]{4,3,2,1,0:T(8,128)(2,1)}, u32[]{:S(2)}) copy-start(bf16[3,3,3,512,512]{4,3,2,1,0:T(8,128)(2,1)} %w1.1) | copy-start | bytes 42467332
  23.5 3.0 %copy-start.1 = (bf16[3,3,3,512,256]{4,3,2,1,0:T(8,128)(2,1)S(1)}, bf16[3,3,3,512,256]{4,3,2,1,0:T(8,128)(2,1)}, u32[]{:S(2)}) copy-start(bf16[3,3,3,512,256]{4,3,2,1,0:T(8,128)(2,1)} %w2.1) | copy-start | bytes 21233668
  26.5 1.5 %copy-start.2 = (bf16[3,3,3,256,128]{4,3,2,1,0:T(8,128)(2,1)S(1)}, bf16[3,3,3,256,128]{4,3,2,1,0:T(8,128)(2,1)}, u32[]{:S(2)}) copy-start(bf16[3,3,3,256,128]{4,3,2,1,0:T(8,128)(2,1)} %w3.1) | copy-start | bytes 5308420

commit v2 on v1

--- a/solution.py
+++ b/solution.py
@@ -1,5 +1,3 @@
-import functools
-
 import jax
 import jax.numpy as jnp
 from jax import lax
@@ -28,15 +26,14 @@
 
 
 def merge_time(source, target):
-    cin = source.shape[3]
-    step = 32
+    cin = source.shape[2]
+    step = 64
 
     def body(n, _):
         at = pl.multiple_of(n * step, step)
-        for i in range(3):
-            for j in range(3):
-                total = source[0, i, j, pl.ds(at, step), :] + source[1, i, j, pl.ds(at, step), :]
-                target[i, pl.ds(j * cin + at, step), :] = total
+        for j in range(3):
+            total = source[0, j, pl.ds(at, step), :] + source[1, j, pl.ds(at, step), :]
+            target[pl.ds(j * cin + at, step), :] = total
         return 0
 
     lax.fori_loop(0, cin // step, body, 0)
@@ -78,64 +75,114 @@
     lax.fori_loop(0, cin // step, body, 0)
 
 
-def kernel(
-    flags, own, halo, own0, halo0, w1, b1, w2, b2, w3, b3, out, v1, v2, v3, xcat, mcat, lcat, wide
+def put_cat(target, at, v):
+    chans = v.shape[1]
+    before, after = shifted(v)
+    target[(*at, slice(None), slice(0, chans))] = before.astype(BF16)
+    target[(*at, slice(None), slice(chans, 2 * chans))] = v.astype(BF16)
+    target[(*at, slice(None), slice(2 * chans, 3 * chans))] = after.astype(BF16)
+
+
+def early_kernel(pair, w1, acc, v1, wn, cat, raw, sems):
+    rows, cols, c1 = pair.shape[1:]
+    second = lax.axis_index("sect") > 0
+
+    def copy(t, i):
+        target = raw.at[i, t] if t < 2 else wn.at[i]
+        return pltpu.make_async_copy(w1.at[t, i], target, sems.at[i, t])
+
+    for i in range(3):
+        for t in range(3):
+            copy(t, i).start()
+    for r in range(rows):
+        mine, other = pair[0, r].astype(F32), pair[1, r].astype(F32)
+        put_cat(cat, (0, r), silu(jnp.where(second, other, mine)))
+        put_cat(cat, (1, r), silu(mine))
+    size = rows * cols
+    acc[...] = jnp.zeros(acc.shape, F32)
+
+    def tap(i, _):
+        for t in range(3):
+            copy(t, i).wait()
+        merge_time(raw.at[i], v1.at[i])
+        both = cat[...].reshape(2 * size, 3 * c1)
+        part = dot(both[:size], v1[i])
+        total = dot(both, wn[i].reshape(3 * c1, c1))
+        for f in range(2):
+            value = (total[f * size : (f + 1) * size] + part).reshape(rows, cols, c1)
+            acc[f, pl.ds(2 - i, rows)] += value
+        return 0
+
+    lax.fori_loop(0, 3, tap, 0)
+
+
+def late_kernel(
+    pair, far, near, acc, v1, wn, b1, w2, b2, w3, b3, out, hcat, mcat, lcat, wide, r2, r3, v2, v3, sems
 ):
-    rows, cols, c1 = own.shape
-    c2 = b2.shape[1]
-    c3 = b3.shape[1]
-    second = flags[0] > 0
-    first_tile = flags[1] > 0
-    last_tile = flags[2] > 0
-    merge_time(w1, v1)
-    merge_space(w2, v2, 16)
-    merge_space(w3, v3, 16)
+    rows, cols, c1 = pair.shape[1:]
+    c2 = b2.shape[0]
+    c3 = b3.shape[0]
+    second = lax.axis_index("sect") > 0
+    tile = lax.axis_index("tile")
+    first_tile = tile == 0
+    last_tile = tile == lax.axis_size("tile") - 1
+    copies = [
+        pltpu.make_async_copy(w2, r2, sems.at[0]),
+        pltpu.make_async_copy(w3, r3, sems.at[1]),
+    ]
+    for copy in copies:
+        copy.start()
 
     def feature(f, r):
         if r < 2:
-            mine, other = halo[r], halo0[r]
-        elif r < rows + 2:
-            mine, other = own[r - 2], own0[r - 2]
-        else:
-            mine, other = halo[r - rows], halo0[r - rows]
-        mine = mine.astype(F32)
-        if f == 1:
-            return mine
-        return jnp.where(second, other.astype(F32), mine)
-
+            if f == 0:
+                return jnp.where(second, far[0, r].astype(F32), near[0, r].astype(F32))
+            return jnp.where(second, far[1, r].astype(F32), near[0, r].astype(F32))
+        if r < rows + 2:
+            mine = pair[0, r - 2].astype(F32)
+            if f == 1:
+                return mine
+            return jnp.where(second, pair[1, r - 2].astype(F32), mine)
+        r = r - rows - 2
+        if f == 0:
+            return jnp.where(second, near[1, r].astype(F32), far[1, r].astype(F32))
+        return jnp.where(second, near[0, r].astype(F32), far[1, r].astype(F32))
+
+    mrows = rows + 2
     for f in range(2):
-        for r in range(rows + 4):
-            v = silu(feature(f, r))
-            before, after = shifted(v)
-            xcat[f, r, :, 0:c1] = before.astype(BF16)
-            xcat[f, r, :, c1 : 2 * c1] = v.astype(BF16)
-            xcat[f, r, :, 2 * c1 : 3 * c1] = after.astype(BF16)
-
-    mrows = rows + 2
-    early = jnp.zeros((mrows * cols, c1), F32)
-    now = [early, early]
-    for i in range(3):
-        lhs = [xcat[f, i : i + mrows].reshape(mrows * cols, 3 * c1) for f in range(2)]
-        early = early + dot(lhs[0], v1[i])
+        for r in range(4):
+            put_cat(hcat, (f, r), silu(feature(f, r if r < 2 else r + rows)))
+    size = 2 * cols
+
+    def tap(i, _):
+        lhs = jnp.concatenate([hcat[f, pl.ds(i, 2)].reshape(size, 3 * c1) for f in range(2)], axis=0)
+        part = dot(lhs[:size], v1[i])
+        total = dot(lhs, wn[i].reshape(3 * c1, c1))
         for f in range(2):
-            now[f] = now[f] + dot(lhs[f], w1[2, i].reshape(3 * c1, c1))
-    bias = b1[...].astype(F32)
+            value = (total[f * size : (f + 1) * size] + part).reshape(2, cols, c1)
+            acc[f, jnp.where(i < 2, 0, rows)] += value[0]
+            acc[f, jnp.where(i < 1, 1, rows + 1)] += value[1]
+        return 0
+
+    lax.fori_loop(0, 3, tap, 0)
+    bias = b1[...].astype(F32)[None, :]
     for f in range(2):
-        total = early + now[f] + bias
         for m in range(mrows):
-            v = total[m * cols : (m + 1) * cols] + feature(f, m + 1)
+            v = acc[f, m] + bias + feature(f, m + 1)
             v = silu(v.astype(BF16).astype(F32))
             if m == 0:
                 v = jnp.where(first_tile, 0.0, v)
             if m == mrows - 1:
                 v = jnp.where(last_tile, 0.0, v)
-            before, after = shifted(v)
-            mcat[f, m, :, 0:c1] = before.astype(BF16)
-            mcat[f, m, :, c1 : 2 * c1] = v.astype(BF16)
-            mcat[f, m, :, 2 * c1 : 3 * c1] = after.astype(BF16)
+            put_cat(mcat, (f, m), v)
+
+    copies[0].wait()
+    merge_space(r2, v2, 16)
+    copies[1].wait()
+    merge_space(r3, v3, 16)
 
     wins = mrows - 1
-    bias = b2[...].astype(F32)
+    bias = b2[...].astype(F32)[None, :]
     for b in range(2):
         lanes = slice(c1, 3 * c1) if b == 0 else slice(0, 2 * c1)
         early = jnp.zeros((wins * cols, 2 * c2), F32)
@@ -166,7 +213,7 @@
 
     lrows = 2 * wins
     wins = lrows - 1
-    bias = b3[...].astype(F32)
+    bias = b3[...].astype(F32)[None, :]
     for q in range(4):
         b = 1 if q % 2 == 0 else 0
         at = (0, c2, c2, 2 * c2)[q]
@@ -194,44 +241,66 @@
     c2 = conv_second.shape[4]
     c3 = conv_third.shape[4]
     tiles = lax.axis_size("tile")
-    forward = [(i, i + 1) for i in range(tiles - 1)]
-    backward = [(i + 1, i) for i in range(tiles - 1)]
-    across = [(0, 1)]
-    own0 = lax.ppermute(own, "sect", across)
-    top = lax.ppermute(own[rows - 2 :], "tile", forward)
-    bottom = lax.ppermute(own[:2], "tile", backward)
-    halo = jnp.concatenate([top, bottom], axis=0)
-    halo0 = lax.ppermute(halo, "sect", across)
-    tile = lax.axis_index("tile")
-    flags = jnp.stack([lax.axis_index("sect"), (tile == 0).astype(jnp.int32), (tile == tiles - 1).astype(jnp.int32)])
+    swap = [(0, 1), (1, 0)]
+    apart = [(i, tiles + i + 1) for i in range(tiles - 1)]
+    apart += [(tiles + i + 1, i) for i in range(tiles - 1)]
     vmem = pl.BlockSpec(memory_space=pltpu.VMEM)
+    anywhere = pl.BlockSpec(memory_space=pl.ANY)
+
+    pair = jnp.stack([own, lax.ppermute(own, "sect", swap)])
+    if rows == 2:
+        edge = pair
+    else:
+        edge = jnp.where(lax.axis_index("sect") == 0, pair[:, rows - 2 :], pair[:, :2])
+    far = lax.ppermute(edge, ("sect", "tile"), apart)
+    near = lax.ppermute(far, "sect", swap)
+    acc, v1, wn = pl.pallas_call(
+        early_kernel,
+        out_shape=[
+            pltpu.VMEM((2, rows + 2, cols, c1), F32),
+            pltpu.VMEM((3, 3 * c1, c1), BF16),
+            pltpu.VMEM((3, 3, c1, c1), BF16),
+        ],
+        in_specs=[vmem, anywhere],
+        out_specs=[vmem] * 3,
+        scratch_shapes=[
+            pltpu.VMEM((2, rows, cols, 3 * c1), BF16),
+            pltpu.VMEM((3, 2, 3, c1, c1), BF16),
+            pltpu.SemaphoreType.DMA((3, 3)),
+        ],
+        cost_estimate=pl.CostEstimate(flops=6_000_000_000, bytes_accessed=1024, transcendentals=0),
+        compiler_params=pltpu.CompilerParams(vmem_limit_bytes=16 << 20),
+    )(in_vmem(pair), pltpu.with_memory_space_constraint(conv_first, pltpu.HBM))
     out = pl.pallas_call(
-        kernel,
+        late_kernel,
         out_shape=jax.ShapeDtypeStruct((4 * rows, 4 * cols, c3), BF16),
-        in_specs=[pl.BlockSpec(memory_space=pltpu.SMEM)] + [vmem] * 10,
+        in_specs=[vmem] * 7 + [anywhere, vmem, anywhere, vmem],
         out_specs=vmem,
         scratch_shapes=[
-            pltpu.VMEM((3, 3 * c1, c1), BF16),
-            pltpu.VMEM((2, 2, 2, 2 * c1, 2 * c2), BF16),
-            pltpu.VMEM((2, 2, 2, 2 * c2, 2 * c3), BF16),
-            pltpu.VMEM((2, rows + 4, cols, 3 * c1), BF16),
+            pltpu.VMEM((2, 4, cols, 3 * c1), BF16),
             pltpu.VMEM((2, rows + 2, cols, 3 * c1), BF16),
             pltpu.VMEM((2, 2 * rows + 2, cols, 4 * c2), BF16),
             pltpu.VMEM((4 * rows, 4 * cols, c3), F32),
+            pltpu.VMEM(conv_second.shape, BF16),
+            pltpu.VMEM(conv_third.shape, BF16),
+            pltpu.VMEM((2, 2, 2, 2 * c1, 2 * c2), BF16),
+            pltpu.VMEM((2, 2, 2, 2 * c2, 2 * c3), BF16),
+            pltpu.SemaphoreType.DMA((2,)),
         ],
+        cost_estimate=pl.CostEstimate(flops=8_000_000_000, bytes_accessed=1024, transcendentals=0),
         compiler_params=pltpu.CompilerParams(vmem_limit_bytes=36 << 20),
     )(
-        flags,
-        own,
-        halo,
-        own0,
-        halo0,
-        in_vmem(conv_first),
-        bias_first.reshape(1, c1),
-        in_vmem(conv_second),
-        bias_second.reshape(1, c2),
-        in_vmem(conv_third),
-        bias_third.reshape(1, c3),
+        in_vmem(pair),
+        in_vmem(far),
+        in_vmem(near),
+        in_vmem(acc),
+        in_vmem(v1),
+        in_vmem(wn),
+        bias_first,
+        pltpu.with_memory_space_constraint(conv_second, pltpu.HBM),
+        bias_second,
+        pltpu.with_memory_space_constraint(conv_third, pltpu.HBM),
+        bias_third,
     )
     return out[None]
 

time: 40.9 us -> 31 us (0.76)
  local copies, waits for them, and re-layouts: 12.7 us -> 0.02 us
  Pallas kernels: 12.6 us -> 16.7 us
  starting transfers between devices: 8.79 us -> 5.15 us
  waiting for transfers between devices: 5.77 us -> 7.88 us
    unnamed x13 -> x6, local copies, waits for them, and re-layouts: 10.2 us -> 0.02 us
    pallas_call x1 -> x2, Pallas kernels: 12.6 us -> 16.7 us  [the longest x1 10.6 us: per_device(): pl.pallas_call(late_kernel, out_shape=jax.ShapeDtypeStruct((4 * rows, 4 *...]
    ppermute x4 -> x3, starting transfers between devices: 8.79 us -> 5.15 us  [the longest x1 4.66 us: per_device(): far = lax.ppermute(edge, ('sect', 'tile'), apart)]
    reshape x2 -> x0, local copies, waits for them, and re-layouts: 2.48 us -> none  [the longest x1 1.24 us: per_device(): bias_first.reshape(1, c1)]
    ppermute x4 -> x3, waiting for transfers between devices: 5.77 us -> 7.88 us  [the longest x1 6.68 us: per_device(): far = lax.ppermute(edge, ('sect', 'tile'), apart)]
  transfers between devices with their start and end apart: 4 -> 3, of which waited for: 2 -> 2; matrix products, arithmetic and copies ran while one was open for 8% -> 0% of each run, Pallas kernels for 0% -> 20%
where the time goes in v2:
time: 31 us; the launch traced here: 30.8 us
  Pallas kernels  16.7 us (54%)
  waiting for transfers between devices  7.88 us (25%)
  starting transfers between devices  5.15 us (17%)
  other arithmetic  0.93 us (3%)
    pallas_call x1, Pallas kernels, per_device(): pl.pallas_call(late_kernel, out_shape=jax.ShapeDtypeStruct((4 * rows, 4 *...  10.6 us
    ppermute x1, waiting for transfers between devices, per_device(): far = lax.ppermute(edge, ('sect', 'tile'), apart)  6.68 us
    pallas_call x1, Pallas kernels, per_device(): pl.pallas_call(early_kernel, out_shape=[pltpu.VMEM((2, rows + 2, cols, c1...  6.13 us
    ppermute x1, starting transfers between devices, per_device(): far = lax.ppermute(edge, ('sect', 'tile'), apart)  4.66 us
    ppermute x1, waiting for transfers between devices, per_device(): pair = jnp.stack([own, lax.ppermute(own, 'sect', swap)])  1.2 us
    another operation x1, other arithmetic, per_device(): pair = jnp.stack([own, lax.ppermute(own, 'sect', swap)])  0.93 us
  transfers between devices with their start and end apart: 3, of which 2 were waited for; matrix products, arithmetic and copies ran while one was open for 0% of the time, Pallas kernels for 20%

profile of v2, /device:TPU:0, one launch (start us, length us, event | category | flops | bytes accessed | tf_op | source)
XLA Modules:
  0.0 30.8 jit_solution(3150742825370140160)
XLA Ops:
  0.0 0.5 %collective-permute-start = (bf16[2,64,512]{2,1,0:T(8,128)(2,1)}, bf16[2,64,512]{2,1,0:T(8,128)(2,1)S(1)}, u32[]{:S(2)}, u32[]{:S(2)}) collective-permute-start(bf16[2,64,512]{2,1,0:T(8,128)(2,1)} %bitcast.3), channel_id=1, source_target_pairs={{0,8},{8,0},{1,9},{9,1},{2,10},{10,2},{3,11},{11,3},{4,12},{12,4},... | collective-permute-start | bytes 393224 | tf_op jit(solution)/shard_map/ppermute | solution.py:250
  0.5 1.2 %collective-permute-done = bf16[2,64,512]{2,1,0:T(8,128)(2,1)S(1)} collective-permute-done((bf16[2,64,512]{2,1,0:T(8,128)(2,1)}, bf16[2,64,512]{2,1,0:T(8,128)(2,1)S(1)}, u32[]{:S(2)}, u32[]{:S(2)}) %collective-permute-start) | collective-permute-done | bytes 131104 | tf_op jit(solution)/shard_map/ppermute | solution.py:250
  1.7 0.9 %pad_maximum_fusion.pair = bf16[2,2,64,512]{3,2,1,0:T(8,128)(2,1)S(1)} fusion(bf16[1,2,64,512]{3,2,1,0:T(8,128)(2,1)S(1)} %bitcast.4, bf16[1,2,64,512]{3,2,1,0:T(8,128)(2,1)} %param.7), kind=kLoop, calls=%fused_computation | loop fusion | flops 131072 | bytes 524288 | tf_op jit(solution)/shard_map/stack | solution.py:250
  2.6 0.0 copy-start
  2.6 0.0 copy-start.1
  2.6 0.0 copy-start.2
  2.7 4.7 %collective-permute-start.1 = (bf16[2,2,64,512]{3,2,1,0:T(8,128)(2,1)S(1)}, bf16[2,2,64,512]{3,2,1,0:T(8,128)(2,1)S(1)}, u32[]{:S(2)}, u32[]{:S(2)}) collective-permute-start(bf16[2,2,64,512]{3,2,1,0:T(8,128)(2,1)S(1)} %pad_maximum_fusion.pair), channel_id=1, source_target_pairs={{0,9},{1,10},{2,11},{3,12},{4,13},{5,14},{6,15},{9,0},{10,1},{11,2... | collective-permute-start | bytes 786440 | tf_op jit(solution)/shard_map/ppermute | solution.py:255
  7.3 6.7 %collective-permute-done.1.far = bf16[2,2,64,512]{3,2,1,0:T(8,128)(2,1)S(1)} collective-permute-done((bf16[2,2,64,512]{3,2,1,0:T(8,128)(2,1)S(1)}, bf16[2,2,64,512]{3,2,1,0:T(8,128)(2,1)S(1)}, u32[]{:S(2)}, u32[]{:S(2)}) %collective-permute-start.1) | collective-permute-done | bytes 262176 | tf_op jit(solution)/shard_map/ppermute | solution.py:255
  14.0 0.0 collective-permute-start.2
  14.0 6.1 %shard_map.73 = (f32[2,4,64,512]{3,2,1,0:T(8,128)S(1)}, bf16[3,1536,512]{2,1,0:T(8,128)(2,1)S(1)}, bf16[3,3,512,512]{3,2,1,0:T(8,128)(2,1)S(1)}) custom-call(bf16[2,2,64,512]{3,2,1,0:T(8,128)(2,1)S(1)} %pad_maximum_fusion.pair, bf16[3,3,3,512,512]{4,3,2,1,0:T(8,128)(2,1)} %w1.1), custom_call_target="tpu_custom_call" | custom-call | flops 6000000000 | bytes 1024 | tf_op jit(solution)/shard_map/pallas_call | solution.py:257
  20.1 0.0 collective-permute-done.2.near
  20.2 0.0 copy-done
  20.2 0.0 copy-done.1
  20.2 0.0 copy-done.2
  20.2 10.6 %shard_map.74 = bf16[8,256,128]{2,1,0:T(8,128)(2,1)} custom-call(bf16[2,2,64,512]{3,2,1,0:T(8,128)(2,1)S(1)} %pad_maximum_fusion.pair, bf16[2,2,64,512]{3,2,1,0:T(8,128)(2,1)S(1)} %collective-permute-done.1.far, bf16[2,2,64,512]{3,2,1,0:T(8,128)(2,1)S(1)} %collective-permute-done.2.near, f32[2,4,64,512]{3,2,1,0:T(8,128)S(1)} %get-tuple-element.8.acc, ...), custom_call_target="tpu_custom_call" | custom-call | flops 8000000000 | bytes 1024 | tf_op jit(solution)/shard_map/pallas_call | solution.py:274
Async XLA Ops:
  0.0 1.7 %collective-permute-start = (bf16[2,64,512]{2,1,0:T(8,128)(2,1)}, bf16[2,64,512]{2,1,0:T(8,128)(2,1)S(1)}, u32[]{:S(2)}, u32[]{:S(2)}) collective-permute-start(bf16[2,64,512]{2,1,0:T(8,128)(2,1)} %bitcast.3), channel_id=1, source_target_pairs={{0,8},{8,0},{1,9},{9,1},{2,10},{10,2},{3,11},{11,3},{4,12},{12,4},... | collective-permute-start | bytes 393224 | tf_op jit(solution)/shard_map/ppermute | solution.py:250
  2.6 17.5 %copy-start = (bf16[512]{0:T(512)(128)(2,1)S(1)}, bf16[512]{0:T(512)(128)(2,1)}, u32[]{:S(2)}) copy-start(bf16[512]{0:T(512)(128)(2,1)} %b1.1) | copy-start | bytes 3076
  2.6 17.5 %copy-start.1 = (bf16[256]{0:T(256)(128)(2,1)S(1)}, bf16[256]{0:T(256)(128)(2,1)}, u32[]{:S(2)}) copy-start(bf16[256]{0:T(256)(128)(2,1)} %b2.1) | copy-start | bytes 1540
  2.6 17.5 %copy-start.2 = (bf16[128]{0:T(256)(128)(2,1)S(1)}, bf16[128]{0:T(256)(128)(2,1)}, u32[]{:S(2)}) copy-start(bf16[128]{0:T(256)(128)(2,1)} %b3.1) | copy-start | bytes 772
  2.7 11.3 %collective-permute-start.1 = (bf16[2,2,64,512]{3,2,1,0:T(8,128)(2,1)S(1)}, bf16[2,2,64,512]{3,2,1,0:T(8,128)(2,1)S(1)}, u32[]{:S(2)}, u32[]{:S(2)}) collective-permute-start(bf16[2,2,64,512]{3,2,1,0:T(8,128)(2,1)S(1)} %pad_maximum_fusion.pair), channel_id=1, source_target_pairs={{0,9},{1,10},{2,11},{3,12},{4,13},{5,14},{6,15},{9,0},{10,1},{11,2... | collective-permute-start | bytes 786440 | tf_op jit(solution)/shard_map/ppermute | solution.py:255
  14.0 6.1 %collective-permute-start.2 = (bf16[2,2,64,512]{3,2,1,0:T(8,128)(2,1)S(1)}, bf16[2,2,64,512]{3,2,1,0:T(8,128)(2,1)S(1)}, u32[]{:S(2)}, u32[]{:S(2)}) collective-permute-start(bf16[2,2,64,512]{3,2,1,0:T(8,128)(2,1)S(1)} %collective-permute-done.1.far), channel_id=1, source_target_pairs={{0,8},{8,0},{1,9},{9,1},{2,10},{10,2},{3,11},{11,3},{4,12},{12,4},... | collective-permute-start | bytes 786440 | tf_op jit(solution)/shard_map/ppermute | solution.py:256

commit v3 on v2

--- a/solution.py
+++ b/solution.py
@@ -83,7 +83,12 @@
     target[(*at, slice(None), slice(2 * chans, 3 * chans))] = after.astype(BF16)
 
 
-def early_kernel(pair, w1, acc, v1, wn, cat, raw, sems):
+def pair_kernel(own, other, pair):
+    pair[0] = own[...]
+    pair[1] = other[...]
+
+
+def early_kernel(pair, w1, w2, w3, acc, v1, wn, v2, v3, cat, raw, sems):
     rows, cols, c1 = pair.shape[1:]
     second = lax.axis_index("sect") > 0
 
@@ -98,6 +103,8 @@
         mine, other = pair[0, r].astype(F32), pair[1, r].astype(F32)
         put_cat(cat, (0, r), silu(jnp.where(second, other, mine)))
         put_cat(cat, (1, r), silu(mine))
+    merge_space(w3, v3, 16)
+    merge_space(w2, v2, 16)
     size = rows * cols
     acc[...] = jnp.zeros(acc.shape, F32)
 
@@ -117,7 +124,7 @@
 
 
 def late_kernel(
-    pair, far, near, acc, v1, wn, b1, w2, b2, w3, b3, out, hcat, mcat, lcat, wide, r2, r3, v2, v3, sems
+    pair, far, near, acc, v1, wn, b1, v2, b2, v3, b3, out, hcat, mcat, lcat, wide
 ):
     rows, cols, c1 = pair.shape[1:]
     c2 = b2.shape[0]
@@ -126,12 +133,6 @@
     tile = lax.axis_index("tile")
     first_tile = tile == 0
     last_tile = tile == lax.axis_size("tile") - 1
-    copies = [
-        pltpu.make_async_copy(w2, r2, sems.at[0]),
-        pltpu.make_async_copy(w3, r3, sems.at[1]),
-    ]
-    for copy in copies:
-        copy.start()
 
     def feature(f, r):
         if r < 2:
@@ -175,11 +176,6 @@
             if m == mrows - 1:
                 v = jnp.where(last_tile, 0.0, v)
             put_cat(mcat, (f, m), v)
-
-    copies[0].wait()
-    merge_space(r2, v2, 16)
-    copies[1].wait()
-    merge_space(r3, v3, 16)
 
     wins = mrows - 1
     bias = b2[...].astype(F32)[None, :]
@@ -247,22 +243,32 @@
     vmem = pl.BlockSpec(memory_space=pltpu.VMEM)
     anywhere = pl.BlockSpec(memory_space=pl.ANY)
 
-    pair = jnp.stack([own, lax.ppermute(own, "sect", swap)])
+    other = lax.ppermute(own, "sect", swap)
+    pair = pl.pallas_call(
+        pair_kernel,
+        out_shape=pltpu.VMEM((2, rows, cols, c1), BF16),
+        in_specs=[vmem] * 2,
+        out_specs=vmem,
+        cost_estimate=pl.CostEstimate(flops=12_000_000_000, bytes_accessed=1024, transcendentals=0),
+        compiler_params=pltpu.CompilerParams(vmem_limit_bytes=1 << 20),
+    )(in_vmem(own), in_vmem(other))
     if rows == 2:
         edge = pair
     else:
         edge = jnp.where(lax.axis_index("sect") == 0, pair[:, rows - 2 :], pair[:, :2])
     far = lax.ppermute(edge, ("sect", "tile"), apart)
     near = lax.ppermute(far, "sect", swap)
-    acc, v1, wn = pl.pallas_call(
+    acc, v1, wn, v2, v3 = pl.pallas_call(
         early_kernel,
         out_shape=[
             pltpu.VMEM((2, rows + 2, cols, c1), F32),
             pltpu.VMEM((3, 3 * c1, c1), BF16),
             pltpu.VMEM((3, 3, c1, c1), BF16),
+            pltpu.VMEM((2, 2, 2, 2 * c1, 2 * c2), BF16),
+            pltpu.VMEM((2, 2, 2, 2 * c2, 2 * c3), BF16),
         ],
-        in_specs=[vmem, anywhere],
-        out_specs=[vmem] * 3,
+        in_specs=[vmem, anywhere, vmem, vmem],
+        out_specs=[vmem] * 5,
         scratch_shapes=[
             pltpu.VMEM((2, rows, cols, 3 * c1), BF16),
             pltpu.VMEM((3, 2, 3, c1, c1), BF16),
@@ -270,25 +276,25 @@
         ],
         cost_estimate=pl.CostEstimate(flops=6_000_000_000, bytes_accessed=1024, transcendentals=0),
         compiler_params=pltpu.CompilerParams(vmem_limit_bytes=16 << 20),
-    )(in_vmem(pair), pltpu.with_memory_space_constraint(conv_first, pltpu.HBM))
+    )(
+        in_vmem(pair),
+        pltpu.with_memory_space_constraint(conv_first, pltpu.HBM),
+        in_vmem(conv_second),
+        in_vmem(conv_third),
+    )
     out = pl.pallas_call(
         late_kernel,
         out_shape=jax.ShapeDtypeStruct((4 * rows, 4 * cols, c3), BF16),
-        in_specs=[vmem] * 7 + [anywhere, vmem, anywhere, vmem],
+        in_specs=[vmem] * 11,
         out_specs=vmem,
         scratch_shapes=[
             pltpu.VMEM((2, 4, cols, 3 * c1), BF16),
             pltpu.VMEM((2, rows + 2, cols, 3 * c1), BF16),
             pltpu.VMEM((2, 2 * rows + 2, cols, 4 * c2), BF16),
             pltpu.VMEM((4 * rows, 4 * cols, c3), F32),
-            pltpu.VMEM(conv_second.shape, BF16),
-            pltpu.VMEM(conv_third.shape, BF16),
-            pltpu.VMEM((2, 2, 2, 2 * c1, 2 * c2), BF16),
-            pltpu.VMEM((2, 2, 2, 2 * c2, 2 * c3), BF16),
-            pltpu.SemaphoreType.DMA((2,)),
         ],
         cost_estimate=pl.CostEstimate(flops=8_000_000_000, bytes_accessed=1024, transcendentals=0),
-        compiler_params=pltpu.CompilerParams(vmem_limit_bytes=36 << 20),
+        compiler_params=pltpu.CompilerParams(vmem_limit_bytes=14 << 20),
     )(
         in_vmem(pair),
         in_vmem(far),
@@ -297,9 +303,9 @@
         in_vmem(v1),
         in_vmem(wn),
         bias_first,
-        pltpu.with_memory_space_constraint(conv_second, pltpu.HBM),
+        in_vmem(v2),
         bias_second,
-        pltpu.with_memory_space_constraint(conv_third, pltpu.HBM),
+        in_vmem(v3),
         bias_third,
     )
     return out[None]

time: 31 us -> 29.2 us (0.942)
  Pallas kernels: 16.7 us -> 14.2 us
  local copies, waits for them, and re-layouts: 0.02 us -> 1.7 us
  other arithmetic: 0.93 us -> 0.01 us
    pallas_call x1, Pallas kernels: 10.6 us -> 8.08 us  [per_device(): pl.pallas_call(late_kernel, out_shape=jax.ShapeDtypeStruct((4 * rows, 4 *...]
    unnamed x6 -> x14, local copies, waits for them, and re-layouts: 0.02 us -> 1.7 us
    another operation x1 -> x0, other arithmetic: 0.93 us -> none  [per_device(): pair = jnp.stack([own, lax.ppermute(own, 'sect', swap)])]
  transfers between devices with their start and end apart: 3 -> 3, of which waited for: 2 -> 2; matrix products, arithmetic and copies ran while one was open for 0% -> 0% of each run, Pallas kernels for 20% -> 21%
where the time goes in v3:
time: 29.2 us; the launch traced here: 29 us
  Pallas kernels  14.2 us (49%)
  waiting for transfers between devices  7.88 us (27%)
  starting transfers between devices  5.09 us (17%)
  local copies, waits for them, and re-layouts  1.7 us (6%)
    pallas_call x1, Pallas kernels, per_device(): pl.pallas_call(late_kernel, out_shape=jax.ShapeDtypeStruct((4 * rows, 4 *...  8.08 us
    ppermute x1, waiting for transfers between devices, per_device(): far = lax.ppermute(edge, ('sect', 'tile'), apart)  6.68 us
    pallas_call x1, Pallas kernels, per_device(): pl.pallas_call(early_kernel, out_shape=[pltpu.VMEM((2, rows + 2, cols, c1...  6.13 us
    ppermute x1, starting transfers between devices, per_device(): far = lax.ppermute(edge, ('sect', 'tile'), apart)  4.53 us
    unnamed x14, local copies, waits for them, and re-layouts  1.7 us
    ppermute x1, waiting for transfers between devices, per_device(): other = lax.ppermute(own, 'sect', swap)  1.2 us
  transfers between devices with their start and end apart: 3, of which 2 were waited for; matrix products, arithmetic and copies ran while one was open for 0% of the time, Pallas kernels for 21%

profile of v3, /device:TPU:0, one launch (start us, length us, event | category | flops | bytes accessed | tf_op | source)
XLA Modules:
  0.0 29.0 jit_solution(783418454618219346)
XLA Ops:
  0.0 0.0 slice-start
  0.0 0.0 slice-start.1
  0.0 0.0 copy-start
  0.0 0.6 %collective-permute-start = (bf16[2,64,512]{2,1,0:T(8,128)(2,1)}, bf16[2,64,512]{2,1,0:T(8,128)(2,1)S(1)}, u32[]{:S(2)}, u32[]{:S(2)}) collective-permute-start(bf16[2,64,512]{2,1,0:T(8,128)(2,1)} %bitcast.4), channel_id=1, source_target_pairs={{0,8},{8,0},{1,9},{9,1},{2,10},{10,2},{3,11},{11,3},{4,12},{12,4},... | collective-permute-start | bytes 393224 | tf_op jit(solution)/shard_map/ppermute | solution.py:246
  0.6 1.2 %collective-permute-done.other = bf16[2,64,512]{2,1,0:T(8,128)(2,1)S(1)} collective-permute-done((bf16[2,64,512]{2,1,0:T(8,128)(2,1)}, bf16[2,64,512]{2,1,0:T(8,128)(2,1)S(1)}, u32[]{:S(2)}, u32[]{:S(2)}) %collective-permute-start) | collective-permute-done | bytes 131104 | tf_op jit(solution)/shard_map/ppermute | solution.py:246
  1.8 0.0 copy-start.1
  1.8 1.7 %copy-done.1 = bf16[1,2,64,512]{3,2,1,0:T(8,128)(2,1)S(1)} copy-done((bf16[1,2,64,512]{3,2,1,0:T(8,128)(2,1)S(1)}, bf16[1,2,64,512]{3,2,1,0:T(8,128)(2,1)}, u32[]{:S(2)}) %copy-start.1) | copy-done | bytes 131096
  3.5 0.0 copy-start.2
  3.5 0.0 copy-start.3
  3.5 0.0 copy-start.4
  3.5 4.5 %collective-permute-start.1 = (bf16[2,2,64,512]{3,2,1,0:T(8,128)(2,1)S(1)}, bf16[2,2,64,512]{3,2,1,0:T(8,128)(2,1)S(1)}, u32[]{:S(2)}, u32[]{:S(2)}) collective-permute-start(bf16[2,2,64,512]{3,2,1,0:T(8,128)(2,1)S(1)} %shard_map.73.pair), channel_id=1, source_target_pairs={{0,9},{1,10},{2,11},{3,12},{4,13},{5,14},{6,15},{9,0},{10,1},{11,2... | collective-permute-start | bytes 786440 | tf_op jit(solution)/shard_map/ppermute | solution.py:259
  8.0 6.7 %collective-permute-done.1.far = bf16[2,2,64,512]{3,2,1,0:T(8,128)(2,1)S(1)} collective-permute-done((bf16[2,2,64,512]{3,2,1,0:T(8,128)(2,1)S(1)}, bf16[2,2,64,512]{3,2,1,0:T(8,128)(2,1)S(1)}, u32[]{:S(2)}, u32[]{:S(2)}) %collective-permute-start.1) | collective-permute-done | bytes 262176 | tf_op jit(solution)/shard_map/ppermute | solution.py:259
  14.7 0.0 collective-permute-start.2
  14.7 0.0 slice-done
  14.7 0.0 slice-done.1
  14.7 0.0 copy-done
  14.7 6.1 %shard_map.74 = (f32[2,4,64,512]{3,2,1,0:T(8,128)S(1)}, bf16[3,1536,512]{2,1,0:T(8,128)(2,1)S(1)}, bf16[3,3,512,512]{3,2,1,0:T(8,128)(2,1)S(1)}, bf16[2,2,2,1024...) custom-call(bf16[2,2,64,512]{3,2,1,0:T(8,128)(2,1)S(1)} %shard_map.73.pair, bf16[3,3,3,512,512]{4,3,2,1,0:T(8,128)(2,1)} %w1.1, ...), custom_call_target="tpu_custom_call" | custom-call | flops 6000000000 | bytes 1024 | tf_op jit(solution)/shard_map/pallas_call | solution.py:261
  20.9 0.0 collective-permute-done.2.near
  20.9 0.0 copy-done.2
  20.9 0.0 copy-done.3
  20.9 0.0 copy-done.4
  20.9 8.1 %shard_map.75 = bf16[8,256,128]{2,1,0:T(8,128)(2,1)} custom-call(bf16[2,2,64,512]{3,2,1,0:T(8,128)(2,1)S(1)} %shard_map.73.pair, bf16[2,2,64,512]{3,2,1,0:T(8,128)(2,1)S(1)} %collective-permute-done.1.far, bf16[2,2,64,512]{3,2,1,0:T(8,128)(2,1)S(1)} %collective-permute-done.2.near, f32[2,4,64,512]{3,2,1,0:T(8,128)S(1)} %get-tuple-element.10.acc, ...), custom_call_target="tpu_custom_call" | custom-call | flops 8000000000 | bytes 1024 | tf_op jit(solution)/shard_map/pallas_call | solution.py:285
  (2 shorter events, 0.0 us)
Async XLA Ops:
  0.0 14.7 %slice-start = ((s8[7077888]{0:T(1024)(128)(4,1)}), s8[4194304]{0:T(1024)(128)(4,1)S(1)}, s32[]{:S(2)}) async-start(s8[7077888]{0:T(1024)(128)(4,1)} %bitcast.2), calls=%async_computation | async-start | bytes 8388608
  0.0 14.7 %slice-start.1 = ((s8[7077888]{0:T(1024)(128)(4,1)}), s8[2883584]{0:T(1024)(128)(4,1)S(1)}, s32[]{:S(2)}) async-start(s8[7077888]{0:T(1024)(128)(4,1)} %bitcast.2), calls=%async_computation.1 | async-start | bytes 5767168
  0.0 14.7 %copy-start = (bf16[3,3,3,256,128]{4,3,2,1,0:T(8,128)(2,1)S(1)}, bf16[3,3,3,256,128]{4,3,2,1,0:T(8,128)(2,1)}, u32[]{:S(2)}) copy-start(bf16[3,3,3,256,128]{4,3,2,1,0:T(8,128)(2,1)} %w3.1) | copy-start | bytes 5308420
  0.0 1.8 %collective-permute-start = (bf16[2,64,512]{2,1,0:T(8,128)(2,1)}, bf16[2,64,512]{2,1,0:T(8,128)(2,1)S(1)}, u32[]{:S(2)}, u32[]{:S(2)}) collective-permute-start(bf16[2,64,512]{2,1,0:T(8,128)(2,1)} %bitcast.4), channel_id=1, source_target_pairs={{0,8},{8,0},{1,9},{9,1},{2,10},{10,2},{3,11},{11,3},{4,12},{12,4},... | collective-permute-start | bytes 393224 | tf_op jit(solution)/shard_map/ppermute | solution.py:246
  1.8 1.7 %copy-start.1 = (bf16[1,2,64,512]{3,2,1,0:T(8,128)(2,1)S(1)}, bf16[1,2,64,512]{3,2,1,0:T(8,128)(2,1)}, u32[]{:S(2)}) copy-start(bf16[1,2,64,512]{3,2,1,0:T(8,128)(2,1)} %param.7) | copy-start | bytes 393220
  3.5 17.4 %copy-start.2 = (bf16[512]{0:T(512)(128)(2,1)S(1)}, bf16[512]{0:T(512)(128)(2,1)}, u32[]{:S(2)}) copy-start(bf16[512]{0:T(512)(128)(2,1)} %b1.1) | copy-start | bytes 3076
  3.5 17.4 %copy-start.3 = (bf16[256]{0:T(256)(128)(2,1)S(1)}, bf16[256]{0:T(256)(128)(2,1)}, u32[]{:S(2)}) copy-start(bf16[256]{0:T(256)(128)(2,1)} %b2.1) | copy-start | bytes 1540
  3.5 17.4 %copy-start.4 = (bf16[128]{0:T(256)(128)(2,1)S(1)}, bf16[128]{0:T(256)(128)(2,1)}, u32[]{:S(2)}) copy-start(bf16[128]{0:T(256)(128)(2,1)} %b3.1) | copy-start | bytes 772
  3.5 11.2 %collective-permute-start.1 = (bf16[2,2,64,512]{3,2,1,0:T(8,128)(2,1)S(1)}, bf16[2,2,64,512]{3,2,1,0:T(8,128)(2,1)S(1)}, u32[]{:S(2)}, u32[]{:S(2)}) collective-permute-start(bf16[2,2,64,512]{3,2,1,0:T(8,128)(2,1)S(1)} %shard_map.73.pair), channel_id=1, source_target_pairs={{0,9},{1,10},{2,11},{3,12},{4,13},{5,14},{6,15},{9,0},{10,1},{11,2... | collective-permute-start | bytes 786440 | tf_op jit(solution)/shard_map/ppermute | solution.py:259
  14.7 6.2 %collective-permute-start.2 = (bf16[2,2,64,512]{3,2,1,0:T(8,128)(2,1)S(1)}, bf16[2,2,64,512]{3,2,1,0:T(8,128)(2,1)S(1)}, u32[]{:S(2)}, u32[]{:S(2)}) collective-permute-start(bf16[2,2,64,512]{3,2,1,0:T(8,128)(2,1)S(1)} %collective-permute-done.1.far), channel_id=1, source_target_pairs={{0,8},{8,0},{1,9},{9,1},{2,10},{10,2},{3,11},{11,3},{4,12},{12,4},... | collective-permute-start | bytes 786440 | tf_op jit(solution)/shard_map/ppermute | solution.py:260

commit v4 on v3

--- a/solution.py
+++ b/solution.py
@@ -10,7 +10,8 @@
 
 
 def silu(v):
-    return v / (1.0 + jnp.exp(-v))
+    half = 0.5 * v
+    return half + half * jnp.tanh(half)
 
 
 def shifted(v):
@@ -83,9 +84,41 @@
     target[(*at, slice(None), slice(2 * chans, 3 * chans))] = after.astype(BF16)
 
 
-def pair_kernel(own, other, pair):
-    pair[0] = own[...]
+def load_kernel(own, pair, sem):
+    copy = pltpu.make_async_copy(own, pair.at[0], sem)
+    copy.start()
+    copy.wait()
+
+
+def pair_kernel(half, other, pair):
     pair[1] = other[...]
+
+
+def halo_part(source, at, upper, acc, v1, wn, cat):
+    cols, c1 = source.shape[2:]
+    rows = acc.shape[1] - 3
+    size = 2 * cols
+    for f in range(2):
+        for r in range(2):
+            put_cat(cat, (f, r), silu(source[at[f], r].astype(F32)))
+
+    def tap(k, _):
+        middle = k == 1
+        i = jnp.where(middle, 1, jnp.where(upper, 0, 2))
+        both = cat[...].reshape(2 * size, 3 * c1)
+        part = dot(both[:size], v1[i])
+        total = dot(both, wn[i].reshape(3 * c1, c1))
+        m = [
+            jnp.where(middle, jnp.where(upper, rows + 2, rows + 1), jnp.where(upper, 0, rows)),
+            jnp.where(middle, jnp.where(upper, 0, rows + 2), jnp.where(upper, 1, rows + 1)),
+        ]
+        for f in range(2):
+            value = (total[f * size : (f + 1) * size] + part).reshape(2, cols, c1)
+            for r in range(2):
+                acc[f, m[r]] += value[r]
+        return 0
+
+    lax.fori_loop(0, 2, tap, 0)
 
 
 def early_kernel(pair, w1, w2, w3, acc, v1, wn, v2, v3, cat, raw, sems):
@@ -123,8 +156,13 @@
     lax.fori_loop(0, 3, tap, 0)
 
 
+def middle_kernel(far, before, v1, wn, acc, cat):
+    second = lax.axis_index("sect") > 0
+    halo_part(far, (jnp.where(second, 0, 1), 1), second, acc, v1, wn, cat)
+
+
 def late_kernel(
-    pair, far, near, acc, v1, wn, b1, v2, b2, v3, b3, out, hcat, mcat, lcat, wide
+    pair, far, near, before, v1, wn, b1, v2, b2, v3, b3, out, acc, hcat, mcat, lcat, wide
 ):
     rows, cols, c1 = pair.shape[1:]
     c2 = b2.shape[0]
@@ -150,22 +188,7 @@
         return jnp.where(second, near[0, r].astype(F32), far[1, r].astype(F32))
 
     mrows = rows + 2
-    for f in range(2):
-        for r in range(4):
-            put_cat(hcat, (f, r), silu(feature(f, r if r < 2 else r + rows)))
-    size = 2 * cols
-
-    def tap(i, _):
-        lhs = jnp.concatenate([hcat[f, pl.ds(i, 2)].reshape(size, 3 * c1) for f in range(2)], axis=0)
-        part = dot(lhs[:size], v1[i])
-        total = dot(lhs, wn[i].reshape(3 * c1, c1))
-        for f in range(2):
-            value = (total[f * size : (f + 1) * size] + part).reshape(2, cols, c1)
-            acc[f, jnp.where(i < 2, 0, rows)] += value[0]
-            acc[f, jnp.where(i < 1, 1, rows + 1)] += value[1]
-        return 0
-
-    lax.fori_loop(0, 3, tap, 0)
+    halo_part(near, (jnp.where(second, 1, 0), 0), jnp.logical_not(second), acc, v1, wn, hcat)
     bias = b1[...].astype(F32)[None, :]
     for f in range(2):
         for m in range(mrows):
@@ -244,14 +267,25 @@
     anywhere = pl.BlockSpec(memory_space=pl.ANY)
 
     other = lax.ppermute(own, "sect", swap)
+    pair_shape = pltpu.VMEM((2, rows, cols, c1), BF16)
+    half = pl.pallas_call(
+        load_kernel,
+        out_shape=pair_shape,
+        in_specs=[anywhere],
+        out_specs=vmem,
+        scratch_shapes=[pltpu.SemaphoreType.DMA],
+        cost_estimate=pl.CostEstimate(flops=6_000_000_000, bytes_accessed=1024, transcendentals=0),
+        compiler_params=pltpu.CompilerParams(vmem_limit_bytes=1 << 20),
+    )(pltpu.with_memory_space_constraint(own, pltpu.HBM))
     pair = pl.pallas_call(
         pair_kernel,
-        out_shape=pltpu.VMEM((2, rows, cols, c1), BF16),
+        out_shape=pair_shape,
         in_specs=[vmem] * 2,
         out_specs=vmem,
-        cost_estimate=pl.CostEstimate(flops=12_000_000_000, bytes_accessed=1024, transcendentals=0),
+        input_output_aliases={0: 0},
+        cost_estimate=pl.CostEstimate(flops=6_000_000_000, bytes_accessed=1024, transcendentals=0),
         compiler_params=pltpu.CompilerParams(vmem_limit_bytes=1 << 20),
-    )(in_vmem(own), in_vmem(other))
+    )(in_vmem(half), in_vmem(other))
     if rows == 2:
         edge = pair
     else:
@@ -261,7 +295,7 @@
     acc, v1, wn, v2, v3 = pl.pallas_call(
         early_kernel,
         out_shape=[
-            pltpu.VMEM((2, rows + 2, cols, c1), F32),
+            pltpu.VMEM((2, rows + 3, cols, c1), F32),
             pltpu.VMEM((3, 3 * c1, c1), BF16),
             pltpu.VMEM((3, 3, c1, c1), BF16),
             pltpu.VMEM((2, 2, 2, 2 * c1, 2 * c2), BF16),
@@ -282,13 +316,25 @@
         in_vmem(conv_second),
         in_vmem(conv_third),
     )
-    out = pl.pallas_call(
+    acc_shape = pltpu.VMEM((2, rows + 3, cols, c1), F32)
+    acc = pl.pallas_call(
+        middle_kernel,
+        out_shape=acc_shape,
+        in_specs=[vmem] * 4,
+        out_specs=vmem,
+        input_output_aliases={1: 0},
+        scratch_shapes=[pltpu.VMEM((2, 2, cols, 3 * c1), BF16)],
+        cost_estimate=pl.CostEstimate(flops=2_000_000_000, bytes_accessed=1024, transcendentals=0),
+        compiler_params=pltpu.CompilerParams(vmem_limit_bytes=8 << 20),
+    )(in_vmem(far), in_vmem(acc), in_vmem(v1), in_vmem(wn))
+    out, _ = pl.pallas_call(
         late_kernel,
-        out_shape=jax.ShapeDtypeStruct((4 * rows, 4 * cols, c3), BF16),
+        out_shape=[jax.ShapeDtypeStruct((4 * rows, 4 * cols, c3), BF16), acc_shape],
         in_specs=[vmem] * 11,
-        out_specs=vmem,
+        out_specs=[vmem] * 2,
+        input_output_aliases={3: 1},
         scratch_shapes=[
-            pltpu.VMEM((2, 4, cols, 3 * c1), BF16),
+            pltpu.VMEM((2, 2, cols, 3 * c1), BF16),
             pltpu.VMEM((2, rows + 2, cols, 3 * c1), BF16),
             pltpu.VMEM((2, 2 * rows + 2, cols, 4 * c2), BF16),
             pltpu.VMEM((4 * rows, 4 * cols, c3), F32),

time: 29.2 us -> 28.3 us (0.969)
  Pallas kernels: 14.2 us -> 15.9 us
  local copies, waits for them, and re-layouts: 1.7 us -> 0.04 us
  waiting for transfers between devices: 7.88 us -> 6.78 us
    pallas_call x3 -> x5, Pallas kernels: 14.2 us -> 15.9 us  [the longest x1 6.96 us: per_device(): pl.pallas_call(late_kernel, out_shape=[jax.ShapeDtypeStruct((4 * rows, 4...]
    unnamed x14 -> x12, local copies, waits for them, and re-layouts: 1.7 us -> 0.04 us
    ppermute x1, waiting for transfers between devices: 1.2 us -> 0.1 us  [per_device(): other = lax.ppermute(own, 'sect', swap)]
  transfers between devices with their start and end apart: 3 -> 3, of which waited for: 2 -> 2; matrix products, arithmetic and copies ran while one was open for 0% -> 0% of each run, Pallas kernels for 21% -> 32%
where the time goes in v4:
time: 28.3 us; the launch traced here: 28.1 us
  Pallas kernels  15.9 us (56%)
  waiting for transfers between devices  6.78 us (24%)
  starting transfers between devices  5.28 us (19%)
    pallas_call x1, Pallas kernels, per_device(): pl.pallas_call(late_kernel, out_shape=[jax.ShapeDtypeStruct((4 * rows, 4...  6.96 us
    ppermute x1, waiting for transfers between devices, per_device(): far = lax.ppermute(edge, ('sect', 'tile'), apart)  6.68 us
    pallas_call x1, Pallas kernels, per_device(): pl.pallas_call(early_kernel, out_shape=[pltpu.VMEM((2, rows + 3, cols, c1...  6.13 us
    ppermute x1, starting transfers between devices, per_device(): far = lax.ppermute(edge, ('sect', 'tile'), apart)  4.79 us
    pallas_call x1, Pallas kernels, per_device(): pl.pallas_call(middle_kernel, out_shape=acc_shape, in_specs=[vmem] * 4, o...  1.76 us
    pallas_call x1, Pallas kernels, per_device(): pl.pallas_call(load_kernel, out_shape=pair_shape, in_specs=[anywhere], ou...  1.06 us
  transfers between devices with their start and end apart: 3, of which 2 were waited for; matrix products, arithmetic and copies ran while one was open for 0% of the time, Pallas kernels for 32%

profile of v4, /device:TPU:0, one launch (start us, length us, event | category | flops | bytes accessed | tf_op | source)
XLA Modules:
  0.0 28.1 jit_solution(6175813593937670511)
XLA Ops:
  0.0 0.5 %collective-permute-start = (bf16[2,64,512]{2,1,0:T(8,128)(2,1)}, bf16[2,64,512]{2,1,0:T(8,128)(2,1)S(1)}, u32[]{:S(2)}, u32[]{:S(2)}) collective-permute-start(bf16[2,64,512]{2,1,0:T(8,128)(2,1)} %bitcast.4), channel_id=1, source_target_pairs={{0,8},{8,0},{1,9},{9,1},{2,10},{10,2},{3,11},{11,3},{4,12},{12,4},... | collective-permute-start | bytes 393224 | tf_op jit(solution)/shard_map/ppermute | solution.py:269
  0.5 0.0 slice-start
  0.5 1.1 %shard_map.73.half = bf16[2,2,64,512]{3,2,1,0:T(8,128)(2,1)S(1)} custom-call(bf16[2,64,512]{2,1,0:T(8,128)(2,1)} %bitcast.5), custom_call_target="tpu_custom_call" | custom-call | flops 6000000000 | bytes 1024 | tf_op jit(solution)/shard_map/pallas_call | solution.py:271
  1.6 0.0 slice-start.1
  1.6 0.0 copy-start
  1.6 0.1 collective-permute-done.other
  1.7 4.8 %collective-permute-start.1 = (bf16[2,2,64,512]{3,2,1,0:T(8,128)(2,1)S(1)}, bf16[2,2,64,512]{3,2,1,0:T(8,128)(2,1)S(1)}, u32[]{:S(2)}, u32[]{:S(2)}) collective-permute-start(bf16[2,2,64,512]{3,2,1,0:T(8,128)(2,1)S(1)} %shard_map.74.pair), channel_id=1, source_target_pairs={{0,9},{1,10},{2,11},{3,12},{4,13},{5,14},{6,15},{9,0},{10,1},{11,2... | collective-permute-start | bytes 786440 | tf_op jit(solution)/shard_map/ppermute | solution.py:293
  6.5 6.7 %collective-permute-done.1.far = bf16[2,2,64,512]{3,2,1,0:T(8,128)(2,1)S(1)} collective-permute-done((bf16[2,2,64,512]{3,2,1,0:T(8,128)(2,1)S(1)}, bf16[2,2,64,512]{3,2,1,0:T(8,128)(2,1)S(1)}, u32[]{:S(2)}, u32[]{:S(2)}) %collective-permute-start.1) | collective-permute-done | bytes 262176 | tf_op jit(solution)/shard_map/ppermute | solution.py:293
  13.2 0.0 collective-permute-start.2
  13.2 0.0 slice-done
  13.2 0.0 slice-done.1
  13.2 0.0 copy-done
  13.2 6.1 %shard_map.75 = (f32[2,5,64,512]{3,2,1,0:T(8,128)S(1)}, bf16[3,1536,512]{2,1,0:T(8,128)(2,1)S(1)}, bf16[3,3,512,512]{3,2,1,0:T(8,128)(2,1)S(1)}, bf16[2,2,2,1024...) custom-call(bf16[2,2,64,512]{3,2,1,0:T(8,128)(2,1)S(1)} %shard_map.74.pair, bf16[3,3,3,512,512]{4,3,2,1,0:T(8,128)(2,1)} %w1.1, ...), custom_call_target="tpu_custom_call" | custom-call | flops 6000000000 | bytes 1024 | tf_op jit(solution)/shard_map/pallas_call | solution.py:295
  19.3 0.0 copy-start.1
  19.3 0.0 copy-start.2
  19.4 0.0 copy-start.3
  19.4 1.8 %shard_map.76.before = f32[2,5,64,512]{3,2,1,0:T(8,128)S(1)} custom-call(bf16[2,2,64,512]{3,2,1,0:T(8,128)(2,1)S(1)} %collective-permute-done.1.far, f32[2,5,64,512]{3,2,1,0:T(8,128)S(1)} %get-tuple-element.11.before, bf16[3,1536,512]{2,1,0:T(8,128)(2,1)S(1)} %get-tuple-element.12.v1, ...), custom_call_target="tpu_custom_call", output_to_operand_aliasing={{}: (1, {})} | custom-call | flops 2000000000 | bytes 1024 | tf_op jit(solution)/shard_map/pallas_call | solution.py:320
  21.1 0.0 collective-permute-done.2.near
  21.2 0.0 copy-done.1
  21.2 0.0 copy-done.2
  21.2 0.0 copy-done.3
  21.2 7.0 %shard_map.77 = (bf16[8,256,128]{2,1,0:T(8,128)(2,1)}, f32[2,5,64,512]{3,2,1,0:T(8,128)S(1)}) custom-call(bf16[2,2,64,512]{3,2,1,0:T(8,128)(2,1)S(1)} %shard_map.74.pair, bf16[2,2,64,512]{3,2,1,0:T(8,128)(2,1)S(1)} %collective-permute-done.1.far, bf16[2,2,64,512]{3,2,1,0:T(8,128)(2,1)S(1)} %collective-permute-done.2.near, ...), custom_call_target="tpu_custom_call", output_to_operand_aliasing={{1}: (3, {})} | custom-call | flops 8000000000 | bytes 1024 | tf_op jit(solution)/shard_map/pallas_call | solution.py:330
  (2 shorter events, 0.0 us)
Async XLA Ops:
  0.0 1.7 %collective-permute-start = (bf16[2,64,512]{2,1,0:T(8,128)(2,1)}, bf16[2,64,512]{2,1,0:T(8,128)(2,1)S(1)}, u32[]{:S(2)}, u32[]{:S(2)}) collective-permute-start(bf16[2,64,512]{2,1,0:T(8,128)(2,1)} %bitcast.4), channel_id=1, source_target_pairs={{0,8},{8,0},{1,9},{9,1},{2,10},{10,2},{3,11},{11,3},{4,12},{12,4},... | collective-permute-start | bytes 393224 | tf_op jit(solution)/shard_map/ppermute | solution.py:269
  0.5 12.7 %slice-start = ((s8[7077888]{0:T(1024)(128)(4,1)}), s8[4194304]{0:T(1024)(128)(4,1)S(1)}, s32[]{:S(2)}) async-start(s8[7077888]{0:T(1024)(128)(4,1)} %bitcast.2), calls=%async_computation | async-start | bytes 8388608
  1.6 11.6 %slice-start.1 = ((s8[7077888]{0:T(1024)(128)(4,1)}), s8[2883584]{0:T(1024)(128)(4,1)S(1)}, s32[]{:S(2)}) async-start(s8[7077888]{0:T(1024)(128)(4,1)} %bitcast.2), calls=%async_computation.1 | async-start | bytes 5767168
  1.6 11.6 %copy-start = (bf16[3,3,3,256,128]{4,3,2,1,0:T(8,128)(2,1)S(1)}, bf16[3,3,3,256,128]{4,3,2,1,0:T(8,128)(2,1)}, u32[]{:S(2)}) copy-start(bf16[3,3,3,256,128]{4,3,2,1,0:T(8,128)(2,1)} %w3.1) | copy-start | bytes 5308420
  1.7 11.5 %collective-permute-start.1 = (bf16[2,2,64,512]{3,2,1,0:T(8,128)(2,1)S(1)}, bf16[2,2,64,512]{3,2,1,0:T(8,128)(2,1)S(1)}, u32[]{:S(2)}, u32[]{:S(2)}) collective-permute-start(bf16[2,2,64,512]{3,2,1,0:T(8,128)(2,1)S(1)} %shard_map.74.pair), channel_id=1, source_target_pairs={{0,9},{1,10},{2,11},{3,12},{4,13},{5,14},{6,15},{9,0},{10,1},{11,2... | collective-permute-start | bytes 786440 | tf_op jit(solution)/shard_map/ppermute | solution.py:293
  13.2 8.0 %collective-permute-start.2 = (bf16[2,2,64,512]{3,2,1,0:T(8,128)(2,1)S(1)}, bf16[2,2,64,512]{3,2,1,0:T(8,128)(2,1)S(1)}, u32[]{:S(2)}, u32[]{:S(2)}) collective-permute-start(bf16[2,2,64,512]{3,2,1,0:T(8,128)(2,1)S(1)} %collective-permute-done.1.far), channel_id=1, source_target_pairs={{0,8},{8,0},{1,9},{9,1},{2,10},{10,2},{3,11},{11,3},{4,12},{12,4},... | collective-permute-start | bytes 786440 | tf_op jit(solution)/shard_map/ppermute | solution.py:294
  19.3 1.8 %copy-start.1 = (bf16[512]{0:T(512)(128)(2,1)S(1)}, bf16[512]{0:T(512)(128)(2,1)}, u32[]{:S(2)}) copy-start(bf16[512]{0:T(512)(128)(2,1)} %b1.1) | copy-start | bytes 3076
  19.3 1.8 %copy-start.2 = (bf16[256]{0:T(256)(128)(2,1)S(1)}, bf16[256]{0:T(256)(128)(2,1)}, u32[]{:S(2)}) copy-start(bf16[256]{0:T(256)(128)(2,1)} %b2.1) | copy-start | bytes 1540
  19.4 1.8 %copy-start.3 = (bf16[128]{0:T(256)(128)(2,1)S(1)}, bf16[128]{0:T(256)(128)(2,1)}, u32[]{:S(2)}) copy-start(bf16[128]{0:T(256)(128)(2,1)} %b3.1) | copy-start | bytes 772

commit v5 on v4

--- a/solution.py
+++ b/solution.py
@@ -22,6 +22,17 @@
     return before, after
 
 
+def column_before(v):
+    column = lax.broadcasted_iota(jnp.int32, v.shape, 0)
+    return jnp.where(column == 0, 0.0, pltpu.roll(v, 1, 0))
+
+
+def column_after(v, last):
+    count = v.shape[0]
+    column = lax.broadcasted_iota(jnp.int32, v.shape, 0)
+    return jnp.where(column == count - 1, last, pltpu.roll(v, count - 1, 0))
+
+
 def dot(a, b):
     return jnp.dot(a, b, preferred_element_type=F32)
 
@@ -40,37 +51,46 @@
     lax.fori_loop(0, cin // step, body, 0)
 
 
-def merge_space(source, target, step):
+ORDER = (0, 2, 1)
+
+
+def merge_second(source, target):
+    cin = source.shape[3]
+    step = 64
+
+    def body(n, _):
+        at = pl.multiple_of(n * step, step)
+        for i in range(3):
+            for place, j in enumerate(ORDER):
+                rows = pl.ds(place * cin + at, step)
+                target[0, i, rows, :] = source[0, i, j, pl.ds(at, step), :] + source[1, i, j, pl.ds(at, step), :]
+                target[1, i, rows, :] = source[2, i, j, pl.ds(at, step), :]
+        return 0
+
+    lax.fori_loop(0, cin // step, body, 0)
+
+
+def merge_third(source, target):
     cin, cout = source.shape[3], source.shape[4]
+    step = 32
 
     def body(n, _):
         at = pl.multiple_of(n * step, step)
         for t in range(2):
-            tap = {}
-            for i in range(3):
-                for j in range(3):
-                    if t == 0:
-                        tap[i, j] = source[0, i, j, pl.ds(at, step), :].astype(F32) + source[
-                            1, i, j, pl.ds(at, step), :
-                        ].astype(F32)
-                    else:
-                        tap[i, j] = source[2, i, j, pl.ds(at, step), :].astype(F32)
-            for a in range(2):
-                for i in range(2):
-                    if a == i:
-                        lo = i
-                        row = [tap[lo, j] + tap[lo + 1, j] for j in range(3)]
-                    else:
-                        row = [tap[2 * i, j] for j in range(3)]
-                    for b in range(2):
-                        if b == 0:
-                            columns = (row[0] + row[1], row[2])
-                        else:
-                            columns = (row[0], row[1] + row[2])
-                        for j in range(2):
-                            target[t, b, i, pl.ds(j * cin + at, step), pl.ds(a * cout, cout)] = columns[
-                                j
-                            ].astype(BF16)
+            for place, j in enumerate(ORDER):
+                if t == 0:
+                    tap = [
+                        source[0, i, j, pl.ds(at, step), :].astype(F32)
+                        + source[1, i, j, pl.ds(at, step), :].astype(F32)
+                        for i in range(3)
+                    ]
+                else:
+                    tap = [source[2, i, j, pl.ds(at, step), :].astype(F32) for i in range(3)]
+                rows = pl.ds(place * cin + at, step)
+                target[t, 0, rows, 0:cout] = (tap[0] + tap[1]).astype(BF16)
+                target[t, 0, rows, cout : 2 * cout] = tap[0].astype(BF16)
+                target[t, 1, rows, 0:cout] = tap[2].astype(BF16)
+                target[t, 1, rows, cout : 2 * cout] = (tap[1] + tap[2]).astype(BF16)
         return 0
 
     lax.fori_loop(0, cin // step, body, 0)
@@ -136,8 +156,8 @@
         mine, other = pair[0, r].astype(F32), pair[1, r].astype(F32)
         put_cat(cat, (0, r), silu(jnp.where(second, other, mine)))
         put_cat(cat, (1, r), silu(mine))
-    merge_space(w3, v3, 16)
-    merge_space(w2, v2, 16)
+    merge_third(w3, v3)
+    merge_second(w2, v2)
     size = rows * cols
     acc[...] = jnp.zeros(acc.shape, F32)
 
@@ -162,7 +182,7 @@
 
 
 def late_kernel(
-    pair, far, near, before, v1, wn, b1, v2, b2, v3, b3, out, acc, hcat, mcat, lcat, wide
+    pair, far, near, before, v1, wn, b1, v2, b2, v3, b3, out, acc, hcat, mcat, medge, lcat, ledge, wide, so, si, uo, ui, po, pi
 ):
     rows, cols, c1 = pair.shape[1:]
     c2 = b2.shape[0]
@@ -190,6 +210,7 @@
     mrows = rows + 2
     halo_part(near, (jnp.where(second, 1, 0), 0), jnp.logical_not(second), acc, v1, wn, hcat)
     bias = b1[...].astype(F32)[None, :]
+    medge[...] = jnp.zeros(medge.shape, F32)
     for f in range(2):
         for m in range(mrows):
             v = acc[f, m] + bias + feature(f, m + 1)
@@ -198,55 +219,107 @@
                 v = jnp.where(first_tile, 0.0, v)
             if m == mrows - 1:
                 v = jnp.where(last_tile, 0.0, v)
-            put_cat(mcat, (f, m), v)
+            mcat[f, m, :, 0:c1] = column_before(v).astype(BF16)
+            mcat[f, m, :, c1 : 2 * c1] = v.astype(BF16)
+            medge[f, m : m + 1, 0:c1] = v[cols - 1 : cols]
 
     wins = mrows - 1
+    size = wins * cols
+
+    def products(t, i, first, count, frames):
+        pieces, singles = [], []
+        for f in range(frames):
+            pieces.append(mcat[f, pl.ds(first, count)].reshape(count * cols, 2 * c1))
+            pieces.append(medge[f].astype(BF16))
+            singles.append(mcat[f, pl.ds(first, count), :, c1 : 2 * c1].reshape(count * cols, c1))
+        outer = dot(jnp.concatenate(pieces, axis=0), v2[t, i, 0 : 2 * c1])
+        inner = dot(jnp.concatenate(singles, axis=0), v2[t, i, 2 * c1 : 3 * c1])
+        return outer, inner
+
+    def around(k, _):
+        so[k, 0, 0 : size + 16], si[k, 0, 0:size] = products(0, 2 * k, k, wins, 1)
+        so[k, 1], si[k, 1] = products(1, 2 * k, k, wins, 2)
+        return 0
+
+    lax.fori_loop(0, 2, around, 0)
+
+    def centre(k, _):
+        uo[0, 0 : size + cols + 16], ui[0, 0 : size + cols] = products(0, 1, k, mrows, 1)
+        uo[1], ui[1] = products(1, 1, k, mrows, 2)
+        return 0
+
+    lax.fori_loop(0, 1, centre, 0)
     bias = b2[...].astype(F32)[None, :]
-    for b in range(2):
-        lanes = slice(c1, 3 * c1) if b == 0 else slice(0, 2 * c1)
-        early = jnp.zeros((wins * cols, 2 * c2), F32)
-        now = [early, early]
-        for i in range(2):
-            lhs = [mcat[f, i : i + wins, :, lanes].reshape(wins * cols, 2 * c1) for f in range(2)]
-            early = early + dot(lhs[0], v2[0, b, i])
-            for f in range(2):
-                now[f] = now[f] + dot(lhs[f], v2[1, b, i])
+    ledge[...] = jnp.zeros(ledge.shape, F32)
+    for f in range(2):
+        for w in range(wins):
+
+            def around_at(ref, at, count, stride):
+                total = 0.0
+                for k in range(2):
+                    row = at + (k if count == 1 else 0)
+                    total = total + ref[k, 0, row : row + count] + ref[k, 1, f * stride + row : f * stride + row + count]
+                return total
+
+            def centre_at(ref, at, count, stride):
+                return ref[0, at : at + count] + ref[1, f * stride + at : f * stride + at + count]
+
+            outer = around_at(so, w * cols, cols, size + 16)
+            inner = around_at(si, w * cols, cols, size)
+            edge = around_at(so, size + w, 1, size + 16)
+            full = mrows * cols
+            for a in range(2):
+                up = outer + centre_at(uo, (w + a) * cols, cols, full + 16)
+                mid = inner + centre_at(ui, (w + a) * cols, cols, full) + bias
+                last = edge + centre_at(uo, full + w + a, 1, full + 16)
+                even = silu(up + mid)
+                odd = silu(column_after(up, last) + mid)
+                if w == 0 and a == 0:
+                    even, odd = jnp.where(first_tile, 0.0, even), jnp.where(first_tile, 0.0, odd)
+                if w == wins - 1 and a == 1:
+                    even, odd = jnp.where(last_tile, 0.0, even), jnp.where(last_tile, 0.0, odd)
+                r = 2 * w + a
+                lcat[f, r, :, 0:c2] = column_before(odd).astype(BF16)
+                lcat[f, r, :, c2 : 2 * c2] = even.astype(BF16)
+                lcat[f, r, :, 2 * c2 : 3 * c2] = odd.astype(BF16)
+                ledge[f, r : r + 1, 0:c2] = odd[cols - 1 : cols]
+
+    wins = 2 * wins - 1
+    size = wins * cols
+    bias = b3[...].astype(F32)[None, :]
+
+    def pairs_of(k, _):
         for f in range(2):
-            total = early + now[f]
-            for w in range(wins):
-                for a in range(2):
-                    v = total[w * cols : (w + 1) * cols, a * c2 : (a + 1) * c2] + bias
-                    v = silu(v)
-                    if w == 0 and a == 0:
-                        v = jnp.where(first_tile, 0.0, v)
-                    if w == wins - 1 and a == 1:
-                        v = jnp.where(last_tile, 0.0, v)
-                    before, after = shifted(v)
-                    r = 2 * w + a
-                    if b == 0:
-                        lcat[f, r, :, 0:c2] = before.astype(BF16)
-                        lcat[f, r, :, 2 * c2 : 3 * c2] = v.astype(BF16)
-                    else:
-                        lcat[f, r, :, c2 : 2 * c2] = v.astype(BF16)
-                        lcat[f, r, :, 3 * c2 : 4 * c2] = after.astype(BF16)
-
-    lrows = 2 * wins
-    wins = lrows - 1
-    bias = b3[...].astype(F32)[None, :]
-    for q in range(4):
-        b = 1 if q % 2 == 0 else 0
-        at = (0, c2, c2, 2 * c2)[q]
-        total = jnp.zeros((wins * cols, 2 * c3), F32)
-        for i in range(2):
-            for f in range(2):
-                lhs = lcat[f, i : i + wins, :, at : at + 2 * c2].reshape(wins * cols, 2 * c2)
-                total = total + dot(lhs, v3[f, b, i])
-        for o in range(4 * rows):
-            a = 1 - o % 2
-            w = (o + 1) // 2
-            v = total[w * cols : (w + 1) * cols, a * c3 : (a + 1) * c3] + bias
+            rows_of = lcat[f, pl.ds(k, wins)].reshape(size, 3 * c2)
+            pairs = jnp.concatenate(
+                [rows_of[:, 0 : 2 * c2], rows_of[:, c2 : 3 * c2], ledge[f].astype(BF16)], axis=0
+            )
+            po[f, k] = dot(pairs, v3[f, k, 0 : 2 * c2])
+            single = jnp.concatenate([rows_of[:, c2 : 2 * c2], rows_of[:, 2 * c2 : 3 * c2]], axis=0)
+            pi[f, k] = dot(single, v3[f, k, 2 * c2 : 3 * c2])
+        return 0
+
+    lax.fori_loop(0, 2, pairs_of, 0)
+    for o in range(4 * rows):
+        a = 1 - o % 2
+        w = (o + 1) // 2
+        lanes = slice(a * c3, (a + 1) * c3)
+
+        def cell(ref, at):
+            here = slice(at * cols, (at + 1) * cols)
+            return ref[0, 0, here, lanes] + ref[0, 1, here, lanes] + ref[1, 0, here, lanes] + ref[1, 1, here, lanes]
+
+        apart = cell(po, w)
+        close = cell(po, wins + w)
+        last = 0.0
+        for f in range(2):
+            for k in range(2):
+                row = 2 * size + w + k
+                last = last + po[f, k, row : row + 1, lanes]
+        even = cell(pi, w) + bias
+        odd = cell(pi, wins + w) + bias
+        for q, v in enumerate((apart + even, close + even, close + odd, column_after(apart, last) + odd)):
             wide[o, pl.ds(q, cols, stride=4), :] = v
-    for o in range(4 * rows):
         out[o] = wide[o].astype(BF16)
 
 
@@ -298,8 +371,8 @@
             pltpu.VMEM((2, rows + 3, cols, c1), F32),
             pltpu.VMEM((3, 3 * c1, c1), BF16),
             pltpu.VMEM((3, 3, c1, c1), BF16),
-            pltpu.VMEM((2, 2, 2, 2 * c1, 2 * c2), BF16),
-            pltpu.VMEM((2, 2, 2, 2 * c2, 2 * c3), BF16),
+            pltpu.VMEM((2, 3, 3 * c1, c2), BF16),
+            pltpu.VMEM((2, 2, 3 * c2, 2 * c3), BF16),
         ],
         in_specs=[vmem, anywhere, vmem, vmem],
         out_specs=[vmem] * 5,
@@ -335,12 +408,20 @@
         input_output_aliases={3: 1},
         scratch_shapes=[
             pltpu.VMEM((2, 2, cols, 3 * c1), BF16),
-            pltpu.VMEM((2, rows + 2, cols, 3 * c1), BF16),
-            pltpu.VMEM((2, 2 * rows + 2, cols, 4 * c2), BF16),
+            pltpu.VMEM((2, rows + 2, cols, 2 * c1), BF16),
+            pltpu.VMEM((2, -(-(rows + 2) // 16) * 16, 2 * c1), F32),
+            pltpu.VMEM((2, 2 * rows + 2, cols, 3 * c2), BF16),
+            pltpu.VMEM((2, -(-(2 * rows + 2) // 16) * 16, 2 * c2), F32),
             pltpu.VMEM((4 * rows, 4 * cols, c3), F32),
+            pltpu.VMEM((2, 2, 2 * ((rows + 1) * cols + 16), c2), F32),
+            pltpu.VMEM((2, 2, 2 * (rows + 1) * cols, c2), F32),
+            pltpu.VMEM((2, 2 * ((rows + 2) * cols + 16), c2), F32),
+            pltpu.VMEM((2, 2 * (rows + 2) * cols, c2), F32),
+            pltpu.VMEM((2, 2, 2 * (2 * rows + 1) * cols + 16, 2 * c3), F32),
+            pltpu.VMEM((2, 2, 2 * (2 * rows + 1) * cols, 2 * c3), F32),
         ],
         cost_estimate=pl.CostEstimate(flops=8_000_000_000, bytes_accessed=1024, transcendentals=0),
-        compiler_params=pltpu.CompilerParams(vmem_limit_bytes=14 << 20),
+        compiler_params=pltpu.CompilerParams(vmem_limit_bytes=24 << 20),
     )(
         in_vmem(pair),
         in_vmem(far),

time: 28.3 us -> 28.9 us (1.021)
  Pallas kernels: 15.9 us -> 16.5 us
    pallas_call x1, Pallas kernels: 6.96 us -> 7.48 us  [per_device(): pl.pallas_call(late_kernel, out_shape=[jax.ShapeDtypeStruct((4 * rows, 4...]
  transfers between devices with their start and end apart: 3 -> 3, of which waited for: 2 -> 2; matrix products, arithmetic and copies ran while one was open for 0% -> 0% of each run, Pallas kernels for 32% -> 31%
where the time goes in v5:
time: 28.9 us; the launch traced here: 28.7 us
  Pallas kernels  16.5 us (57%)
  waiting for transfers between devices  6.78 us (23%)
  starting transfers between devices  5.28 us (18%)
    pallas_call x1, Pallas kernels, per_device(): pl.pallas_call(late_kernel, out_shape=[jax.ShapeDtypeStruct((4 * rows, 4...  7.48 us
    ppermute x1, waiting for transfers between devices, per_device(): far = lax.ppermute(edge, ('sect', 'tile'), apart)  6.68 us
    pallas_call x1, Pallas kernels, per_device(): pl.pallas_call(early_kernel, out_shape=[pltpu.VMEM((2, rows + 3, cols, c1...  6.14 us
    ppermute x1, starting transfers between devices, per_device(): far = lax.ppermute(edge, ('sect', 'tile'), apart)  4.79 us
    pallas_call x1, Pallas kernels, per_device(): pl.pallas_call(middle_kernel, out_shape=acc_shape, in_specs=[vmem] * 4, o...  1.78 us
    pallas_call x1, Pallas kernels, per_device(): pl.pallas_call(load_kernel, out_shape=pair_shape, in_specs=[anywhere], ou...  1.06 us
  transfers between devices with their start and end apart: 3, of which 2 were waited for; matrix products, arithmetic and copies ran while one was open for 0% of the time, Pallas kernels for 31%

profile of v5, /device:TPU:0, one launch (start us, length us, event | category | flops | bytes accessed | tf_op | source)
XLA Modules:
  0.0 28.7 jit_solution(3416005262209798306)
XLA Ops:
  0.0 0.5 %collective-permute-start = (bf16[2,64,512]{2,1,0:T(8,128)(2,1)}, bf16[2,64,512]{2,1,0:T(8,128)(2,1)S(1)}, u32[]{:S(2)}, u32[]{:S(2)}) collective-permute-start(bf16[2,64,512]{2,1,0:T(8,128)(2,1)} %bitcast.4), channel_id=1, source_target_pairs={{0,8},{8,0},{1,9},{9,1},{2,10},{10,2},{3,11},{11,3},{4,12},{12,4},... | collective-permute-start | bytes 393224 | tf_op jit(solution)/shard_map/ppermute | solution.py:342
  0.5 0.0 slice-start
  0.5 1.1 %shard_map.73.half = bf16[2,2,64,512]{3,2,1,0:T(8,128)(2,1)S(1)} custom-call(bf16[2,64,512]{2,1,0:T(8,128)(2,1)} %bitcast.5), custom_call_target="tpu_custom_call" | custom-call | flops 6000000000 | bytes 1024 | tf_op jit(solution)/shard_map/pallas_call | solution.py:344
  1.6 0.0 slice-start.1
  1.6 0.0 copy-start
  1.6 0.1 collective-permute-done.other
  1.7 4.8 %collective-permute-start.1 = (bf16[2,2,64,512]{3,2,1,0:T(8,128)(2,1)S(1)}, bf16[2,2,64,512]{3,2,1,0:T(8,128)(2,1)S(1)}, u32[]{:S(2)}, u32[]{:S(2)}) collective-permute-start(bf16[2,2,64,512]{3,2,1,0:T(8,128)(2,1)S(1)} %shard_map.74.pair), channel_id=1, source_target_pairs={{0,9},{1,10},{2,11},{3,12},{4,13},{5,14},{6,15},{9,0},{10,1},{11,2... | collective-permute-start | bytes 786440 | tf_op jit(solution)/shard_map/ppermute | solution.py:366
  6.5 6.7 %collective-permute-done.1.far = bf16[2,2,64,512]{3,2,1,0:T(8,128)(2,1)S(1)} collective-permute-done((bf16[2,2,64,512]{3,2,1,0:T(8,128)(2,1)S(1)}, bf16[2,2,64,512]{3,2,1,0:T(8,128)(2,1)S(1)}, u32[]{:S(2)}, u32[]{:S(2)}) %collective-permute-start.1) | collective-permute-done | bytes 262176 | tf_op jit(solution)/shard_map/ppermute | solution.py:366
  13.2 0.0 collective-permute-start.2
  13.2 0.0 slice-done
  13.2 0.0 slice-done.1
  13.2 0.0 copy-done
  13.2 6.1 %shard_map.75 = (f32[2,5,64,512]{3,2,1,0:T(8,128)S(1)}, bf16[3,1536,512]{2,1,0:T(8,128)(2,1)S(1)}, bf16[3,3,512,512]{3,2,1,0:T(8,128)(2,1)S(1)}, bf16[2,3,1536,2...) custom-call(bf16[2,2,64,512]{3,2,1,0:T(8,128)(2,1)S(1)} %shard_map.74.pair, bf16[3,3,3,512,512]{4,3,2,1,0:T(8,128)(2,1)} %w1.1, ...), custom_call_target="tpu_custom_call" | custom-call | flops 6000000000 | bytes 1024 | tf_op jit(solution)/shard_map/pallas_call | solution.py:368
  19.3 0.0 copy-start.1
  19.4 0.0 copy-start.2
  19.4 0.0 copy-start.3
  19.4 1.8 %shard_map.76.before = f32[2,5,64,512]{3,2,1,0:T(8,128)S(1)} custom-call(bf16[2,2,64,512]{3,2,1,0:T(8,128)(2,1)S(1)} %collective-permute-done.1.far, f32[2,5,64,512]{3,2,1,0:T(8,128)S(1)} %get-tuple-element.11.before, bf16[3,1536,512]{2,1,0:T(8,128)(2,1)S(1)} %get-tuple-element.12.v1, ...), custom_call_target="tpu_custom_call", output_to_operand_aliasing={{}: (1, {})} | custom-call | flops 2000000000 | bytes 1024 | tf_op jit(solution)/shard_map/pallas_call | solution.py:393
  21.2 0.0 collective-permute-done.2.near
  21.2 0.0 copy-done.1
  21.2 0.0 copy-done.2
  21.2 0.0 copy-done.3
  21.2 7.5 %shard_map.77 = (bf16[8,256,128]{2,1,0:T(8,128)(2,1)}, f32[2,5,64,512]{3,2,1,0:T(8,128)S(1)}) custom-call(bf16[2,2,64,512]{3,2,1,0:T(8,128)(2,1)S(1)} %shard_map.74.pair, bf16[2,2,64,512]{3,2,1,0:T(8,128)(2,1)S(1)} %collective-permute-done.1.far, bf16[2,2,64,512]{3,2,1,0:T(8,128)(2,1)S(1)} %collective-permute-done.2.near, ...), custom_call_target="tpu_custom_call", output_to_operand_aliasing={{1}: (3, {})} | custom-call | flops 8000000000 | bytes 1024 | tf_op jit(solution)/shard_map/pallas_call | solution.py:403
  (2 shorter events, 0.0 us)
Async XLA Ops:
  0.0 1.7 %collective-permute-start = (bf16[2,64,512]{2,1,0:T(8,128)(2,1)}, bf16[2,64,512]{2,1,0:T(8,128)(2,1)S(1)}, u32[]{:S(2)}, u32[]{:S(2)}) collective-permute-start(bf16[2,64,512]{2,1,0:T(8,128)(2,1)} %bitcast.4), channel_id=1, source_target_pairs={{0,8},{8,0},{1,9},{9,1},{2,10},{10,2},{3,11},{11,3},{4,12},{12,4},... | collective-permute-start | bytes 393224 | tf_op jit(solution)/shard_map/ppermute | solution.py:342
  0.5 12.7 %slice-start = ((s8[7077888]{0:T(1024)(128)(4,1)}), s8[4194304]{0:T(1024)(128)(4,1)S(1)}, s32[]{:S(2)}) async-start(s8[7077888]{0:T(1024)(128)(4,1)} %bitcast.2), calls=%async_computation | async-start | bytes 8388608
  1.6 11.6 %slice-start.1 = ((s8[7077888]{0:T(1024)(128)(4,1)}), s8[2883584]{0:T(1024)(128)(4,1)S(1)}, s32[]{:S(2)}) async-start(s8[7077888]{0:T(1024)(128)(4,1)} %bitcast.2), calls=%async_computation.1 | async-start | bytes 5767168
  1.6 11.6 %copy-start = (bf16[3,3,3,256,128]{4,3,2,1,0:T(8,128)(2,1)S(1)}, bf16[3,3,3,256,128]{4,3,2,1,0:T(8,128)(2,1)}, u32[]{:S(2)}) copy-start(bf16[3,3,3,256,128]{4,3,2,1,0:T(8,128)(2,1)} %w3.1) | copy-start | bytes 5308420
  1.7 11.5 %collective-permute-start.1 = (bf16[2,2,64,512]{3,2,1,0:T(8,128)(2,1)S(1)}, bf16[2,2,64,512]{3,2,1,0:T(8,128)(2,1)S(1)}, u32[]{:S(2)}, u32[]{:S(2)}) collective-permute-start(bf16[2,2,64,512]{3,2,1,0:T(8,128)(2,1)S(1)} %shard_map.74.pair), channel_id=1, source_target_pairs={{0,9},{1,10},{2,11},{3,12},{4,13},{5,14},{6,15},{9,0},{10,1},{11,2... | collective-permute-start | bytes 786440 | tf_op jit(solution)/shard_map/ppermute | solution.py:366
  13.2 8.0 %collective-permute-start.2 = (bf16[2,2,64,512]{3,2,1,0:T(8,128)(2,1)S(1)}, bf16[2,2,64,512]{3,2,1,0:T(8,128)(2,1)S(1)}, u32[]{:S(2)}, u32[]{:S(2)}) collective-permute-start(bf16[2,2,64,512]{3,2,1,0:T(8,128)(2,1)S(1)} %collective-permute-done.1.far), channel_id=1, source_target_pairs={{0,8},{8,0},{1,9},{9,1},{2,10},{10,2},{3,11},{11,3},{4,12},{12,4},... | collective-permute-start | bytes 786440 | tf_op jit(solution)/shard_map/ppermute | solution.py:367
  19.3 1.8 %copy-start.1 = (bf16[512]{0:T(512)(128)(2,1)S(1)}, bf16[512]{0:T(512)(128)(2,1)}, u32[]{:S(2)}) copy-start(bf16[512]{0:T(512)(128)(2,1)} %b1.1) | copy-start | bytes 3076
  19.4 1.8 %copy-start.2 = (bf16[256]{0:T(256)(128)(2,1)S(1)}, bf16[256]{0:T(256)(128)(2,1)}, u32[]{:S(2)}) copy-start(bf16[256]{0:T(256)(128)(2,1)} %b2.1) | copy-start | bytes 1540
  19.4 1.8 %copy-start.3 = (bf16[128]{0:T(256)(128)(2,1)S(1)}, bf16[128]{0:T(256)(128)(2,1)}, u32[]{:S(2)}) copy-start(bf16[128]{0:T(256)(128)(2,1)} %b3.1) | copy-start | bytes 772

commit v6 on v3

--- a/solution.py
+++ b/solution.py
@@ -10,7 +10,8 @@
 
 
 def silu(v):
-    return v / (1.0 + jnp.exp(-v))
+    half = 0.5 * v
+    return half + half * jnp.tanh(half)
 
 
 def shifted(v):
@@ -83,28 +84,34 @@
     target[(*at, slice(None), slice(2 * chans, 3 * chans))] = after.astype(BF16)
 
 
-def pair_kernel(own, other, pair):
-    pair[0] = own[...]
-    pair[1] = other[...]
-
-
-def early_kernel(pair, w1, w2, w3, acc, v1, wn, v2, v3, cat, raw, sems):
-    rows, cols, c1 = pair.shape[1:]
+def mark_kernel(other, out):
+    pass
+
+
+def halo_rows(i, rows):
+    return jnp.where(i < 2, 0, rows), jnp.where(i < 1, 1, rows + 1)
+
+
+def early_kernel(own, other, w1, w2, w3, mine, acc, v1, wn, v2, v3, cat, raw, sems, own_sem):
+    rows, cols, c1 = other.shape
     second = lax.axis_index("sect") > 0
 
     def copy(t, i):
         target = raw.at[i, t] if t < 2 else wn.at[i]
         return pltpu.make_async_copy(w1.at[t, i], target, sems.at[i, t])
 
+    load = pltpu.make_async_copy(own, mine, own_sem)
+    load.start()
     for i in range(3):
         for t in range(3):
             copy(t, i).start()
-    for r in range(rows):
-        mine, other = pair[0, r].astype(F32), pair[1, r].astype(F32)
-        put_cat(cat, (0, r), silu(jnp.where(second, other, mine)))
-        put_cat(cat, (1, r), silu(mine))
     merge_space(w3, v3, 16)
     merge_space(w2, v2, 16)
+    load.wait()
+    for r in range(rows):
+        v = mine[r].astype(F32)
+        put_cat(cat, (0, r), silu(jnp.where(second, other[r].astype(F32), v)))
+        put_cat(cat, (1, r), silu(v))
     size = rows * cols
     acc[...] = jnp.zeros(acc.shape, F32)
 
@@ -123,10 +130,26 @@
     lax.fori_loop(0, 3, tap, 0)
 
 
+def middle_kernel(halo, before, wn, acc, cat):
+    cols, c1 = halo.shape[1:]
+    rows = acc.shape[1] - 2
+    for r in range(4):
+        put_cat(cat, (r,), silu(halo[r].astype(F32)))
+
+    def tap(i, _):
+        lhs = cat[pl.ds(i, 2)].reshape(2 * cols, 3 * c1)
+        value = dot(lhs, wn[i].reshape(3 * c1, c1)).reshape(2, cols, c1)
+        for r, m in enumerate(halo_rows(i, rows)):
+            acc[1, m] += value[r]
+        return 0
+
+    lax.fori_loop(0, 3, tap, 0)
+
+
 def late_kernel(
-    pair, far, near, acc, v1, wn, b1, v2, b2, v3, b3, out, hcat, mcat, lcat, wide
+    own, halo, own0, halo0, before, v1, wn, b1, v2, b2, v3, b3, out, acc, hcat, mcat, lcat, wide
 ):
-    rows, cols, c1 = pair.shape[1:]
+    rows, cols, c1 = own.shape
     c2 = b2.shape[0]
     c3 = b3.shape[0]
     second = lax.axis_index("sect") > 0
@@ -136,33 +159,27 @@
 
     def feature(f, r):
         if r < 2:
-            if f == 0:
-                return jnp.where(second, far[0, r].astype(F32), near[0, r].astype(F32))
-            return jnp.where(second, far[1, r].astype(F32), near[0, r].astype(F32))
-        if r < rows + 2:
-            mine = pair[0, r - 2].astype(F32)
-            if f == 1:
-                return mine
-            return jnp.where(second, pair[1, r - 2].astype(F32), mine)
-        r = r - rows - 2
-        if f == 0:
-            return jnp.where(second, near[1, r].astype(F32), far[1, r].astype(F32))
-        return jnp.where(second, near[0, r].astype(F32), far[1, r].astype(F32))
+            mine, other = halo[r], halo0[r]
+        elif r < rows + 2:
+            mine, other = own[r - 2], own0[r - 2]
+        else:
+            mine, other = halo[r - rows], halo0[r - rows]
+        mine = mine.astype(F32)
+        if f == 1:
+            return mine
+        return jnp.where(second, other.astype(F32), mine)
 
     mrows = rows + 2
-    for f in range(2):
-        for r in range(4):
-            put_cat(hcat, (f, r), silu(feature(f, r if r < 2 else r + rows)))
-    size = 2 * cols
+    for r in range(4):
+        put_cat(hcat, (r,), silu(feature(0, r if r < 2 else r + rows)))
 
     def tap(i, _):
-        lhs = jnp.concatenate([hcat[f, pl.ds(i, 2)].reshape(size, 3 * c1) for f in range(2)], axis=0)
-        part = dot(lhs[:size], v1[i])
-        total = dot(lhs, wn[i].reshape(3 * c1, c1))
-        for f in range(2):
-            value = (total[f * size : (f + 1) * size] + part).reshape(2, cols, c1)
-            acc[f, jnp.where(i < 2, 0, rows)] += value[0]
-            acc[f, jnp.where(i < 1, 1, rows + 1)] += value[1]
+        lhs = hcat[pl.ds(i, 2)].reshape(2 * cols, 3 * c1)
+        part = dot(lhs, v1[i]).reshape(2, cols, c1)
+        now = dot(lhs, wn[i].reshape(3 * c1, c1)).reshape(2, cols, c1)
+        for r, m in enumerate(halo_rows(i, rows)):
+            acc[0, m] += part[r] + now[r]
+            acc[1, m] += part[r]
         return 0
 
     lax.fori_loop(0, 3, tap, 0)
@@ -237,58 +254,73 @@
     c2 = conv_second.shape[4]
     c3 = conv_third.shape[4]
     tiles = lax.axis_size("tile")
-    swap = [(0, 1), (1, 0)]
-    apart = [(i, tiles + i + 1) for i in range(tiles - 1)]
-    apart += [(tiles + i + 1, i) for i in range(tiles - 1)]
+    forward = [(i, i + 1) for i in range(tiles - 1)]
+    backward = [(i + 1, i) for i in range(tiles - 1)]
+    across = [(0, 1)]
     vmem = pl.BlockSpec(memory_space=pltpu.VMEM)
     anywhere = pl.BlockSpec(memory_space=pl.ANY)
-
-    other = lax.ppermute(own, "sect", swap)
-    pair = pl.pallas_call(
-        pair_kernel,
-        out_shape=pltpu.VMEM((2, rows, cols, c1), BF16),
-        in_specs=[vmem] * 2,
+    acc_shape = pltpu.VMEM((2, rows + 2, cols, c1), F32)
+    own_shape = pltpu.VMEM((rows, cols, c1), BF16)
+
+    own0 = lax.ppermute(own, "sect", across)
+    top = lax.ppermute(own[rows - 2 :], "tile", forward)
+    bottom = lax.ppermute(own[:2], "tile", backward)
+    own0 = pl.pallas_call(
+        mark_kernel,
+        out_shape=own_shape,
+        in_specs=[vmem],
         out_specs=vmem,
+        input_output_aliases={0: 0},
         cost_estimate=pl.CostEstimate(flops=12_000_000_000, bytes_accessed=1024, transcendentals=0),
         compiler_params=pltpu.CompilerParams(vmem_limit_bytes=1 << 20),
-    )(in_vmem(own), in_vmem(other))
-    if rows == 2:
-        edge = pair
-    else:
-        edge = jnp.where(lax.axis_index("sect") == 0, pair[:, rows - 2 :], pair[:, :2])
-    far = lax.ppermute(edge, ("sect", "tile"), apart)
-    near = lax.ppermute(far, "sect", swap)
-    acc, v1, wn, v2, v3 = pl.pallas_call(
+    )(in_vmem(own0))
+    halo = jnp.concatenate([top, bottom], axis=0)
+    halo0 = lax.ppermute(halo, "sect", across)
+    mine, acc, v1, wn, v2, v3 = pl.pallas_call(
         early_kernel,
         out_shape=[
-            pltpu.VMEM((2, rows + 2, cols, c1), F32),
+            own_shape,
+            acc_shape,
             pltpu.VMEM((3, 3 * c1, c1), BF16),
             pltpu.VMEM((3, 3, c1, c1), BF16),
             pltpu.VMEM((2, 2, 2, 2 * c1, 2 * c2), BF16),
             pltpu.VMEM((2, 2, 2, 2 * c2, 2 * c3), BF16),
         ],
-        in_specs=[vmem, anywhere, vmem, vmem],
-        out_specs=[vmem] * 5,
+        in_specs=[anywhere, vmem, anywhere, vmem, vmem],
+        out_specs=[vmem] * 6,
         scratch_shapes=[
             pltpu.VMEM((2, rows, cols, 3 * c1), BF16),
             pltpu.VMEM((3, 2, 3, c1, c1), BF16),
             pltpu.SemaphoreType.DMA((3, 3)),
+            pltpu.SemaphoreType.DMA,
         ],
         cost_estimate=pl.CostEstimate(flops=6_000_000_000, bytes_accessed=1024, transcendentals=0),
         compiler_params=pltpu.CompilerParams(vmem_limit_bytes=16 << 20),
     )(
-        in_vmem(pair),
+        pltpu.with_memory_space_constraint(own, pltpu.HBM),
+        in_vmem(own0),
         pltpu.with_memory_space_constraint(conv_first, pltpu.HBM),
         in_vmem(conv_second),
         in_vmem(conv_third),
     )
-    out = pl.pallas_call(
+    acc = pl.pallas_call(
+        middle_kernel,
+        out_shape=acc_shape,
+        in_specs=[vmem] * 3,
+        out_specs=vmem,
+        input_output_aliases={1: 0},
+        scratch_shapes=[pltpu.VMEM((4, cols, 3 * c1), BF16)],
+        cost_estimate=pl.CostEstimate(flops=2_000_000_000, bytes_accessed=1024, transcendentals=0),
+        compiler_params=pltpu.CompilerParams(vmem_limit_bytes=8 << 20),
+    )(in_vmem(halo), in_vmem(acc), in_vmem(wn))
+    out, _ = pl.pallas_call(
         late_kernel,
-        out_shape=jax.ShapeDtypeStruct((4 * rows, 4 * cols, c3), BF16),
-        in_specs=[vmem] * 11,
-        out_specs=vmem,
+        out_shape=[jax.ShapeDtypeStruct((4 * rows, 4 * cols, c3), BF16), acc_shape],
+        in_specs=[vmem] * 12,
+        out_specs=[vmem] * 2,
+        input_output_aliases={4: 1},
         scratch_shapes=[
-            pltpu.VMEM((2, 4, cols, 3 * c1), BF16),
+            pltpu.VMEM((4, cols, 3 * c1), BF16),
             pltpu.VMEM((2, rows + 2, cols, 3 * c1), BF16),
             pltpu.VMEM((2, 2 * rows + 2, cols, 4 * c2), BF16),
             pltpu.VMEM((4 * rows, 4 * cols, c3), F32),
@@ -296,9 +328,10 @@
         cost_estimate=pl.CostEstimate(flops=8_000_000_000, bytes_accessed=1024, transcendentals=0),
         compiler_params=pltpu.CompilerParams(vmem_limit_bytes=14 << 20),
     )(
-        in_vmem(pair),
-        in_vmem(far),
-        in_vmem(near),
+        in_vmem(mine),
+        in_vmem(halo),
+        in_vmem(own0),
+        in_vmem(halo0),
         in_vmem(acc),
         in_vmem(v1),
         in_vmem(wn),

time: 29.2 us -> 32.3 us (1.11)
  starting transfers between devices: 5.09 us -> 9.23 us
  waiting for transfers between devices: 7.88 us -> 4.29 us
  Pallas kernels: 14.2 us -> 16.4 us
    ppermute x3 -> x4, starting transfers between devices: 5.09 us -> 9.23 us  [the longest x1 4.9 us: per_device(): top = lax.ppermute(own[rows - 2:], 'tile', forward)]
    ppermute x3 -> x4, waiting for transfers between devices: 7.88 us -> 4.29 us  [the longest x1 4.02 us: per_device(): bottom = lax.ppermute(own[:2], 'tile', backward)]
    pallas_call x3 -> x4, Pallas kernels: 14.2 us -> 16.4 us  [the longest x1 7.85 us: per_device(): pl.pallas_call(early_kernel, out_shape=[own_shape, acc_shape, pltpu.VMEM(...]
    unnamed x14 -> x13, local copies, waits for them, and re-layouts: 1.7 us -> 1.98 us
  transfers between devices with their start and end apart: 3 -> 4, of which waited for: 2 -> 2; matrix products, arithmetic and copies ran while one was open for 0% -> 0% of each run, Pallas kernels for 21% -> 29%
where the time goes in v6:
time: 32.3 us; the launch traced here: 32 us
  Pallas kernels  16.4 us (51%)
  starting transfers between devices  9.23 us (29%)
  waiting for transfers between devices  4.29 us (13%)
  local copies, waits for them, and re-layouts  1.99 us (6%)
    pallas_call x1, Pallas kernels, per_device(): pl.pallas_call(early_kernel, out_shape=[own_shape, acc_shape, pltpu.VMEM(...  7.85 us
    pallas_call x1, Pallas kernels, per_device(): pl.pallas_call(late_kernel, out_shape=[jax.ShapeDtypeStruct((4 * rows, 4...  7.21 us
    ppermute x1, starting transfers between devices, per_device(): top = lax.ppermute(own[rows - 2:], 'tile', forward)  4.9 us
    ppermute x1, waiting for transfers between devices, per_device(): bottom = lax.ppermute(own[:2], 'tile', backward)  4.02 us
    unnamed x13, local copies, waits for them, and re-layouts  1.98 us
    ppermute x1, starting transfers between devices, per_device(): halo0 = lax.ppermute(halo, 'sect', across)  1.57 us
    ppermute x1, starting transfers between devices, per_device(): own0 = lax.ppermute(own, 'sect', across)  1.47 us
    pallas_call x1, Pallas kernels, per_device(): pl.pallas_call(middle_kernel, out_shape=acc_shape, in_specs=[vmem] * 3, o...  1.32 us
  transfers between devices with their start and end apart: 4, of which 2 were waited for; matrix products, arithmetic and copies ran while one was open for 0% of the time, Pallas kernels for 29%

profile of v6, /device:TPU:0, one launch (start us, length us, event | category | flops | bytes accessed | tf_op | source)
XLA Modules:
  0.0 32.0 jit_solution(3675947595834143464)
XLA Ops:
  0.0 4.9 %collective-permute-start.1 = (bf16[2,64,512]{2,1,0:T(8,128)(2,1)}, bf16[2,64,512]{2,1,0:T(8,128)(2,1)S(1)}, u32[]{:S(2)}, u32[]{:S(2)}) collective-permute-start(bf16[2,64,512]{2,1,0:T(8,128)(2,1)} %bitcast.4), channel_id=1, source_target_pairs={{0,1},{1,2},{2,3},{3,4},{4,5},{5,6},{6,7},{8,9},{9,10},{10,11},{11... | collective-permute-start | bytes 393224 | tf_op jit(solution)/shard_map/ppermute | solution.py:266
  4.9 1.3 %collective-permute-start.2 = (bf16[2,64,512]{2,1,0:T(8,128)(2,1)}, bf16[2,64,512]{2,1,0:T(8,128)(2,1)S(1)}, u32[]{:S(2)}, u32[]{:S(2)}) collective-permute-start(bf16[2,64,512]{2,1,0:T(8,128)(2,1)} %bitcast.5), channel_id=1, source_target_pairs={{1,0},{2,1},{3,2},{4,3},{5,4},{6,5},{7,6},{9,8},{10,9},{11,10},{12... | collective-permute-start | bytes 393224 | tf_op jit(solution)/shard_map/ppermute | solution.py:267
  6.2 1.5 %collective-permute-start = (bf16[2,64,512]{2,1,0:T(8,128)(2,1)}, bf16[2,64,512]{2,1,0:T(8,128)(2,1)S(1)}, u32[]{:S(2)}, u32[]{:S(2)}) collective-permute-start(bf16[2,64,512]{2,1,0:T(8,128)(2,1)} %bitcast.6), channel_id=1, source_target_pairs={{0,8},{1,9},{2,10},{3,11},{4,12},{5,13},{6,14},{7,15},{16,24},{17,... | collective-permute-start | bytes 393224 | tf_op jit(solution)/shard_map/ppermute | solution.py:265
  7.7 0.3 collective-permute-done.1
  8.0 4.0 %collective-permute-done.2 = bf16[2,64,512]{2,1,0:T(8,128)(2,1)S(1)} collective-permute-done((bf16[2,64,512]{2,1,0:T(8,128)(2,1)}, bf16[2,64,512]{2,1,0:T(8,128)(2,1)S(1)}, u32[]{:S(2)}, u32[]{:S(2)}) %collective-permute-start.2) | collective-permute-done | bytes 131104 | tf_op jit(solution)/shard_map/ppermute | solution.py:267
  12.0 0.0 slice-start
  12.0 0.0 slice-start.1
  12.0 0.0 copy-start
  12.0 1.6 %collective-permute-start.3 = (bf16[4,64,512]{2,1,0:T(8,128)(2,1)S(1)}, bf16[4,64,512]{2,1,0:T(8,128)(2,1)S(1)}, u32[]{:S(2)}, u32[]{:S(2)}) collective-permute-start(bf16[4,64,512]{2,1,0:T(8,128)(2,1)S(1)} %constant_dynamic-update-slice_fusion.halo), channel_id=1, source_target_pairs={{0,8},{1,9},{2,10},{3,11},{4,12},{5,13},{6,14},{7,15},{16,24},{17,... | collective-permute-start | bytes 786440 | tf_op jit(solution)/shard_map/ppermute | solution.py:278
  13.6 0.0 collective-permute-done.other
  13.6 0.6 %slice-done = s8[4194304]{0:T(1024)(128)(4,1)S(1)} async-done(((s8[7077888]{0:T(1024)(128)(4,1)}), s8[4194304]{0:T(1024)(128)(4,1)S(1)}, s32[]{:S(2)}) %slice-start) | async-done | bytes 4194328
  14.2 0.9 %slice-done.1 = s8[2883584]{0:T(1024)(128)(4,1)S(1)} async-done(((s8[7077888]{0:T(1024)(128)(4,1)}), s8[2883584]{0:T(1024)(128)(4,1)S(1)}, s32[]{:S(2)}) %slice-start.1) | async-done | bytes 2883608
  15.1 0.5 %copy-done = bf16[3,3,3,256,128]{4,3,2,1,0:T(8,128)(2,1)S(1)} copy-done((bf16[3,3,3,256,128]{4,3,2,1,0:T(8,128)(2,1)S(1)}, bf16[3,3,3,256,128]{4,3,2,1,0:T(8,128)(2,1)}, u32[]{:S(2)}) %copy-start) | copy-done | bytes 1769496
  15.6 7.9 %shard_map.74 = (bf16[2,64,512]{2,1,0:T(8,128)(2,1)S(1)}, f32[2,4,64,512]{3,2,1,0:T(8,128)S(1)}, bf16[3,1536,512]{2,1,0:T(8,128)(2,1)S(1)}, bf16[3,3,512,512]{3,...) custom-call(bf16[2,64,512]{2,1,0:T(8,128)(2,1)} %bitcast.7, ...), custom_call_target="tpu_custom_call" | custom-call | flops 6000000000 | bytes 1024 | tf_op jit(solution)/shard_map/pallas_call | solution.py:279
  23.4 0.0 copy-start.1
  23.4 0.0 copy-start.2
  23.4 0.0 copy-start.3
  23.5 1.3 %shard_map.75.before = f32[2,4,64,512]{3,2,1,0:T(8,128)S(1)} custom-call(bf16[4,64,512]{2,1,0:T(8,128)(2,1)S(1)} %constant_dynamic-update-slice_fusion.halo, f32[2,4,64,512]{3,2,1,0:T(8,128)S(1)} %get-tuple-element.13.before, bf16[3,3,512,512]{3,2,1,0:T(8,128)(2,1)S(1)} %get-tuple-element.14.wn), custom_call_target="tpu_custom_call", output_to_operand_aliasing={{}: (1, {})} | custom-call | flops 2000000000 | bytes 1024 | tf_op jit(solution)/shard_map/pallas_call | solution.py:306
  24.8 0.0 collective-permute-done.3.halo0
  24.8 0.0 copy-done.1
  24.8 0.0 copy-done.2
  24.8 0.0 copy-done.3
  24.8 7.2 %shard_map.76 = (bf16[8,256,128]{2,1,0:T(8,128)(2,1)}, f32[2,4,64,512]{3,2,1,0:T(8,128)S(1)}) custom-call(bf16[2,64,512]{2,1,0:T(8,128)(2,1)S(1)} %get-tuple-element.12.own, bf16[4,64,512]{2,1,0:T(8,128)(2,1)S(1)} %constant_dynamic-update-slice_fusion.halo, bf16[2,64,512]{2,1,0:T(8,128)(2,1)S(1)} %shard_map.73.other.own0, ...), custom_call_target="tpu_custom_call", output_to_operand_aliasing={{1}: (4, {})} | custom-call | flops 8000000000 | bytes 1024 | tf_op jit(solution)/shard_map/pallas_call | solution.py:316
  (4 shorter events, 0.0 us)
Async XLA Ops:
  0.0 8.0 %collective-permute-start.1 = (bf16[2,64,512]{2,1,0:T(8,128)(2,1)}, bf16[2,64,512]{2,1,0:T(8,128)(2,1)S(1)}, u32[]{:S(2)}, u32[]{:S(2)}) collective-permute-start(bf16[2,64,512]{2,1,0:T(8,128)(2,1)} %bitcast.4), channel_id=1, source_target_pairs={{0,1},{1,2},{2,3},{3,4},{4,5},{5,6},{6,7},{8,9},{9,10},{10,11},{11... | collective-permute-start | bytes 393224 | tf_op jit(solution)/shard_map/ppermute | solution.py:266
  4.9 7.1 %collective-permute-start.2 = (bf16[2,64,512]{2,1,0:T(8,128)(2,1)}, bf16[2,64,512]{2,1,0:T(8,128)(2,1)S(1)}, u32[]{:S(2)}, u32[]{:S(2)}) collective-permute-start(bf16[2,64,512]{2,1,0:T(8,128)(2,1)} %bitcast.5), channel_id=1, source_target_pairs={{1,0},{2,1},{3,2},{4,3},{5,4},{6,5},{7,6},{9,8},{10,9},{11,10},{12... | collective-permute-start | bytes 393224 | tf_op jit(solution)/shard_map/ppermute | solution.py:267
  6.2 7.4 %collective-permute-start = (bf16[2,64,512]{2,1,0:T(8,128)(2,1)}, bf16[2,64,512]{2,1,0:T(8,128)(2,1)S(1)}, u32[]{:S(2)}, u32[]{:S(2)}) collective-permute-start(bf16[2,64,512]{2,1,0:T(8,128)(2,1)} %bitcast.6), channel_id=1, source_target_pairs={{0,8},{1,9},{2,10},{3,11},{4,12},{5,13},{6,14},{7,15},{16,24},{17,... | collective-permute-start | bytes 393224 | tf_op jit(solution)/shard_map/ppermute | solution.py:265
  12.0 2.2 %slice-start = ((s8[7077888]{0:T(1024)(128)(4,1)}), s8[4194304]{0:T(1024)(128)(4,1)S(1)}, s32[]{:S(2)}) async-start(s8[7077888]{0:T(1024)(128)(4,1)} %bitcast.2), calls=%async_computation | async-start | bytes 8388608
  12.0 3.1 %slice-start.1 = ((s8[7077888]{0:T(1024)(128)(4,1)}), s8[2883584]{0:T(1024)(128)(4,1)S(1)}, s32[]{:S(2)}) async-start(s8[7077888]{0:T(1024)(128)(4,1)} %bitcast.2), calls=%async_computation.1 | async-start | bytes 5767168
  12.0 3.5 %copy-start = (bf16[3,3,3,256,128]{4,3,2,1,0:T(8,128)(2,1)S(1)}, bf16[3,3,3,256,128]{4,3,2,1,0:T(8,128)(2,1)}, u32[]{:S(2)}) copy-start(bf16[3,3,3,256,128]{4,3,2,1,0:T(8,128)(2,1)} %w3.1) | copy-start | bytes 5308420
  12.0 12.8 %collective-permute-start.3 = (bf16[4,64,512]{2,1,0:T(8,128)(2,1)S(1)}, bf16[4,64,512]{2,1,0:T(8,128)(2,1)S(1)}, u32[]{:S(2)}, u32[]{:S(2)}) collective-permute-start(bf16[4,64,512]{2,1,0:T(8,128)(2,1)S(1)} %constant_dynamic-update-slice_fusion.halo), channel_id=1, source_target_pairs={{0,8},{1,9},{2,10},{3,11},{4,12},{5,13},{6,14},{7,15},{16,24},{17,... | collective-permute-start | bytes 786440 | tf_op jit(solution)/shard_map/ppermute | solution.py:278
  23.4 1.4 %copy-start.1 = (bf16[512]{0:T(512)(128)(2,1)S(1)}, bf16[512]{0:T(512)(128)(2,1)}, u32[]{:S(2)}) copy-start(bf16[512]{0:T(512)(128)(2,1)} %b1.1) | copy-start | bytes 3076
  23.4 1.4 %copy-start.2 = (bf16[256]{0:T(256)(128)(2,1)S(1)}, bf16[256]{0:T(256)(128)(2,1)}, u32[]{:S(2)}) copy-start(bf16[256]{0:T(256)(128)(2,1)} %b2.1) | copy-start | bytes 1540
  23.4 1.4 %copy-start.3 = (bf16[128]{0:T(256)(128)(2,1)S(1)}, bf16[128]{0:T(256)(128)(2,1)}, u32[]{:S(2)}) copy-start(bf16[128]{0:T(256)(128)(2,1)} %b3.1) | copy-start | bytes 772

commit v7 on v4

--- a/solution.py
+++ b/solution.py
@@ -68,7 +68,7 @@
                         else:
                             columns = (row[0], row[1] + row[2])
                         for j in range(2):
-                            target[t, b, i, pl.ds(j * cin + at, step), pl.ds(a * cout, cout)] = columns[
+                            target[b, t, i, pl.ds(j * cin + at, step), pl.ds(a * cout, cout)] = columns[
                                 j
                             ].astype(BF16)
         return 0
@@ -102,23 +102,28 @@
         for r in range(2):
             put_cat(cat, (f, r), silu(source[at[f], r].astype(F32)))
 
-    def tap(k, _):
-        middle = k == 1
-        i = jnp.where(middle, 1, jnp.where(upper, 0, 2))
+    def outer(k, _):
+        i = jnp.where(upper, 0, 2)
         both = cat[...].reshape(2 * size, 3 * c1)
         part = dot(both[:size], v1[i])
         total = dot(both, wn[i].reshape(3 * c1, c1))
-        m = [
-            jnp.where(middle, jnp.where(upper, rows + 2, rows + 1), jnp.where(upper, 0, rows)),
-            jnp.where(middle, jnp.where(upper, 0, rows + 2), jnp.where(upper, 1, rows + 1)),
-        ]
+        m = jnp.where(upper, 0, rows)
         for f in range(2):
-            value = (total[f * size : (f + 1) * size] + part).reshape(2, cols, c1)
-            for r in range(2):
-                acc[f, m[r]] += value[r]
-        return 0
-
-    lax.fori_loop(0, 2, tap, 0)
+            acc[f, pl.ds(m, 2)] += (total[f * size : (f + 1) * size] + part).reshape(2, cols, c1)
+        return 0
+
+    def middle(k, _):
+        r = jnp.where(upper, 1, 0)
+        one = [cat[f, r] for f in range(2)]
+        part = dot(one[0], v1[1])
+        total = dot(jnp.concatenate(one, axis=0), wn[1].reshape(3 * c1, c1))
+        m = jnp.where(upper, 0, rows + 1)
+        for f in range(2):
+            acc[f, m] += total[f * cols : (f + 1) * cols] + part
+        return 0
+
+    lax.fori_loop(0, 1, outer, 0)
+    lax.fori_loop(0, 1, middle, 0)
 
 
 def early_kernel(pair, w1, w2, w3, acc, v1, wn, v2, v3, cat, raw, sems):
@@ -208,9 +213,9 @@
         now = [early, early]
         for i in range(2):
             lhs = [mcat[f, i : i + wins, :, lanes].reshape(wins * cols, 2 * c1) for f in range(2)]
-            early = early + dot(lhs[0], v2[0, b, i])
+            early = early + dot(lhs[0], v2[b, 0, i])
             for f in range(2):
-                now[f] = now[f] + dot(lhs[f], v2[1, b, i])
+                now[f] = now[f] + dot(lhs[f], v2[b, 1, i])
         for f in range(2):
             total = early + now[f]
             for w in range(wins):
@@ -236,11 +241,11 @@
     for q in range(4):
         b = 1 if q % 2 == 0 else 0
         at = (0, c2, c2, 2 * c2)[q]
-        total = jnp.zeros((wins * cols, 2 * c3), F32)
-        for i in range(2):
-            for f in range(2):
-                lhs = lcat[f, i : i + wins, :, at : at + 2 * c2].reshape(wins * cols, 2 * c2)
-                total = total + dot(lhs, v3[f, b, i])
+        lhs = jnp.concatenate(
+            [lcat[f, i : i + wins, :, at : at + 2 * c2].reshape(wins * cols, 2 * c2) for f in range(2) for i in range(2)],
+            axis=1,
+        )
+        total = dot(lhs, v3[b].reshape(8 * c2, 2 * c3))
         for o in range(4 * rows):
             a = 1 - o % 2
             w = (o + 1) // 2

time: 28.3 us -> 27.1 us (0.958)
  Pallas kernels: 15.9 us -> 14.7 us
    pallas_call x1, Pallas kernels: 6.96 us -> 6.18 us  [per_device(): pl.pallas_call(late_kernel, out_shape=[jax.ShapeDtypeStruct((4 * rows, 4...]
    pallas_call x1, Pallas kernels: 1.76 us -> 1.3 us  [per_device(): pl.pallas_call(middle_kernel, out_shape=acc_shape, in_specs=[vmem] * 4, o...]
where the time goes in v7:
time: 27.1 us; the launch traced here: 26.9 us
  Pallas kernels  14.7 us (54%)
  waiting for transfers between devices  6.78 us (25%)
  starting transfers between devices  5.28 us (19%)
    ppermute x1, waiting for transfers between devices, per_device(): far = lax.ppermute(edge, ('sect', 'tile'), apart)  6.68 us
    pallas_call x1, Pallas kernels, per_device(): pl.pallas_call(late_kernel, out_shape=[jax.ShapeDtypeStruct((4 * rows, 4...  6.18 us
    pallas_call x1, Pallas kernels, per_device(): pl.pallas_call(early_kernel, out_shape=[pltpu.VMEM((2, rows + 3, cols, c1...  6.13 us
    ppermute x1, starting transfers between devices, per_device(): far = lax.ppermute(edge, ('sect', 'tile'), apart)  4.79 us
    pallas_call x1, Pallas kernels, per_device(): pl.pallas_call(middle_kernel, out_shape=acc_shape, in_specs=[vmem] * 4, o...  1.3 us
    pallas_call x1, Pallas kernels, per_device(): pl.pallas_call(load_kernel, out_shape=pair_shape, in_specs=[anywhere], ou...  1.06 us
  transfers between devices with their start and end apart: 3, of which 2 were waited for; matrix products, arithmetic and copies ran while one was open for 0% of the time, Pallas kernels for 32%

profile of v7, /device:TPU:0, one launch (start us, length us, event | category | flops | bytes accessed | tf_op | source)
XLA Modules:
  0.0 26.9 jit_solution(14720008767534393347)
XLA Ops:
  0.0 0.5 %collective-permute-start = (bf16[2,64,512]{2,1,0:T(8,128)(2,1)}, bf16[2,64,512]{2,1,0:T(8,128)(2,1)S(1)}, u32[]{:S(2)}, u32[]{:S(2)}) collective-permute-start(bf16[2,64,512]{2,1,0:T(8,128)(2,1)} %bitcast.4), channel_id=1, source_target_pairs={{0,8},{8,0},{1,9},{9,1},{2,10},{10,2},{3,11},{11,3},{4,12},{12,4},... | collective-permute-start | bytes 393224 | tf_op jit(solution)/shard_map/ppermute | solution.py:274
  0.5 0.0 slice-start
  0.5 1.1 %shard_map.73.half = bf16[2,2,64,512]{3,2,1,0:T(8,128)(2,1)S(1)} custom-call(bf16[2,64,512]{2,1,0:T(8,128)(2,1)} %bitcast.5), custom_call_target="tpu_custom_call" | custom-call | flops 6000000000 | bytes 1024 | tf_op jit(solution)/shard_map/pallas_call | solution.py:276
  1.6 0.0 slice-start.1
  1.6 0.0 copy-start
  1.6 0.1 collective-permute-done.other
  1.7 4.8 %collective-permute-start.1 = (bf16[2,2,64,512]{3,2,1,0:T(8,128)(2,1)S(1)}, bf16[2,2,64,512]{3,2,1,0:T(8,128)(2,1)S(1)}, u32[]{:S(2)}, u32[]{:S(2)}) collective-permute-start(bf16[2,2,64,512]{3,2,1,0:T(8,128)(2,1)S(1)} %shard_map.74.pair), channel_id=1, source_target_pairs={{0,9},{1,10},{2,11},{3,12},{4,13},{5,14},{6,15},{9,0},{10,1},{11,2... | collective-permute-start | bytes 786440 | tf_op jit(solution)/shard_map/ppermute | solution.py:298
  6.5 6.7 %collective-permute-done.1.far = bf16[2,2,64,512]{3,2,1,0:T(8,128)(2,1)S(1)} collective-permute-done((bf16[2,2,64,512]{3,2,1,0:T(8,128)(2,1)S(1)}, bf16[2,2,64,512]{3,2,1,0:T(8,128)(2,1)S(1)}, u32[]{:S(2)}, u32[]{:S(2)}) %collective-permute-start.1) | collective-permute-done | bytes 262176 | tf_op jit(solution)/shard_map/ppermute | solution.py:298
  13.2 0.0 collective-permute-start.2
  13.2 0.0 slice-done
  13.2 0.0 slice-done.1
  13.2 0.0 copy-done
  13.2 6.1 %shard_map.75 = (f32[2,5,64,512]{3,2,1,0:T(8,128)S(1)}, bf16[3,1536,512]{2,1,0:T(8,128)(2,1)S(1)}, bf16[3,3,512,512]{3,2,1,0:T(8,128)(2,1)S(1)}, bf16[2,2,2,1024...) custom-call(bf16[2,2,64,512]{3,2,1,0:T(8,128)(2,1)S(1)} %shard_map.74.pair, bf16[3,3,3,512,512]{4,3,2,1,0:T(8,128)(2,1)} %w1.1, ...), custom_call_target="tpu_custom_call" | custom-call | flops 6000000000 | bytes 1024 | tf_op jit(solution)/shard_map/pallas_call | solution.py:300
  19.3 0.0 copy-start.1
  19.3 0.0 copy-start.2
  19.4 0.0 copy-start.3
  19.4 1.3 %shard_map.76.before = f32[2,5,64,512]{3,2,1,0:T(8,128)S(1)} custom-call(bf16[2,2,64,512]{3,2,1,0:T(8,128)(2,1)S(1)} %collective-permute-done.1.far, f32[2,5,64,512]{3,2,1,0:T(8,128)S(1)} %get-tuple-element.11.before, bf16[3,1536,512]{2,1,0:T(8,128)(2,1)S(1)} %get-tuple-element.12.v1, ...), custom_call_target="tpu_custom_call", output_to_operand_aliasing={{}: (1, {})} | custom-call | flops 2000000000 | bytes 1024 | tf_op jit(solution)/shard_map/pallas_call | solution.py:325
  20.7 0.0 collective-permute-done.2.near
  20.7 0.0 copy-done.1
  20.7 0.0 copy-done.2
  20.7 0.0 copy-done.3
  20.7 6.2 %shard_map.77 = (bf16[8,256,128]{2,1,0:T(8,128)(2,1)}, f32[2,5,64,512]{3,2,1,0:T(8,128)S(1)}) custom-call(bf16[2,2,64,512]{3,2,1,0:T(8,128)(2,1)S(1)} %shard_map.74.pair, bf16[2,2,64,512]{3,2,1,0:T(8,128)(2,1)S(1)} %collective-permute-done.1.far, bf16[2,2,64,512]{3,2,1,0:T(8,128)(2,1)S(1)} %collective-permute-done.2.near, ...), custom_call_target="tpu_custom_call", output_to_operand_aliasing={{1}: (3, {})} | custom-call | flops 8000000000 | bytes 1024 | tf_op jit(solution)/shard_map/pallas_call | solution.py:335
  (2 shorter events, 0.0 us)
Async XLA Ops:
  0.0 1.7 %collective-permute-start = (bf16[2,64,512]{2,1,0:T(8,128)(2,1)}, bf16[2,64,512]{2,1,0:T(8,128)(2,1)S(1)}, u32[]{:S(2)}, u32[]{:S(2)}) collective-permute-start(bf16[2,64,512]{2,1,0:T(8,128)(2,1)} %bitcast.4), channel_id=1, source_target_pairs={{0,8},{8,0},{1,9},{9,1},{2,10},{10,2},{3,11},{11,3},{4,12},{12,4},... | collective-permute-start | bytes 393224 | tf_op jit(solution)/shard_map/ppermute | solution.py:274
  0.5 12.7 %slice-start = ((s8[7077888]{0:T(1024)(128)(4,1)}), s8[4194304]{0:T(1024)(128)(4,1)S(1)}, s32[]{:S(2)}) async-start(s8[7077888]{0:T(1024)(128)(4,1)} %bitcast.2), calls=%async_computation | async-start | bytes 8388608
  1.6 11.6 %slice-start.1 = ((s8[7077888]{0:T(1024)(128)(4,1)}), s8[2883584]{0:T(1024)(128)(4,1)S(1)}, s32[]{:S(2)}) async-start(s8[7077888]{0:T(1024)(128)(4,1)} %bitcast.2), calls=%async_computation.1 | async-start | bytes 5767168
  1.6 11.6 %copy-start = (bf16[3,3,3,256,128]{4,3,2,1,0:T(8,128)(2,1)S(1)}, bf16[3,3,3,256,128]{4,3,2,1,0:T(8,128)(2,1)}, u32[]{:S(2)}) copy-start(bf16[3,3,3,256,128]{4,3,2,1,0:T(8,128)(2,1)} %w3.1) | copy-start | bytes 5308420
  1.7 11.5 %collective-permute-start.1 = (bf16[2,2,64,512]{3,2,1,0:T(8,128)(2,1)S(1)}, bf16[2,2,64,512]{3,2,1,0:T(8,128)(2,1)S(1)}, u32[]{:S(2)}, u32[]{:S(2)}) collective-permute-start(bf16[2,2,64,512]{3,2,1,0:T(8,128)(2,1)S(1)} %shard_map.74.pair), channel_id=1, source_target_pairs={{0,9},{1,10},{2,11},{3,12},{4,13},{5,14},{6,15},{9,0},{10,1},{11,2... | collective-permute-start | bytes 786440 | tf_op jit(solution)/shard_map/ppermute | solution.py:298
  13.2 7.5 %collective-permute-start.2 = (bf16[2,2,64,512]{3,2,1,0:T(8,128)(2,1)S(1)}, bf16[2,2,64,512]{3,2,1,0:T(8,128)(2,1)S(1)}, u32[]{:S(2)}, u32[]{:S(2)}) collective-permute-start(bf16[2,2,64,512]{3,2,1,0:T(8,128)(2,1)S(1)} %collective-permute-done.1.far), channel_id=1, source_target_pairs={{0,8},{8,0},{1,9},{9,1},{2,10},{10,2},{3,11},{11,3},{4,12},{12,4},... | collective-permute-start | bytes 786440 | tf_op jit(solution)/shard_map/ppermute | solution.py:299
  19.3 1.4 %copy-start.1 = (bf16[512]{0:T(512)(128)(2,1)S(1)}, bf16[512]{0:T(512)(128)(2,1)}, u32[]{:S(2)}) copy-start(bf16[512]{0:T(512)(128)(2,1)} %b1.1) | copy-start | bytes 3076
  19.3 1.4 %copy-start.2 = (bf16[256]{0:T(256)(128)(2,1)S(1)}, bf16[256]{0:T(256)(128)(2,1)}, u32[]{:S(2)}) copy-start(bf16[256]{0:T(256)(128)(2,1)} %b2.1) | copy-start | bytes 1540
  19.4 1.4 %copy-start.3 = (bf16[128]{0:T(256)(128)(2,1)S(1)}, bf16[128]{0:T(256)(128)(2,1)}, u32[]{:S(2)}) copy-start(bf16[128]{0:T(256)(128)(2,1)} %b3.1) | copy-start | bytes 772

commit v8 on v7

--- a/solution.py
+++ b/solution.py
@@ -167,7 +167,7 @@
 
 
 def late_kernel(
-    pair, far, near, before, v1, wn, b1, v2, b2, v3, b3, out, acc, hcat, mcat, lcat, wide
+    pair, far, near, before, v1, wn, b1, v2, b2, v3, b3, out, acc, hcat, mcat, lcat, wide, narrow, sems
 ):
     rows, cols, c1 = pair.shape[1:]
     c2 = b2.shape[0]
@@ -251,8 +251,12 @@
             w = (o + 1) // 2
             v = total[w * cols : (w + 1) * cols, a * c3 : (a + 1) * c3] + bias
             wide[o, pl.ds(q, cols, stride=4), :] = v
+    copies = [pltpu.make_async_copy(narrow.at[o], out.at[o], sems.at[o]) for o in range(4 * rows)]
     for o in range(4 * rows):
-        out[o] = wide[o].astype(BF16)
+        narrow[o] = wide[o].astype(BF16)
+        copies[o].start()
+    for copy in copies:
+        copy.wait()
 
 
 def in_vmem(x):
@@ -336,13 +340,15 @@
         late_kernel,
         out_shape=[jax.ShapeDtypeStruct((4 * rows, 4 * cols, c3), BF16), acc_shape],
         in_specs=[vmem] * 11,
-        out_specs=[vmem] * 2,
+        out_specs=[anywhere, vmem],
         input_output_aliases={3: 1},
         scratch_shapes=[
             pltpu.VMEM((2, 2, cols, 3 * c1), BF16),
             pltpu.VMEM((2, rows + 2, cols, 3 * c1), BF16),
             pltpu.VMEM((2, 2 * rows + 2, cols, 4 * c2), BF16),
             pltpu.VMEM((4 * rows, 4 * cols, c3), F32),
+            pltpu.VMEM((4 * rows, 4 * cols, c3), BF16),
+            pltpu.SemaphoreType.DMA((4 * rows,)),
         ],
         cost_estimate=pl.CostEstimate(flops=8_000_000_000, bytes_accessed=1024, transcendentals=0),
         compiler_params=pltpu.CompilerParams(vmem_limit_bytes=14 << 20),

time: 27.1 us -> 27 us (level)
  no operation moved by 1% of the time
where the time goes in v8:
time: 27 us; the launch traced here: 26.9 us
  Pallas kernels  14.6 us (54%)
  waiting for transfers between devices  6.78 us (25%)
  starting transfers between devices  5.28 us (20%)
    ppermute x1, waiting for transfers between devices, per_device(): far = lax.ppermute(edge, ('sect', 'tile'), apart)  6.68 us
    pallas_call x1, Pallas kernels, per_device(): pl.pallas_call(late_kernel, out_shape=[jax.ShapeDtypeStruct((4 * rows, 4...  6.15 us
    pallas_call x1, Pallas kernels, per_device(): pl.pallas_call(early_kernel, out_shape=[pltpu.VMEM((2, rows + 3, cols, c1...  6.13 us
    ppermute x1, starting transfers between devices, per_device(): far = lax.ppermute(edge, ('sect', 'tile'), apart)  4.79 us
    pallas_call x1, Pallas kernels, per_device(): pl.pallas_call(middle_kernel, out_shape=acc_shape, in_specs=[vmem] * 4, o...  1.3 us
    pallas_call x1, Pallas kernels, per_device(): pl.pallas_call(load_kernel, out_shape=pair_shape, in_specs=[anywhere], ou...  1.06 us
  transfers between devices with their start and end apart: 3, of which 2 were waited for; matrix products, arithmetic and copies ran while one was open for 0% of the time, Pallas kernels for 32%

profile of v8, /device:TPU:0, one launch (start us, length us, event | category | flops | bytes accessed | tf_op | source)
XLA Modules:
  0.0 26.9 jit_solution(6455409388439470366)
XLA Ops:
  0.0 0.5 %collective-permute-start = (bf16[2,64,512]{2,1,0:T(8,128)(2,1)}, bf16[2,64,512]{2,1,0:T(8,128)(2,1)S(1)}, u32[]{:S(2)}, u32[]{:S(2)}) collective-permute-start(bf16[2,64,512]{2,1,0:T(8,128)(2,1)} %bitcast.4), channel_id=1, source_target_pairs={{0,8},{8,0},{1,9},{9,1},{2,10},{10,2},{3,11},{11,3},{4,12},{12,4},... | collective-permute-start | bytes 393224 | tf_op jit(solution)/shard_map/ppermute | solution.py:278
  0.5 0.0 slice-start
  0.5 1.1 %shard_map.73.half = bf16[2,2,64,512]{3,2,1,0:T(8,128)(2,1)S(1)} custom-call(bf16[2,64,512]{2,1,0:T(8,128)(2,1)} %bitcast.5), custom_call_target="tpu_custom_call" | custom-call | flops 6000000000 | bytes 1024 | tf_op jit(solution)/shard_map/pallas_call | solution.py:280
  1.6 0.0 slice-start.1
  1.6 0.0 copy-start
  1.6 0.1 collective-permute-done.other
  1.7 4.8 %collective-permute-start.1 = (bf16[2,2,64,512]{3,2,1,0:T(8,128)(2,1)S(1)}, bf16[2,2,64,512]{3,2,1,0:T(8,128)(2,1)S(1)}, u32[]{:S(2)}, u32[]{:S(2)}) collective-permute-start(bf16[2,2,64,512]{3,2,1,0:T(8,128)(2,1)S(1)} %shard_map.74.pair), channel_id=1, source_target_pairs={{0,9},{1,10},{2,11},{3,12},{4,13},{5,14},{6,15},{9,0},{10,1},{11,2... | collective-permute-start | bytes 786440 | tf_op jit(solution)/shard_map/ppermute | solution.py:302
  6.5 6.7 %collective-permute-done.1.far = bf16[2,2,64,512]{3,2,1,0:T(8,128)(2,1)S(1)} collective-permute-done((bf16[2,2,64,512]{3,2,1,0:T(8,128)(2,1)S(1)}, bf16[2,2,64,512]{3,2,1,0:T(8,128)(2,1)S(1)}, u32[]{:S(2)}, u32[]{:S(2)}) %collective-permute-start.1) | collective-permute-done | bytes 262176 | tf_op jit(solution)/shard_map/ppermute | solution.py:302
  13.2 0.0 collective-permute-start.2
  13.2 0.0 slice-done
  13.2 0.0 slice-done.1
  13.2 0.0 copy-done
  13.2 6.1 %shard_map.75 = (f32[2,5,64,512]{3,2,1,0:T(8,128)S(1)}, bf16[3,1536,512]{2,1,0:T(8,128)(2,1)S(1)}, bf16[3,3,512,512]{3,2,1,0:T(8,128)(2,1)S(1)}, bf16[2,2,2,1024...) custom-call(bf16[2,2,64,512]{3,2,1,0:T(8,128)(2,1)S(1)} %shard_map.74.pair, bf16[3,3,3,512,512]{4,3,2,1,0:T(8,128)(2,1)} %w1.1, ...), custom_call_target="tpu_custom_call" | custom-call | flops 6000000000 | bytes 1024 | tf_op jit(solution)/shard_map/pallas_call | solution.py:304
  19.3 0.0 copy-start.1
  19.3 0.0 copy-start.2
  19.4 0.0 copy-start.3
  19.4 1.3 %shard_map.76.before = f32[2,5,64,512]{3,2,1,0:T(8,128)S(1)} custom-call(bf16[2,2,64,512]{3,2,1,0:T(8,128)(2,1)S(1)} %collective-permute-done.1.far, f32[2,5,64,512]{3,2,1,0:T(8,128)S(1)} %get-tuple-element.11.before, bf16[3,1536,512]{2,1,0:T(8,128)(2,1)S(1)} %get-tuple-element.12.v1, ...), custom_call_target="tpu_custom_call", output_to_operand_aliasing={{}: (1, {})} | custom-call | flops 2000000000 | bytes 1024 | tf_op jit(solution)/shard_map/pallas_call | solution.py:329
  20.7 0.0 collective-permute-done.2.near
  20.7 0.0 copy-done.1
  20.7 0.0 copy-done.2
  20.7 0.0 copy-done.3
  20.7 6.1 %shard_map.77 = (bf16[8,256,128]{2,1,0:T(8,128)(2,1)}, f32[2,5,64,512]{3,2,1,0:T(8,128)S(1)}) custom-call(bf16[2,2,64,512]{3,2,1,0:T(8,128)(2,1)S(1)} %shard_map.74.pair, bf16[2,2,64,512]{3,2,1,0:T(8,128)(2,1)S(1)} %collective-permute-done.1.far, bf16[2,2,64,512]{3,2,1,0:T(8,128)(2,1)S(1)} %collective-permute-done.2.near, ...), custom_call_target="tpu_custom_call", output_to_operand_aliasing={{1}: (3, {})} | custom-call | flops 8000000000 | bytes 1024 | tf_op jit(solution)/shard_map/pallas_call | solution.py:339
  (2 shorter events, 0.0 us)
Async XLA Ops:
  0.0 1.7 %collective-permute-start = (bf16[2,64,512]{2,1,0:T(8,128)(2,1)}, bf16[2,64,512]{2,1,0:T(8,128)(2,1)S(1)}, u32[]{:S(2)}, u32[]{:S(2)}) collective-permute-start(bf16[2,64,512]{2,1,0:T(8,128)(2,1)} %bitcast.4), channel_id=1, source_target_pairs={{0,8},{8,0},{1,9},{9,1},{2,10},{10,2},{3,11},{11,3},{4,12},{12,4},... | collective-permute-start | bytes 393224 | tf_op jit(solution)/shard_map/ppermute | solution.py:278
  0.5 12.7 %slice-start = ((s8[7077888]{0:T(1024)(128)(4,1)}), s8[4194304]{0:T(1024)(128)(4,1)S(1)}, s32[]{:S(2)}) async-start(s8[7077888]{0:T(1024)(128)(4,1)} %bitcast.2), calls=%async_computation | async-start | bytes 8388608
  1.6 11.6 %slice-start.1 = ((s8[7077888]{0:T(1024)(128)(4,1)}), s8[2883584]{0:T(1024)(128)(4,1)S(1)}, s32[]{:S(2)}) async-start(s8[7077888]{0:T(1024)(128)(4,1)} %bitcast.2), calls=%async_computation.1 | async-start | bytes 5767168
  1.6 11.6 %copy-start = (bf16[3,3,3,256,128]{4,3,2,1,0:T(8,128)(2,1)S(1)}, bf16[3,3,3,256,128]{4,3,2,1,0:T(8,128)(2,1)}, u32[]{:S(2)}) copy-start(bf16[3,3,3,256,128]{4,3,2,1,0:T(8,128)(2,1)} %w3.1) | copy-start | bytes 5308420
  1.7 11.5 %collective-permute-start.1 = (bf16[2,2,64,512]{3,2,1,0:T(8,128)(2,1)S(1)}, bf16[2,2,64,512]{3,2,1,0:T(8,128)(2,1)S(1)}, u32[]{:S(2)}, u32[]{:S(2)}) collective-permute-start(bf16[2,2,64,512]{3,2,1,0:T(8,128)(2,1)S(1)} %shard_map.74.pair), channel_id=1, source_target_pairs={{0,9},{1,10},{2,11},{3,12},{4,13},{5,14},{6,15},{9,0},{10,1},{11,2... | collective-permute-start | bytes 786440 | tf_op jit(solution)/shard_map/ppermute | solution.py:302
  13.2 7.5 %collective-permute-start.2 = (bf16[2,2,64,512]{3,2,1,0:T(8,128)(2,1)S(1)}, bf16[2,2,64,512]{3,2,1,0:T(8,128)(2,1)S(1)}, u32[]{:S(2)}, u32[]{:S(2)}) collective-permute-start(bf16[2,2,64,512]{3,2,1,0:T(8,128)(2,1)S(1)} %collective-permute-done.1.far), channel_id=1, source_target_pairs={{0,8},{8,0},{1,9},{9,1},{2,10},{10,2},{3,11},{11,3},{4,12},{12,4},... | collective-permute-start | bytes 786440 | tf_op jit(solution)/shard_map/ppermute | solution.py:303
  19.3 1.4 %copy-start.1 = (bf16[512]{0:T(512)(128)(2,1)S(1)}, bf16[512]{0:T(512)(128)(2,1)}, u32[]{:S(2)}) copy-start(bf16[512]{0:T(512)(128)(2,1)} %b1.1) | copy-start | bytes 3076
  19.3 1.4 %copy-start.2 = (bf16[256]{0:T(256)(128)(2,1)S(1)}, bf16[256]{0:T(256)(128)(2,1)}, u32[]{:S(2)}) copy-start(bf16[256]{0:T(256)(128)(2,1)} %b2.1) | copy-start | bytes 1540
  19.4 1.4 %copy-start.3 = (bf16[128]{0:T(256)(128)(2,1)S(1)}, bf16[128]{0:T(256)(128)(2,1)}, u32[]{:S(2)}) copy-start(bf16[128]{0:T(256)(128)(2,1)} %b3.1) | copy-start | bytes 772

commit v9 on v8

--- a/solution.py
+++ b/solution.py
@@ -94,6 +94,10 @@
     pair[1] = other[...]
 
 
+def far_above():
+    return (lax.axis_index("sect") + lax.axis_index("tile")) % 2 == 1
+
+
 def halo_part(source, at, upper, acc, v1, wn, cat):
     cols, c1 = source.shape[2:]
     rows = acc.shape[1] - 3
@@ -163,7 +167,7 @@
 
 def middle_kernel(far, before, v1, wn, acc, cat):
     second = lax.axis_index("sect") > 0
-    halo_part(far, (jnp.where(second, 0, 1), 1), second, acc, v1, wn, cat)
+    halo_part(far, (jnp.where(second, 1, 0), 0), far_above(), acc, v1, wn, cat)
 
 
 def late_kernel(
@@ -178,22 +182,23 @@
     last_tile = tile == lax.axis_size("tile") - 1
 
     def feature(f, r):
-        if r < 2:
-            if f == 0:
-                return jnp.where(second, far[0, r].astype(F32), near[0, r].astype(F32))
-            return jnp.where(second, far[1, r].astype(F32), near[0, r].astype(F32))
-        if r < rows + 2:
+        if 2 <= r < rows + 2:
             mine = pair[0, r - 2].astype(F32)
             if f == 1:
                 return mine
             return jnp.where(second, pair[1, r - 2].astype(F32), mine)
-        r = r - rows - 2
-        if f == 0:
-            return jnp.where(second, near[1, r].astype(F32), far[1, r].astype(F32))
-        return jnp.where(second, near[0, r].astype(F32), far[1, r].astype(F32))
+        above = r < 2
+        r = r if above else r - rows - 2
+        if f == 1:
+            own, other = far[0, r].astype(F32), near[1, r].astype(F32)
+        else:
+            own = jnp.where(second, far[1, r].astype(F32), far[0, r].astype(F32))
+            other = jnp.where(second, near[0, r].astype(F32), near[1, r].astype(F32))
+        upper = far_above()
+        return jnp.where(upper if above else jnp.logical_not(upper), own, other)
 
     mrows = rows + 2
-    halo_part(near, (jnp.where(second, 1, 0), 0), jnp.logical_not(second), acc, v1, wn, hcat)
+    halo_part(near, (jnp.where(second, 0, 1), 1), jnp.logical_not(far_above()), acc, v1, wn, hcat)
     bias = b1[...].astype(F32)[None, :]
     for f in range(2):
         for m in range(mrows):
@@ -270,8 +275,10 @@
     c3 = conv_third.shape[4]
     tiles = lax.axis_size("tile")
     swap = [(0, 1), (1, 0)]
-    apart = [(i, tiles + i + 1) for i in range(tiles - 1)]
-    apart += [(tiles + i + 1, i) for i in range(tiles - 1)]
+    apart = []
+    for i in range(tiles - 1):
+        core = tiles * (i % 2)
+        apart += [(core + i, core + i + 1), (core + i + 1, core + i)]
     vmem = pl.BlockSpec(memory_space=pltpu.VMEM)
     anywhere = pl.BlockSpec(memory_space=pl.ANY)
 
@@ -298,7 +305,7 @@
     if rows == 2:
         edge = pair
     else:
-        edge = jnp.where(lax.axis_index("sect") == 0, pair[:, rows - 2 :], pair[:, :2])
+        edge = jnp.where(far_above(), pair[:, :2], pair[:, rows - 2 :])
     far = lax.ppermute(edge, ("sect", "tile"), apart)
     near = lax.ppermute(far, "sect", swap)
     acc, v1, wn, v2, v3 = pl.pallas_call(

time: 27 us -> 27.5 us (1.019)
  transfers between devices with their start and end apart: 3 -> 3, of which waited for: 2 -> 2; matrix products, arithmetic and copies ran while one was open for 0% -> 0% of each run, Pallas kernels for 32% -> 31%
where the time goes in v9:
time: 27.5 us; the launch traced here: 27.1 us
  Pallas kernels  14.7 us (53%)
  waiting for transfers between devices  6.78 us (25%)
  starting transfers between devices  5.53 us (20%)
    ppermute x1, waiting for transfers between devices, per_device(): far = lax.ppermute(edge, ('sect', 'tile'), apart)  6.68 us
    pallas_call x1, Pallas kernels, per_device(): pl.pallas_call(late_kernel, out_shape=[jax.ShapeDtypeStruct((4 * rows, 4...  6.17 us
    pallas_call x1, Pallas kernels, per_device(): pl.pallas_call(early_kernel, out_shape=[pltpu.VMEM((2, rows + 3, cols, c1...  6.13 us
    ppermute x1, starting transfers between devices, per_device(): far = lax.ppermute(edge, ('sect', 'tile'), apart)  5.04 us
    pallas_call x1, Pallas kernels, per_device(): pl.pallas_call(middle_kernel, out_shape=acc_shape, in_specs=[vmem] * 4, o...  1.3 us
    pallas_call x1, Pallas kernels, per_device(): pl.pallas_call(load_kernel, out_shape=pair_shape, in_specs=[anywhere], ou...  1.06 us
  transfers between devices with their start and end apart: 3, of which 2 were waited for; matrix products, arithmetic and copies ran while one was open for 0% of the time, Pallas kernels for 31%

profile of v9, /device:TPU:0, one launch (start us, length us, event | category | flops | bytes accessed | tf_op | source)
XLA Modules:
  0.0 27.1 jit_solution(1435935318228815955)
XLA Ops:
  0.0 0.5 %collective-permute-start = (bf16[2,64,512]{2,1,0:T(8,128)(2,1)}, bf16[2,64,512]{2,1,0:T(8,128)(2,1)S(1)}, u32[]{:S(2)}, u32[]{:S(2)}) collective-permute-start(bf16[2,64,512]{2,1,0:T(8,128)(2,1)} %bitcast.4), channel_id=1, source_target_pairs={{0,8},{8,0},{1,9},{9,1},{2,10},{10,2},{3,11},{11,3},{4,12},{12,4},... | collective-permute-start | bytes 393224 | tf_op jit(solution)/shard_map/ppermute | solution.py:285
  0.5 0.0 slice-start
  0.5 1.1 %shard_map.73.half = bf16[2,2,64,512]{3,2,1,0:T(8,128)(2,1)S(1)} custom-call(bf16[2,64,512]{2,1,0:T(8,128)(2,1)} %bitcast.5), custom_call_target="tpu_custom_call" | custom-call | flops 6000000000 | bytes 1024 | tf_op jit(solution)/shard_map/pallas_call | solution.py:287
  1.6 0.0 slice-start.1
  1.6 0.0 copy-start
  1.6 0.1 collective-permute-done.other
  1.7 5.0 %collective-permute-start.1 = (bf16[2,2,64,512]{3,2,1,0:T(8,128)(2,1)S(1)}, bf16[2,2,64,512]{3,2,1,0:T(8,128)(2,1)S(1)}, u32[]{:S(2)}, u32[]{:S(2)}) collective-permute-start(bf16[2,2,64,512]{3,2,1,0:T(8,128)(2,1)S(1)} %shard_map.74.pair), channel_id=1, source_target_pairs={{0,1},{1,0},{9,10},{10,9},{2,3},{3,2},{11,12},{12,11},{4,5},{5,4},... | collective-permute-start | bytes 786440 | tf_op jit(solution)/shard_map/ppermute | solution.py:309
  6.7 6.7 %collective-permute-done.1.far = bf16[2,2,64,512]{3,2,1,0:T(8,128)(2,1)S(1)} collective-permute-done((bf16[2,2,64,512]{3,2,1,0:T(8,128)(2,1)S(1)}, bf16[2,2,64,512]{3,2,1,0:T(8,128)(2,1)S(1)}, u32[]{:S(2)}, u32[]{:S(2)}) %collective-permute-start.1) | collective-permute-done | bytes 262176 | tf_op jit(solution)/shard_map/ppermute | solution.py:309
  13.4 0.0 collective-permute-start.2
  13.4 0.0 slice-done
  13.4 0.0 slice-done.1
  13.4 0.0 copy-done
  13.4 6.1 %shard_map.75 = (f32[2,5,64,512]{3,2,1,0:T(8,128)S(1)}, bf16[3,1536,512]{2,1,0:T(8,128)(2,1)S(1)}, bf16[3,3,512,512]{3,2,1,0:T(8,128)(2,1)S(1)}, bf16[2,2,2,1024...) custom-call(bf16[2,2,64,512]{3,2,1,0:T(8,128)(2,1)S(1)} %shard_map.74.pair, bf16[3,3,3,512,512]{4,3,2,1,0:T(8,128)(2,1)} %w1.1, ...), custom_call_target="tpu_custom_call" | custom-call | flops 6000000000 | bytes 1024 | tf_op jit(solution)/shard_map/pallas_call | solution.py:311
  19.6 0.0 copy-start.1
  19.6 0.0 copy-start.2
  19.6 0.0 copy-start.3
  19.6 1.3 %shard_map.76.before = f32[2,5,64,512]{3,2,1,0:T(8,128)S(1)} custom-call(bf16[2,2,64,512]{3,2,1,0:T(8,128)(2,1)S(1)} %collective-permute-done.1.far, f32[2,5,64,512]{3,2,1,0:T(8,128)S(1)} %get-tuple-element.11.before, bf16[3,1536,512]{2,1,0:T(8,128)(2,1)S(1)} %get-tuple-element.12.v1, ...), custom_call_target="tpu_custom_call", output_to_operand_aliasing={{}: (1, {})} | custom-call | flops 2000000000 | bytes 1024 | tf_op jit(solution)/shard_map/pallas_call | solution.py:336
  20.9 0.0 collective-permute-done.2.near
  20.9 0.0 copy-done.1
  21.0 0.0 copy-done.2
  21.0 0.0 copy-done.3
  21.0 6.2 %shard_map.77 = (bf16[8,256,128]{2,1,0:T(8,128)(2,1)}, f32[2,5,64,512]{3,2,1,0:T(8,128)S(1)}) custom-call(bf16[2,2,64,512]{3,2,1,0:T(8,128)(2,1)S(1)} %shard_map.74.pair, bf16[2,2,64,512]{3,2,1,0:T(8,128)(2,1)S(1)} %collective-permute-done.1.far, bf16[2,2,64,512]{3,2,1,0:T(8,128)(2,1)S(1)} %collective-permute-done.2.near, ...), custom_call_target="tpu_custom_call", output_to_operand_aliasing={{1}: (3, {})} | custom-call | flops 8000000000 | bytes 1024 | tf_op jit(solution)/shard_map/pallas_call | solution.py:346
  (2 shorter events, 0.0 us)
Async XLA Ops:
  0.0 1.7 %collective-permute-start = (bf16[2,64,512]{2,1,0:T(8,128)(2,1)}, bf16[2,64,512]{2,1,0:T(8,128)(2,1)S(1)}, u32[]{:S(2)}, u32[]{:S(2)}) collective-permute-start(bf16[2,64,512]{2,1,0:T(8,128)(2,1)} %bitcast.4), channel_id=1, source_target_pairs={{0,8},{8,0},{1,9},{9,1},{2,10},{10,2},{3,11},{11,3},{4,12},{12,4},... | collective-permute-start | bytes 393224 | tf_op jit(solution)/shard_map/ppermute | solution.py:285
  0.5 12.9 %slice-start = ((s8[7077888]{0:T(1024)(128)(4,1)}), s8[4194304]{0:T(1024)(128)(4,1)S(1)}, s32[]{:S(2)}) async-start(s8[7077888]{0:T(1024)(128)(4,1)} %bitcast.2), calls=%async_computation | async-start | bytes 8388608
  1.6 11.9 %slice-start.1 = ((s8[7077888]{0:T(1024)(128)(4,1)}), s8[2883584]{0:T(1024)(128)(4,1)S(1)}, s32[]{:S(2)}) async-start(s8[7077888]{0:T(1024)(128)(4,1)} %bitcast.2), calls=%async_computation.1 | async-start | bytes 5767168
  1.6 11.9 %copy-start = (bf16[3,3,3,256,128]{4,3,2,1,0:T(8,128)(2,1)S(1)}, bf16[3,3,3,256,128]{4,3,2,1,0:T(8,128)(2,1)}, u32[]{:S(2)}) copy-start(bf16[3,3,3,256,128]{4,3,2,1,0:T(8,128)(2,1)} %w3.1) | copy-start | bytes 5308420
  1.7 11.7 %collective-permute-start.1 = (bf16[2,2,64,512]{3,2,1,0:T(8,128)(2,1)S(1)}, bf16[2,2,64,512]{3,2,1,0:T(8,128)(2,1)S(1)}, u32[]{:S(2)}, u32[]{:S(2)}) collective-permute-start(bf16[2,2,64,512]{3,2,1,0:T(8,128)(2,1)S(1)} %shard_map.74.pair), channel_id=1, source_target_pairs={{0,1},{1,0},{9,10},{10,9},{2,3},{3,2},{11,12},{12,11},{4,5},{5,4},... | collective-permute-start | bytes 786440 | tf_op jit(solution)/shard_map/ppermute | solution.py:309
  13.4 7.5 %collective-permute-start.2 = (bf16[2,2,64,512]{3,2,1,0:T(8,128)(2,1)S(1)}, bf16[2,2,64,512]{3,2,1,0:T(8,128)(2,1)S(1)}, u32[]{:S(2)}, u32[]{:S(2)}) collective-permute-start(bf16[2,2,64,512]{3,2,1,0:T(8,128)(2,1)S(1)} %collective-permute-done.1.far), channel_id=1, source_target_pairs={{0,8},{8,0},{1,9},{9,1},{2,10},{10,2},{3,11},{11,3},{4,12},{12,4},... | collective-permute-start | bytes 786440 | tf_op jit(solution)/shard_map/ppermute | solution.py:310
  19.6 1.4 %copy-start.1 = (bf16[512]{0:T(512)(128)(2,1)S(1)}, bf16[512]{0:T(512)(128)(2,1)}, u32[]{:S(2)}) copy-start(bf16[512]{0:T(512)(128)(2,1)} %b1.1) | copy-start | bytes 3076
  19.6 1.4 %copy-start.2 = (bf16[256]{0:T(256)(128)(2,1)S(1)}, bf16[256]{0:T(256)(128)(2,1)}, u32[]{:S(2)}) copy-start(bf16[256]{0:T(256)(128)(2,1)} %b2.1) | copy-start | bytes 1540
  19.6 1.4 %copy-start.3 = (bf16[128]{0:T(256)(128)(2,1)S(1)}, bf16[128]{0:T(256)(128)(2,1)}, u32[]{:S(2)}) copy-start(bf16[128]{0:T(256)(128)(2,1)} %b3.1) | copy-start | bytes 772

commit v10 on v9

--- a/solution.py
+++ b/solution.py
@@ -94,10 +94,6 @@
     pair[1] = other[...]
 
 
-def far_above():
-    return (lax.axis_index("sect") + lax.axis_index("tile")) % 2 == 1
-
-
 def halo_part(source, at, upper, acc, v1, wn, cat):
     cols, c1 = source.shape[2:]
     rows = acc.shape[1] - 3
@@ -151,11 +147,12 @@
     acc[...] = jnp.zeros(acc.shape, F32)
 
     def tap(i, _):
-        for t in range(3):
+        for t in range(2):
             copy(t, i).wait()
         merge_time(raw.at[i], v1.at[i])
         both = cat[...].reshape(2 * size, 3 * c1)
         part = dot(both[:size], v1[i])
+        copy(2, i).wait()
         total = dot(both, wn[i].reshape(3 * c1, c1))
         for f in range(2):
             value = (total[f * size : (f + 1) * size] + part).reshape(rows, cols, c1)
@@ -167,7 +164,7 @@
 
 def middle_kernel(far, before, v1, wn, acc, cat):
     second = lax.axis_index("sect") > 0
-    halo_part(far, (jnp.where(second, 1, 0), 0), far_above(), acc, v1, wn, cat)
+    halo_part(far, (jnp.where(second, 0, 1), 1), jnp.logical_not(second), acc, v1, wn, cat)
 
 
 def late_kernel(
@@ -189,16 +186,14 @@
             return jnp.where(second, pair[1, r - 2].astype(F32), mine)
         above = r < 2
         r = r if above else r - rows - 2
-        if f == 1:
-            own, other = far[0, r].astype(F32), near[1, r].astype(F32)
+        if above:
+            own, other = (near[1 - f, r], far[1, r])
         else:
-            own = jnp.where(second, far[1, r].astype(F32), far[0, r].astype(F32))
-            other = jnp.where(second, near[0, r].astype(F32), near[1, r].astype(F32))
-        upper = far_above()
-        return jnp.where(upper if above else jnp.logical_not(upper), own, other)
+            own, other = (far[f, r], near[0, r])
+        return jnp.where(second, own.astype(F32), other.astype(F32))
 
     mrows = rows + 2
-    halo_part(near, (jnp.where(second, 0, 1), 1), jnp.logical_not(far_above()), acc, v1, wn, hcat)
+    halo_part(near, (jnp.where(second, 1, 0), 0), second, acc, v1, wn, hcat)
     bias = b1[...].astype(F32)[None, :]
     for f in range(2):
         for m in range(mrows):
@@ -275,10 +270,8 @@
     c3 = conv_third.shape[4]
     tiles = lax.axis_size("tile")
     swap = [(0, 1), (1, 0)]
-    apart = []
-    for i in range(tiles - 1):
-        core = tiles * (i % 2)
-        apart += [(core + i, core + i + 1), (core + i + 1, core + i)]
+    apart = [(i + 1, tiles + i) for i in range(tiles - 1)]
+    apart += [(tiles + i, i + 1) for i in range(tiles - 1)]
     vmem = pl.BlockSpec(memory_space=pltpu.VMEM)
     anywhere = pl.BlockSpec(memory_space=pl.ANY)
 
@@ -305,7 +298,7 @@
     if rows == 2:
         edge = pair
     else:
-        edge = jnp.where(far_above(), pair[:, :2], pair[:, rows - 2 :])
+        edge = jnp.where(lax.axis_index("sect") == 1, pair[:, rows - 2 :], pair[:, :2])
     far = lax.ppermute(edge, ("sect", "tile"), apart)
     near = lax.ppermute(far, "sect", swap)
     acc, v1, wn, v2, v3 = pl.pallas_call(

time: 27.5 us -> 26.7 us (0.971)
  waiting for transfers between devices: 6.78 us -> 0.1 us
  starting transfers between devices: 5.53 us -> 11.7 us
    ppermute x1, starting transfers between devices: 0.01 us -> 10.4 us  [per_device(): near = lax.ppermute(far, 'sect', swap)]
    ppermute x1, waiting for transfers between devices: 6.68 us -> 0.01 us  [per_device(): far = lax.ppermute(edge, ('sect', 'tile'), apart)]
    ppermute x1, starting transfers between devices: 5.04 us -> 0.81 us  [per_device(): far = lax.ppermute(edge, ('sect', 'tile'), apart)]
  transfers between devices with their start and end apart: 3 -> 3, of which waited for: 2 -> 1; matrix products, arithmetic and copies ran while one was open for 0% -> 0% of each run, Pallas kernels for 31% -> 32%
where the time goes in v10:
time: 26.7 us; the launch traced here: 26.5 us
  Pallas kernels  14.5 us (54%)
  starting transfers between devices  11.7 us (44%)
    ppermute x1, starting transfers between devices, per_device(): near = lax.ppermute(far, 'sect', swap)  10.4 us
    pallas_call x1, Pallas kernels, per_device(): pl.pallas_call(late_kernel, out_shape=[jax.ShapeDtypeStruct((4 * rows, 4...  6.15 us
    pallas_call x1, Pallas kernels, per_device(): pl.pallas_call(early_kernel, out_shape=[pltpu.VMEM((2, rows + 3, cols, c1...  6 us
    pallas_call x1, Pallas kernels, per_device(): pl.pallas_call(middle_kernel, out_shape=acc_shape, in_specs=[vmem] * 4, o...  1.3 us
    pallas_call x1, Pallas kernels, per_device(): pl.pallas_call(load_kernel, out_shape=pair_shape, in_specs=[anywhere], ou...  1.06 us
    ppermute x1, starting transfers between devices, per_device(): far = lax.ppermute(edge, ('sect', 'tile'), apart)  0.81 us
  transfers between devices with their start and end apart: 3, of which 1 were waited for; matrix products, arithmetic and copies ran while one was open for 0% of the time, Pallas kernels for 32%

profile of v10, /device:TPU:0, one launch (start us, length us, event | category | flops | bytes accessed | tf_op | source)
XLA Modules:
  0.0 26.5 jit_solution(6666122402699801982)
XLA Ops:
  0.0 0.5 %collective-permute-start = (bf16[2,64,512]{2,1,0:T(8,128)(2,1)}, bf16[2,64,512]{2,1,0:T(8,128)(2,1)S(1)}, u32[]{:S(2)}, u32[]{:S(2)}) collective-permute-start(bf16[2,64,512]{2,1,0:T(8,128)(2,1)} %bitcast.4), channel_id=1, source_target_pairs={{0,8},{8,0},{1,9},{9,1},{2,10},{10,2},{3,11},{11,3},{4,12},{12,4},... | collective-permute-start | bytes 393224 | tf_op jit(solution)/shard_map/ppermute | solution.py:278
  0.5 0.0 slice-start
  0.5 1.1 %shard_map.73.half = bf16[2,2,64,512]{3,2,1,0:T(8,128)(2,1)S(1)} custom-call(bf16[2,64,512]{2,1,0:T(8,128)(2,1)} %bitcast.5), custom_call_target="tpu_custom_call" | custom-call | flops 6000000000 | bytes 1024 | tf_op jit(solution)/shard_map/pallas_call | solution.py:280
  1.6 0.0 slice-start.1
  1.6 0.0 copy-start
  1.6 0.1 collective-permute-done.other
  1.7 0.8 %collective-permute-start.1 = (bf16[2,2,64,512]{3,2,1,0:T(8,128)(2,1)S(1)}, bf16[2,2,64,512]{3,2,1,0:T(8,128)(2,1)S(1)}, u32[]{:S(2)}, u32[]{:S(2)}) collective-permute-start(bf16[2,2,64,512]{3,2,1,0:T(8,128)(2,1)S(1)} %shard_map.74.pair), channel_id=1, source_target_pairs={{1,8},{2,9},{3,10},{4,11},{5,12},{6,13},{7,14},{8,1},{9,2},{10,3},... | collective-permute-start | bytes 786440 | tf_op jit(solution)/shard_map/ppermute | solution.py:302
  2.5 0.0 collective-permute-done.1.far
  2.5 10.4 %collective-permute-start.2 = (bf16[2,2,64,512]{3,2,1,0:T(8,128)(2,1)S(1)}, bf16[2,2,64,512]{3,2,1,0:T(8,128)(2,1)S(1)}, u32[]{:S(2)}, u32[]{:S(2)}) collective-permute-start(bf16[2,2,64,512]{3,2,1,0:T(8,128)(2,1)S(1)} %collective-permute-done.1.far), channel_id=1, source_target_pairs={{0,8},{8,0},{1,9},{9,1},{2,10},{10,2},{3,11},{11,3},{4,12},{12,4},... | collective-permute-start | bytes 786440 | tf_op jit(solution)/shard_map/ppermute | solution.py:303
  13.0 0.0 slice-done
  13.0 0.0 slice-done.1
  13.0 0.0 copy-done
  13.0 6.0 %shard_map.75 = (f32[2,5,64,512]{3,2,1,0:T(8,128)S(1)}, bf16[3,1536,512]{2,1,0:T(8,128)(2,1)S(1)}, bf16[3,3,512,512]{3,2,1,0:T(8,128)(2,1)S(1)}, bf16[2,2,2,1024...) custom-call(bf16[2,2,64,512]{3,2,1,0:T(8,128)(2,1)S(1)} %shard_map.74.pair, bf16[3,3,3,512,512]{4,3,2,1,0:T(8,128)(2,1)} %w1.1, ...), custom_call_target="tpu_custom_call" | custom-call | flops 6000000000 | bytes 1024 | tf_op jit(solution)/shard_map/pallas_call | solution.py:304
  19.0 0.0 copy-start.1
  19.0 0.0 copy-start.2
  19.0 0.0 copy-start.3
  19.0 1.3 %shard_map.76.before = f32[2,5,64,512]{3,2,1,0:T(8,128)S(1)} custom-call(bf16[2,2,64,512]{3,2,1,0:T(8,128)(2,1)S(1)} %collective-permute-done.1.far, f32[2,5,64,512]{3,2,1,0:T(8,128)S(1)} %get-tuple-element.11.before, bf16[3,1536,512]{2,1,0:T(8,128)(2,1)S(1)} %get-tuple-element.12.v1, ...), custom_call_target="tpu_custom_call", output_to_operand_aliasing={{}: (1, {})} | custom-call | flops 2000000000 | bytes 1024 | tf_op jit(solution)/shard_map/pallas_call | solution.py:329
  20.3 0.0 collective-permute-done.2.near
  20.3 0.0 copy-done.1
  20.3 0.0 copy-done.2
  20.4 0.0 copy-done.3
  20.4 6.1 %shard_map.77 = (bf16[8,256,128]{2,1,0:T(8,128)(2,1)}, f32[2,5,64,512]{3,2,1,0:T(8,128)S(1)}) custom-call(bf16[2,2,64,512]{3,2,1,0:T(8,128)(2,1)S(1)} %shard_map.74.pair, bf16[2,2,64,512]{3,2,1,0:T(8,128)(2,1)S(1)} %collective-permute-done.1.far, bf16[2,2,64,512]{3,2,1,0:T(8,128)(2,1)S(1)} %collective-permute-done.2.near, ...), custom_call_target="tpu_custom_call", output_to_operand_aliasing={{1}: (3, {})} | custom-call | flops 8000000000 | bytes 1024 | tf_op jit(solution)/shard_map/pallas_call | solution.py:339
  (2 shorter events, 0.0 us)
Async XLA Ops:
  0.0 1.7 %collective-permute-start = (bf16[2,64,512]{2,1,0:T(8,128)(2,1)}, bf16[2,64,512]{2,1,0:T(8,128)(2,1)S(1)}, u32[]{:S(2)}, u32[]{:S(2)}) collective-permute-start(bf16[2,64,512]{2,1,0:T(8,128)(2,1)} %bitcast.4), channel_id=1, source_target_pairs={{0,8},{8,0},{1,9},{9,1},{2,10},{10,2},{3,11},{11,3},{4,12},{12,4},... | collective-permute-start | bytes 393224 | tf_op jit(solution)/shard_map/ppermute | solution.py:278
  0.5 12.5 %slice-start = ((s8[7077888]{0:T(1024)(128)(4,1)}), s8[4194304]{0:T(1024)(128)(4,1)S(1)}, s32[]{:S(2)}) async-start(s8[7077888]{0:T(1024)(128)(4,1)} %bitcast.2), calls=%async_computation | async-start | bytes 8388608
  1.6 11.4 %slice-start.1 = ((s8[7077888]{0:T(1024)(128)(4,1)}), s8[2883584]{0:T(1024)(128)(4,1)S(1)}, s32[]{:S(2)}) async-start(s8[7077888]{0:T(1024)(128)(4,1)} %bitcast.2), calls=%async_computation.1 | async-start | bytes 5767168
  1.6 11.4 %copy-start = (bf16[3,3,3,256,128]{4,3,2,1,0:T(8,128)(2,1)S(1)}, bf16[3,3,3,256,128]{4,3,2,1,0:T(8,128)(2,1)}, u32[]{:S(2)}) copy-start(bf16[3,3,3,256,128]{4,3,2,1,0:T(8,128)(2,1)} %w3.1) | copy-start | bytes 5308420
  1.7 0.8 %collective-permute-start.1 = (bf16[2,2,64,512]{3,2,1,0:T(8,128)(2,1)S(1)}, bf16[2,2,64,512]{3,2,1,0:T(8,128)(2,1)S(1)}, u32[]{:S(2)}, u32[]{:S(2)}) collective-permute-start(bf16[2,2,64,512]{3,2,1,0:T(8,128)(2,1)S(1)} %shard_map.74.pair), channel_id=1, source_target_pairs={{1,8},{2,9},{3,10},{4,11},{5,12},{6,13},{7,14},{8,1},{9,2},{10,3},... | collective-permute-start | bytes 786440 | tf_op jit(solution)/shard_map/ppermute | solution.py:302
  2.5 17.8 %collective-permute-start.2 = (bf16[2,2,64,512]{3,2,1,0:T(8,128)(2,1)S(1)}, bf16[2,2,64,512]{3,2,1,0:T(8,128)(2,1)S(1)}, u32[]{:S(2)}, u32[]{:S(2)}) collective-permute-start(bf16[2,2,64,512]{3,2,1,0:T(8,128)(2,1)S(1)} %collective-permute-done.1.far), channel_id=1, source_target_pairs={{0,8},{8,0},{1,9},{9,1},{2,10},{10,2},{3,11},{11,3},{4,12},{12,4},... | collective-permute-start | bytes 786440 | tf_op jit(solution)/shard_map/ppermute | solution.py:303
  19.0 1.4 %copy-start.1 = (bf16[512]{0:T(512)(128)(2,1)S(1)}, bf16[512]{0:T(512)(128)(2,1)}, u32[]{:S(2)}) copy-start(bf16[512]{0:T(512)(128)(2,1)} %b1.1) | copy-start | bytes 3076
  19.0 1.4 %copy-start.2 = (bf16[256]{0:T(256)(128)(2,1)S(1)}, bf16[256]{0:T(256)(128)(2,1)}, u32[]{:S(2)}) copy-start(bf16[256]{0:T(256)(128)(2,1)} %b2.1) | copy-start | bytes 1540
  19.0 1.3 %copy-start.3 = (bf16[128]{0:T(256)(128)(2,1)S(1)}, bf16[128]{0:T(256)(128)(2,1)}, u32[]{:S(2)}) copy-start(bf16[128]{0:T(256)(128)(2,1)} %b3.1) | copy-start | bytes 772
